TPU v7x, 128 devices: a whole 4x4x4 slice. The times are simulated.
128 devices in a mesh: req: 32 (over y_hi, x, z), sub: 4 (over y_lo, core).
Axes of the slice: x: 4, y: 4 (y_hi: 2, y_lo: 2; y = y_hi * 2 + y_lo), z: 4, core: 2. Of those that a mesh axis runs over, the one named last changes fastest.
Arguments:
- tokens: bfloat16 [16384, 2048], P(('req', 'sub')), may hold values from -6 to 6
- attn_gain: float32 [2048], replicated, may hold values from 0.25 to 1.75
- w_query: bfloat16 [2048, 1536], replicated, may hold values from -0.125 to 0.125
- w_latent: bfloat16 [2048, 576], replicated, may hold values from -0.125 to 0.125
- latent_gain: float32 [512], replicated, may hold values from 0.25 to 1.75
- w_key_up: bfloat16 [8, 128, 512], replicated, may hold values from -0.5 to 0.5
- w_value_up: bfloat16 [8, 512, 128], replicated, may hold values from -0.25 to 0.25
- w_out: bfloat16 [1024, 2048], replicated, may hold values from -0.1875 to 0.1875
- moe_gain: float32 [2048], replicated, may hold values from 0.25 to 1.75
- w_gate: bfloat16 [128, 2048, 704], P(('req', 'sub')), may hold values from -0.125 to 0.125
- w_up: bfloat16 [128, 2048, 704], P(('req', 'sub')), may hold values from -0.125 to 0.125
- w_down: bfloat16 [128, 704, 2048], P(('req', 'sub')), may hold values from -0.15625 to 0.15625
- expert_ids: int32 [16384, 6], P(('req', 'sub')), may hold values from 0 to 63, all different within a row; in each aligned block of 128 rows (0 to 127, 128 to 255, ...) at most 16 rows name the same one
- gate_weights: float32 [16384, 6], P(('req', 'sub')), may hold values from 0.1 to 0.6
- lengths: int32 [32, 3], P('req'), may hold values from 1 to 256, 512 in all within a row
- slab_group: int32 [32], P('req'), may hold values from 0 to 3
- owners: int32 [4], replicated, may hold values from 0 to 31, as said below
- prefix_pool: bfloat16 [32, 1024, 576], P('req'), as said below
Outputs:
- hidden_out: bfloat16 [16384, 2048], P(('req', 'sub'))
- new_cache: bfloat16 [16384, 576], P(('req', 'sub'))
Inputs may be any that keep to these rules, and one draw needn't show every extreme that they name: `expert_ids`: each row names 6 different experts; in each aligned block of 128 rows (the rows of one device) no expert is named by more than 16 rows, and in some block one expert is named by exactly 16 rows. Each slab's 3 lengths sum to 512, and its longest request has exactly half of 512 tokens. 4 distinct slots, among them slot 0 and slot 31; group g's cached prefix is prefix_pool[owners[g]]. `prefix_pool`: each row holds 512 latent entries followed by 64 rotary key entries.
All inputs are finite; a program needn't handle non-finite values.
Results may differ from a plain program's by a relative error of at most 0.013.
The roundings to bfloat16 on the way count: a program that leaves them out, or rounds other values in their place, can miss the bound.
Values may be sent and summed in bfloat16 or wider, within the bound.
No kernel may reach another device: no remote copies, remote signals or barrier semaphores. Data moves between devices by JAX's collectives and lax.ppermute only.
A program may use at most 128 MiB of HBM per device.

v0:
```python
import jax
import jax.numpy as jnp
from jax import lax
from jax.sharding import PartitionSpec as P

EPSILON = 1e-06
FLOOR_SCORE = -1e30


def from_root(x, axis, root):
    mine = lax.axis_index(axis) == root
    return lax.psum(jnp.where(mine, x, jnp.zeros_like(x)), axis)


def rms_scale(values, gain):
    return values * lax.rsqrt(jnp.mean(values * values, axis=-1, keepdims=True) + EPSILON) * gain


def angle_tables(positions, rope_width):
    half_width = rope_width // 2
    inverse = 10000.0 ** (-jnp.arange(half_width, dtype=jnp.float32) / half_width)
    angles = positions.astype(jnp.float32)[:, None] * inverse[None, :]
    return (jnp.cos(angles), jnp.sin(angles))


def rotate(values, cos_part, sin_part):
    half_width = values.shape[-1] // 2
    first_half = values[..., :half_width]
    second = values[..., half_width:]
    return jnp.concatenate(
        [first_half * cos_part - second * sin_part, second * cos_part + first_half * sin_part],
        axis=-1,
    )


def slab_layout(req_lengths, slab_rows):
    req_ends = jnp.cumsum(req_lengths)
    req_starts = req_ends - req_lengths
    slab_pos = jnp.arange(slab_rows, dtype=jnp.int32)
    segment = jnp.sum((slab_pos[:, None] >= req_ends[None, :]).astype(jnp.int32), axis=1)
    member_of = segment[:, None] == jnp.arange(req_lengths.shape[0], dtype=jnp.int32)[None, :]
    seg_start = jnp.sum(jnp.where(member_of, req_starts[None, :], 0), axis=1)
    return (slab_pos, segment, slab_pos - seg_start)


def block_attend(running, query_full, key_rows, allowed, score_scale, lat_width):
    row_top, denominator, weighted = running
    scores = (
        jnp.einsum("thc,kc->thk", query_full, key_rows, preferred_element_type=jnp.float32)
        * score_scale
    )
    scores = jnp.where(allowed[:, None, :], scores, FLOOR_SCORE)
    new_top = jnp.maximum(row_top, jnp.max(scores, axis=2))
    weights = jnp.where(allowed[:, None, :], jnp.exp(scores - new_top[:, :, None]), 0.0)
    rescale = jnp.exp(row_top - new_top)
    denominator = denominator * rescale + jnp.sum(weights, axis=2)
    weighted = weighted * rescale[:, :, None] + jnp.einsum(
        "thk,kc->thc",
        weights.astype(jnp.bfloat16),
        key_rows[:, :lat_width],
        preferred_element_type=jnp.float32,
    )
    return (new_top, denominator, weighted)


def expert_half(slot_rows, gate_half, up_half, down_half):
    gate_proj = jnp.dot(slot_rows, gate_half, preferred_element_type=jnp.float32)
    up_proj = jnp.dot(slot_rows, up_half, preferred_element_type=jnp.float32)
    activated = (jax.nn.silu(gate_proj) * up_proj).astype(jnp.bfloat16)
    return jnp.dot(activated, down_half, preferred_element_type=jnp.float32)


def local(
    tokens,
    attn_gain,
    w_query,
    w_latent,
    latent_gain,
    w_key_up,
    w_value_up,
    w_out,
    moe_gain,
    w_gate,
    w_up,
    w_down,
    expert_ids,
    gate_weights,
    lengths,
    slab_group,
    owners,
    prefix_pool,
):
    rows_dev, model_width = tokens.shape
    head_count, nope_width, lat_width = w_key_up.shape
    rope_width = w_latent.shape[1] - lat_width
    prefix_len = prefix_pool.shape[1]
    sub_count = lax.axis_size("sub")
    device_count = lax.axis_size("req") * sub_count
    sub_index = lax.axis_index("sub")
    slab_rows = rows_dev * sub_count
    slab_pos, segment, offset = slab_layout(lengths[0], slab_rows)
    own_first = sub_index * rows_dev
    own_pos = lax.dynamic_slice_in_dim(slab_pos, own_first, rows_dev)
    own_seg = lax.dynamic_slice_in_dim(segment, own_first, rows_dev)
    own_offset = lax.dynamic_slice_in_dim(offset, own_first, rows_dev)
    cos_part, sin_part = angle_tables(prefix_len + own_offset, rope_width)
    normed = rms_scale(tokens.astype(jnp.float32), attn_gain).astype(jnp.bfloat16)
    latent = jnp.dot(normed, w_latent, preferred_element_type=jnp.float32)
    cache_rows = jnp.concatenate(
        [
            rms_scale(latent[:, :lat_width], latent_gain),
            rotate(latent[:, lat_width:], cos_part, sin_part),
        ],
        axis=1,
    ).astype(jnp.bfloat16)
    queries = jnp.dot(normed, w_query, preferred_element_type=jnp.float32).astype(jnp.bfloat16)
    queries = queries.reshape(rows_dev, head_count, nope_width + rope_width)
    query_lat = jnp.einsum(
        "thj,hjc->thc", queries[:, :, :nope_width], w_key_up, preferred_element_type=jnp.float32
    )
    query_rot = rotate(
        queries[:, :, nope_width:].astype(jnp.float32), cos_part[:, None, :], sin_part[:, None, :]
    )
    query_full = jnp.concatenate([query_lat, query_rot], axis=2).astype(jnp.bfloat16)
    score_scale = (nope_width + rope_width) ** (-0.5)
    my_group = slab_group[0]
    start_state = (
        jnp.full((rows_dev, head_count), FLOOR_SCORE, dtype=jnp.float32),
        jnp.zeros((rows_dev, head_count), dtype=jnp.float32),
        jnp.zeros((rows_dev, head_count, lat_width), dtype=jnp.float32),
    )
    local_prefix = prefix_pool[0]
    prefix = jnp.zeros_like(local_prefix)
    for member in range(owners.shape[0]):
        copied = from_root(local_prefix, "req", owners[member])
        prefix = jnp.where(my_group == member, copied, prefix)
    everyone = jnp.ones((rows_dev, prefix_len), dtype=bool)
    running = block_attend(start_state, query_full, prefix, everyone, score_scale, lat_width)
    key_block = lax.all_gather(cache_rows, "sub", axis=0, tiled=True)
    block_len = key_block.shape[0]
    key_pos = jnp.arange(block_len, dtype=jnp.int32)
    allowed = (segment[None, :] == own_seg[:, None]) & (key_pos[None, :] <= own_pos[:, None])
    running = block_attend(running, query_full, key_block, allowed, score_scale, lat_width)
    row_top, denominator, weighted = running
    latent_out = (weighted / denominator[:, :, None]).astype(jnp.bfloat16)
    head_out = jnp.einsum(
        "thc,hcv->thv", latent_out, w_value_up, preferred_element_type=jnp.float32
    ).astype(jnp.bfloat16)
    head_out = head_out.reshape(rows_dev, head_count * w_value_up.shape[2])
    residual = tokens.astype(jnp.float32) + jnp.dot(
        head_out, w_out, preferred_element_type=jnp.float32
    )
    normed_mid = rms_scale(residual, moe_gain).astype(jnp.bfloat16)
    top_count = expert_ids.shape[1]
    expert_count = device_count // 2
    capacity = 4 * rows_dev * top_count // (3 * expert_count)
    flat_ids = expert_ids.reshape(-1)
    onehot = (flat_ids[:, None] == jnp.arange(expert_count, dtype=jnp.int32)[None, :]).astype(
        jnp.int32
    )
    slot_index = jnp.sum(onehot * (jnp.cumsum(onehot, axis=0) - 1), axis=1)
    target = flat_ids * capacity + slot_index
    chosen = (
        target[:, None] == jnp.arange(expert_count * capacity, dtype=jnp.int32)[None, :]
    ).astype(jnp.float32)
    chosen = chosen.reshape(rows_dev, top_count, expert_count * capacity)
    placing = jnp.sum(chosen, axis=1).astype(jnp.bfloat16)
    mixing = jnp.sum(chosen * gate_weights[:, :, None], axis=1)
    outbound = jnp.einsum(
        "ts,td->sd", placing, normed_mid, preferred_element_type=jnp.float32
    ).astype(jnp.bfloat16)
    doubled = jnp.broadcast_to(
        outbound.reshape(expert_count, 1, capacity, model_width),
        (expert_count, 2, capacity, model_width),
    )
    arrived = lax.all_to_all(
        doubled.reshape(device_count, capacity, model_width),
        ("req", "sub"),
        split_axis=0,
        concat_axis=0,
        tiled=True,
    )
    partial_value = expert_half(arrived.reshape(-1, model_width), w_gate[0], w_up[0], w_down[0])
    returned = lax.all_to_all(
        partial_value.reshape(device_count, capacity, model_width).astype(jnp.bfloat16),
        ("req", "sub"),
        split_axis=0,
        concat_axis=0,
        tiled=True,
    ).astype(jnp.float32)
    merged = returned.reshape(expert_count, 2, capacity, model_width)
    expert_out = (merged[:, 0] + merged[:, 1]).astype(jnp.bfloat16)
    expert_flat = expert_out.reshape(-1, model_width)
    mixing_high = mixing.astype(jnp.bfloat16)
    mixing_low = (mixing - mixing_high.astype(jnp.float32)).astype(jnp.bfloat16)
    routed_sum = jnp.dot(mixing_high, expert_flat, preferred_element_type=jnp.float32) + jnp.dot(
        mixing_low, expert_flat, preferred_element_type=jnp.float32
    )
    hidden_out = (residual + routed_sum).astype(jnp.bfloat16)
    return (hidden_out, cache_rows)


def solution(mesh):
    in_specs = (
        P(("req", "sub"), None),
        P(),
        P(),
        P(),
        P(),
        P(),
        P(),
        P(),
        P(),
        P(("req", "sub"), None, None),
        P(("req", "sub"), None, None),
        P(("req", "sub"), None, None),
        P(("req", "sub"), None),
        P(("req", "sub"), None),
        P("req", None),
        P("req"),
        P(),
        P("req", None, None),
    )
    out_specs = (P(("req", "sub"), None), P(("req", "sub"), None))
    return jax.shard_map(local, mesh=mesh, in_specs=in_specs, out_specs=out_specs, check_vma=False)
```

profile of v0, /device:TPU:0, one launch (start us, length us, event | category | flops | bytes accessed | tf_op | source)
XLA Modules:
  0.0 711.4 jit_solution(11006835649669770364)
XLA Ops:
  11.3 2.4 copy.122
  13.7 3.8 select_bitcast_fusion
  19.3 4.4 reduce-window.11
  29.3 2.5 fusion.50
  34.7 4.6 convolution_convert_fusion.2
  39.3 1.9 copy.117
  47.7 2.3 select_reduce_fusion
  50.0 7.9 %all_gather.3 = bf16[512,576]{0,1:T(8,128)(2,1)S(1)} all-gather(bf16[128,576]{0,1:T(8,128)(2,1)S(1)} %pad_maximum_fusion.3), channel_id=1, replica_groups=mesh['req'=32,'sub'=4] {'sub'}, dimensions={0}, use_global_device_ids=true | all-gather | bytes 737280 | tf_op jit(solution)/shard_map/all_gather | solution.py:139
  60.6 2.4 fusion.14
  62.9 328.0 %all-reduce.3.cloned.1.call-done = (bf16[1024,576]{1,0:T(8,128)(2,1)}, bf16[1024,576]{1,0:T(8,128)(2,1)}, bf16[1024,576]{1,0:T(8,128)(2,1)}, bf16[1024,576]{1,0:T(8,128)(2,1)}) async-done(((bf16[1024,576]{1,0:T(8,128)(2,1)}, bf16[1024,576]{1,0:T(8,128)(2,1)}, bf16[1024,576]{1,0:T(8,128)(2,1)}, bf16[1024,576]{1,0:T(8,128)(2,1)}), (bf16[1024,576]{1,0:T(8,128)(2,1)}, bf16[1024,576]{1,0:T(8,128)(2,1)}, ...) | async-done | bytes 4718608 | tf_op jit(solution)/shard_map/psum | solution.py:12
  395.6 2.6 fusion.10
  398.9 5.0 fusion.21
  403.9 3.1 multiply_reduce_fusion.1
  407.1 3.3 convolution_convert_fusion.1
  410.4 6.8 broadcast_in_dim.97
  417.1 109.7 %all_to_all.10 = bf16[128,16,2048]{2,1,0:T(8,128)(2,1)S(1)} all-to-all(bf16[128,16,2048]{2,1,0:T(8,128)(2,1)} %bitcast.94), channel_id=1, replica_groups=mesh['req'=32,'sub'=4] {'req','sub'}, dimensions={0} | all-to-all | bytes 16777216 | tf_op jit(solution)/shard_map/all_to_all | solution.py:176
  526.9 6.3 fusion.6
  533.1 8.1 %multiply_convert_fusion = bf16[2048,704]{0,1:T(8,128)(2,1)} fusion(f32[2048,704]{0,1:T(8,128)S(1)} %fusion.6, bf16[2048,2048]{1,0:T(8,128)(2,1)S(1)} %bitcast.97, bf16[1,2048,704]{1,2,0:T(8,128)(2,1)S(1)} %copy-done.29), kind=kOutput, calls=%fused_computation.2 | convolution fusion | flops 5914230784 | bytes 19922944 | tf_op jit(solution)/shard_map/dot_general | solution.py:68
  541.3 4.6 copy.135
  545.9 11.5 %convolution_convert_fusion = bf16[128,16,2048]{2,0,1:T(8,128)(2,1)} fusion(bf16[128,16,704]{2,1,0:T(8,128)(2,1)} %bitcast.98, bf16[1,704,2048]{2,1,0:T(8,128)(2,1)S(1)} %copy-done), kind=kOutput, calls=%fused_computation.3 | convolution fusion | flops 5909774336 | bytes 14155776 | tf_op jit(solution)/shard_map/dot_general | solution.py:70
  557.4 11.2 %copy.137 = bf16[128,16,2048]{2,1,0:T(8,128)(2,1)} copy(bf16[128,16,2048]{2,0,1:T(8,128)(2,1)} %convolution_convert_fusion) | data formatting | bytes 16777216 | tf_op jit(solution)/shard_map/convert_element_type | solution.py:185
  568.7 114.9 %all_to_all.11 = bf16[128,16,2048]{2,1,0:T(8,128)(2,1)} all-to-all(bf16[128,16,2048]{2,1,0:T(8,128)(2,1)} %copy.137), channel_id=1, replica_groups=mesh['req'=32,'sub'=4] {'req','sub'}, dimensions={0} | all-to-all | bytes 16777216 | tf_op jit(solution)/shard_map/all_to_all | solution.py:184
  683.5 11.2 %convert.26 = f32[64,2,16,2048]{3,2,1,0:T(8,128)} convert(bf16[64,2,16,2048]{3,2,1,0:T(8,128)(2,1)} %bitcast.93) | non-fusion elementwise | flops 4194304 | bytes 25165824 | tf_op jit(solution)/shard_map/reshape | solution.py:191
  694.7 6.6 fusion
  (109 shorter events, 28.2 us)
Async XLA Ops:
  7.2 538.8 %copy-start = (bf16[1,704,2048]{2,1,0:T(8,128)(2,1)S(1)}, bf16[1,704,2048]{2,1,0:T(8,128)(2,1)}, u32[]{:S(2)}) copy-start(bf16[1,704,2048]{2,1,0:T(8,128)(2,1)} %param.29) | copy-start | bytes 8650756
  7.2 383.8 %all-reduce.3.cloned.1.call-start = ((), (), s32[]{:S(2)}) async-start(), calls=%async_computation.2 | async-start | bytes 10485760 | tf_op jit(solution)/shard_map/psum | solution.py:12
  17.5 1.6 copy-start.30
  17.5 11.5 %copy-start.3 = (bf16[128,2048]{1,0:T(8,128)(2,1)S(1)}, bf16[128,2048]{1,0:T(8,128)(2,1)}, u32[]{:S(2)}) copy-start(bf16[128,2048]{1,0:T(8,128)(2,1)} %param.18) | copy-start | bytes 1572868
  17.5 11.7 %copy-start.22 = (f32[2048]{0:T(1024)S(1)}, f32[2048]{0:T(1024)}, u32[]{:S(2)}) copy-start(f32[2048]{0:T(1024)} %param.19) | copy-start | bytes 24580
  25.0 14.3 %copy-start.23 = (s32[512]{0:T(512)}, s32[512]{0:T(512)S(1)}, u32[]{:S(2)}) copy-start(s32[512]{0:T(512)S(1)} %convert_reduce_fusion.1) | copy-start | bytes 6148
  34.7 10.5 %copy-start.27 = (f32[512]{0:T(512)S(1)}, f32[512]{0:T(512)}, u32[]{:S(2)}) copy-start(f32[512]{0:T(512)} %param.22) | copy-start | bytes 6148
  43.0 14.9 %copy-start.24 = (s32[512]{0:T(512)S(1)}, s32[512]{0:T(512)}, u32[]{:S(2)}) copy-start(s32[512]{0:T(512)} %copy-done.23) | copy-start | bytes 6148
  43.0 15.7 %copy-start.20 = (f32[128,32]{1,0:T(8,128)S(1)}, f32[128,32]{1,0:T(8,128)}, u32[]{:S(2)}) copy-start(f32[128,32]{1,0:T(8,128)} %copy.121) | copy-start | bytes 49156
  43.0 15.7 %copy-start.21 = (f32[128,32]{1,0:T(8,128)S(1)}, f32[128,32]{1,0:T(8,128)}, u32[]{:S(2)}) copy-start(f32[128,32]{1,0:T(8,128)} %copy.120) | copy-start | bytes 49156
  43.0 16.0 %copy-start.8 = (bf16[128,1536]{0,1:T(8,128)(2,1)S(1)}, bf16[128,1536]{0,1:T(8,128)(2,1)}, u32[]{:S(2)}) copy-start(bf16[128,1536]{0,1:T(8,128)(2,1)} %copy.117) | copy-start | bytes 1179652
  43.0 16.0 %copy-start.9 = (bf16[8,128,512]{2,1,0:T(8,128)(2,1)S(1)}, bf16[8,128,512]{2,1,0:T(8,128)(2,1)}, u32[]{:S(2)}) copy-start(bf16[8,128,512]{2,1,0:T(8,128)(2,1)} %param.23) | copy-start | bytes 3145732
  47.0 12.5 %copy-start.13 = (bf16[128,576]{0,1:T(8,128)(2,1)}, bf16[128,576]{0,1:T(8,128)(2,1)S(1)}, u32[]{:S(2)}) copy-start(bf16[128,576]{0,1:T(8,128)(2,1)S(1)} %pad_maximum_fusion.3) | copy-start | bytes 442372
  391.0 1.7 copy-start.11
  391.0 1.7 copy-start.17
  391.0 1.7 copy-start.19
  395.6 2.7 copy-start.6
  395.6 2.6 copy-start.15
  403.9 3.2 copy-start.7
  403.9 3.2 copy-start.26
  407.0 3.3 copy-start.1
  417.1 109.7 %copy-start.28 = (bf16[1,2048,704]{1,2,0:T(8,128)(2,1)S(1)}, bf16[1,2048,704]{1,2,0:T(8,128)(2,1)}, u32[]{:S(2)}) copy-start(bf16[1,2048,704]{1,2,0:T(8,128)(2,1)} %param.27) | copy-start | bytes 8650756
  526.9 6.3 copy-start.29
  694.7 6.6 copy-start.4
  (8 other events, 7.6 us)
Sparse Core Ops, SparseCore 0:
  17.7 373.2 all-reduce.2
where the time goes:
time: 724 us; the launch traced here: 711 us
  waiting for transfers between devices  328 us (45%)
  blocking collectives  232 us (32%)
  matrix products  54.1 us (7%)
  other arithmetic  40.4 us (6%)
  local copies, waits for them, and re-layouts  38.3 us (5%)
  between operations  18.1 us (3%)
    psum x1, waiting for transfers between devices, from_root(): return lax.psum(jnp.where(mine, x, jnp.zeros_like(x)), axis)  328 us
    all_to_all x1, blocking collectives, local(): lax.all_to_all(partial_value.reshape(device_count, capacity, model_width)...  115 us
    all_to_all x1, blocking collectives, local(): lax.all_to_all(doubled.reshape(device_count, capacity, model_width), ('re...  110 us
  transfers between devices with their start and end apart: 1, of which 1 were waited for; matrix products, arithmetic and copies ran while one was open for 5% of the time, Pallas kernels for 0%

commit v1 on v0

v1 whole, which is shorter than its diff:
```python
import functools

import jax
import jax.numpy as jnp
import numpy as np
from jax import lax
from jax.experimental import pallas as pl
from jax.experimental.pallas import tpu as pltpu
from jax.sharding import Mesh
from jax.sharding import PartitionSpec as P

EPSILON = 1e-06
FLOOR_SCORE = -1e30
PARTS = 2
CHIP = ("req", "ylo")
BF16 = jnp.bfloat16
F32 = jnp.float32
NT = (((1,), (1,)), ((), ()))


def dot(a, b):
    return jnp.dot(a, b, preferred_element_type=F32)


def dot_nt(a, b):
    return lax.dot_general(a, b, NT, preferred_element_type=F32)


def iota(shape, axis):
    return lax.broadcasted_iota(jnp.int32, shape, axis)


def seg_starts(lengths_ref, pos):
    end_0 = lengths_ref[0, 0]
    end_1 = end_0 + lengths_ref[0, 1]
    return jnp.where(pos >= end_1, end_1, jnp.where(pos >= end_0, end_0, 0))


def route_kernel(depth, ids_ref, gates_ref, place_ref, mix_ref):
    top, rows = ids_ref.shape
    parts, part_slots, _ = place_ref.shape
    experts = part_slots // depth
    e_iota = iota((experts, rows), 0)
    named = jnp.zeros((experts, rows), F32)
    gate = jnp.zeros((experts, rows), F32)
    for k in range(top):
        hit = ids_ref[k : k + 1, :] == e_iota
        named = named + jnp.where(hit, 1.0, 0.0)
        gate = gate + jnp.where(hit, gates_ref[k : k + 1, :], 0.0)
    before = jnp.where(iota((rows, rows), 0) < iota((rows, rows), 1), 1.0, 0.0).astype(BF16)
    rank = dot(named.astype(BF16), before)
    order = (named * (rank + 1.0)).astype(BF16)
    gate_high = gate.astype(BF16)
    gate_low = (gate - gate_high.astype(F32)).astype(BF16)
    owner = iota((part_slots, experts), 0) // depth
    spread = jnp.where(owner == iota((part_slots, experts), 1), 1.0, 0.0).astype(BF16)
    order_at = dot(spread, order)
    high_at = dot(spread, gate_high)
    low_at = dot(spread, gate_low)
    level = (iota((part_slots, rows), 0) % depth).astype(F32)
    for part in range(parts):
        put = order_at == level + (1.0 + part * depth)
        place_ref[part] = jnp.where(put, 1.0, 0.0).astype(BF16)
        mix_ref[part, :rows] = jnp.where(put, high_at, 0.0).T.astype(BF16)
        mix_ref[part, rows:] = jnp.where(put, low_at, 0.0).T.astype(BF16)


def project_kernel(
    lengths_ref, sub_ref, tokens_ref, gain_ref, wq_ref, wl_ref, lgain_ref, wk_ref, inverse_ref,
    cache_ref, query_ref, normed, angle,
):
    rows = tokens_ref.shape[0]
    heads, nope, lat = wk_ref.shape
    rope = wl_ref.shape[0] - lat
    half = rope // 2

    @pl.when(pl.program_id(0) == 0)
    def _():
        x = tokens_ref[...].astype(F32)
        scale = lax.rsqrt(jnp.mean(x * x, axis=-1, keepdims=True) + EPSILON)
        normed[...] = (x * scale * gain_ref[...]).astype(BF16)
        pos = sub_ref[0] * rows + iota((half, rows), 1)
        offset = sub_ref[1] + pos - seg_starts(lengths_ref, pos)
        angles = offset.astype(F32) * inverse_ref[...]
        cos_part = jnp.cos(angles)
        sin_part = jnp.sin(angles)
        angle[...] = jnp.concatenate([cos_part, sin_part], axis=0).T
        latent = dot_nt(wl_ref[...], normed[...])
        low = latent[:lat]
        scale = lax.rsqrt(jnp.mean(low * low, axis=0, keepdims=True) + EPSILON)
        gain = jnp.broadcast_to(lgain_ref[...], (rows, lat)).T
        cache_ref[:lat] = (low * scale * gain).astype(BF16)
        first = latent[lat : lat + half]
        second = latent[lat + half :]
        cache_ref[lat : lat + half] = (first * cos_part - second * sin_part).astype(BF16)
        cache_ref[lat + half :] = (second * cos_part + first * sin_part).astype(BF16)

    queries = dot(normed[...], wq_ref[...]).astype(BF16)
    cos_part = angle[:, :half]
    sin_part = angle[:, half:]
    for h in range(heads):
        base = h * (nope + rope)
        query_ref[h, :, :lat] = dot(queries[:, base : base + nope], wk_ref[h]).astype(BF16)
        first = queries[:, base + nope : base + nope + half].astype(F32)
        second = queries[:, base + nope + half : base + nope + rope].astype(F32)
        query_ref[h, :, lat:] = jnp.concatenate(
            [first * cos_part - second * sin_part, second * cos_part + first * sin_part], axis=1
        ).astype(BF16)


def attend_kernel(
    score_scale, lengths_ref, sub_ref, query_ref, own_ref, back_1_ref, back_2_ref, back_3_ref, near_ref, far_ref,
    wv_ref, wo_ref, tokens_ref, gain_ref, place_ref,
    residual_ref, mid_ref, out_ref, keys, bias,
):
    rows = tokens_ref.shape[0]
    heads, _, width = query_ref.shape
    lat = wv_ref.shape[1]
    step = pl.program_id(0)
    tiles = near_ref.shape[0] + far_ref.shape[0]
    suffix = (own_ref, back_1_ref, back_2_ref, back_3_ref)

    @pl.when(step == 0)
    def _():
        for i in range(near_ref.shape[0]):
            keys[:, i * rows : (i + 1) * rows] = near_ref[i]
        for i in range(far_ref.shape[0]):
            at = (near_ref.shape[0] + i) * rows
            keys[:, at : at + rows] = far_ref[i]
        pos = sub_ref[0] * rows + iota((rows, rows), 0)
        start = seg_starts(lengths_ref, pos)
        for d, ref in enumerate(suffix):
            keys[:, (tiles + d) * rows : (tiles + d + 1) * rows] = ref[...]
            key_pos = ((sub_ref[0] + len(suffix) - d) % len(suffix)) * rows + iota((rows, rows), 1)
            allowed = (key_pos >= start) & (key_pos <= pos)
            bias[:, d * rows : (d + 1) * rows] = jnp.where(allowed, 0.0, FLOOR_SCORE)
        residual_ref[...] = tokens_ref[...].astype(F32)

    query = query_ref[...].reshape(heads * rows, width)
    scores = dot(query, keys[...]) * score_scale
    cut = tiles * rows
    mask = jnp.concatenate([bias[...]] * heads, axis=0)
    scores = jnp.concatenate([scores[:, :cut], scores[:, cut:] + mask], axis=1)
    weights = jnp.exp(scores - jnp.max(scores, axis=1, keepdims=True))
    denominator = jnp.sum(weights, axis=1, keepdims=True)
    latent_out = (dot_nt(weights.astype(BF16), keys[:lat]) / denominator).astype(BF16)
    head_out = jnp.concatenate(
        [dot(latent_out[h * rows : (h + 1) * rows], wv_ref[h]).astype(BF16) for h in range(heads)],
        axis=1,
    )
    residual_ref[...] += dot(head_out, wo_ref[...])

    @pl.when(step == pl.num_programs(0) - 1)
    def _():
        x = residual_ref[...]
        scale = lax.rsqrt(jnp.mean(x * x, axis=-1, keepdims=True) + EPSILON)
        mid = (x * scale * gain_ref[...]).astype(BF16)
        mid_ref[...] = mid
        out_ref[...] = dot(place_ref[...], mid).astype(BF16)


def place_kernel(place_ref, mid_ref, out_ref):
    out_ref[...] = dot(place_ref[...], mid_ref[...]).astype(BF16)


def expert_kernel(x_ref, g0, u0, d0, g1, u1, d1, out_ref, buf, sems):
    copies = [
        pltpu.make_async_copy(src, buf.at[i], sems.at[i])
        for i, src in enumerate((g0, u0, g1, u1, d0, d1))
    ]
    for copy in copies:
        copy.start()
    activated = []
    for half in range(2):
        copies[2 * half].wait()
        gate = dot_nt(x_ref[...], buf[2 * half])
        copies[2 * half + 1].wait()
        up = dot_nt(x_ref[...], buf[2 * half + 1])
        activated.append((gate / (1.0 + jnp.exp(-gate)) * up).astype(BF16))
    copies[4].wait()
    total = dot(activated[0], buf[4])
    copies[5].wait()
    out_ref[...] = (total + dot(activated[1], buf[5])).astype(BF16)


def mix_kernel(base_ref, mix_ref, rows_ref, out_ref):
    rows = base_ref.shape[0]
    both = dot(mix_ref[...], rows_ref[...])
    out_ref[...] = (base_ref[...] + (both[:rows] + both[rows:])).astype(out_ref.dtype)


def cost(flops, moved):
    return pl.CostEstimate(flops=int(flops), bytes_accessed=int(moved), transcendentals=0)


SMEM = pl.BlockSpec(memory_space=pltpu.SMEM)


def whole(array):
    return pl.BlockSpec(array.shape, lambda *_: (0,) * array.ndim)


def local(
    tokens, attn_gain, w_query, w_latent, latent_gain, w_key_up, w_value_up, w_out, moe_gain,
    w_gate, w_up, w_down, expert_ids, gate_weights, lengths, slab_group, owners, prefix_pool,
):
    rows, model = tokens.shape
    head_count, nope, lat = w_key_up.shape
    width = w_latent.shape[1]
    rope = width - lat
    value = w_value_up.shape[2]
    prefix_len = prefix_pool.shape[1]
    hidden = w_down.shape[1]
    top = expert_ids.shape[1]
    req_count = lax.axis_size("req")
    core_count = lax.axis_size("core")
    sub_count = lax.axis_size("ylo") * core_count
    chips = req_count * lax.axis_size("ylo")
    sub = lax.axis_index("ylo") * core_count + lax.axis_index("core")
    place_info = jnp.stack([sub, jnp.int32(prefix_len)]).astype(jnp.int32)

    quarter_len = prefix_len // sub_count
    quarter = lax.dynamic_slice(prefix_pool[0].T, (0, sub * quarter_len), (width, quarter_len))
    lanes = 128
    piece = width * quarter_len // lanes // req_count
    pieces = (
        quarter.reshape(width, quarter_len // lanes, lanes).transpose(1, 0, 2)
        .reshape(req_count, piece, lanes)
    )
    tag_rows = -piece % 8 or 8
    tag = jnp.broadcast_to(slab_group[0].astype(BF16), (req_count, tag_rows, lanes))
    spread = lax.all_to_all(
        jnp.concatenate([pieces, tag], axis=1), "req", split_axis=0, concat_axis=0, tiled=True
    )
    groups = spread[:, piece, 0].astype(jnp.int32)
    slots = jnp.sum(
        jnp.where(
            groups[:, None] == jnp.arange(owners.shape[0], dtype=jnp.int32)[None, :], owners[None, :], 0
        ),
        axis=1,
    )
    picked = jnp.take(spread, slots, axis=0, mode="clip")
    ylo_count = lax.axis_size("ylo")
    doubled = jnp.broadcast_to(picked[:, None], (req_count, ylo_count) + picked.shape[1:])
    near = lax.all_to_all(
        doubled.reshape((chips,) + picked.shape[1:]), CHIP, split_axis=0, concat_axis=0, tiled=True
    )
    near = near[:, :piece].reshape(req_count, ylo_count, piece, lanes).transpose(1, 0, 2, 3)
    near = near.reshape(ylo_count * quarter_len // lanes, width, lanes)
    swap = [(0, 1), (1, 0)]
    far = lax.ppermute(near, "core", swap)

    gate_t = w_gate[0].T
    up_t = w_up[0].T
    down = w_down[0]
    gate_far = lax.ppermute(gate_t, "core", swap)
    up_far = lax.ppermute(up_t, "core", swap)
    down_far = lax.ppermute(down, "core", swap)

    pair = 2
    steps = head_count // pair
    inverse = (10000.0 ** (-np.arange(rope // 2) / (rope // 2))).astype(np.float32)
    inverse = jnp.broadcast_to(jnp.asarray(inverse)[:, None], (rope // 2, rows))
    w_latent_t = w_latent.T
    gain_row = attn_gain[None, :]
    lgain_row = latent_gain[None, :]
    cache_t, query_full = pl.pallas_call(
        project_kernel,
        name="project",
        grid=(steps,),
        in_specs=[
            SMEM, SMEM, whole(tokens), whole(gain_row),
            pl.BlockSpec((model, pair * (nope + rope)), lambda i: (0, i)),
            whole(w_latent_t), whole(lgain_row),
            pl.BlockSpec((pair, nope, lat), lambda i: (i, 0, 0)),
            whole(inverse),
        ],
        out_specs=[
            pl.BlockSpec((width, rows), lambda i: (0, 0)),
            pl.BlockSpec((pair, rows, width), lambda i: (i, 0, 0)),
        ],
        out_shape=[
            jax.ShapeDtypeStruct((width, rows), BF16),
            jax.ShapeDtypeStruct((head_count, rows, width), BF16),
        ],
        scratch_shapes=[pltpu.VMEM((rows, model), BF16), pltpu.VMEM((rows, rope), F32)],
        cost_estimate=cost(2 * rows * model * (w_query.shape[1] + width), 14e6),
    )(lengths, place_info, tokens, gain_row, w_query, w_latent_t, lgain_row, w_key_up, inverse)

    back = [
        lax.ppermute(cache_t, ("ylo", "core"), [(k, (k + d) % sub_count) for k in range(sub_count)])
        for d in range(1, sub_count)
    ]

    slot_count = 4 * rows * top // 3
    part_slots = slot_count // PARTS
    depth = part_slots // chips
    ids_t = expert_ids.T
    gates_t = gate_weights.T
    placing, mixing = pl.pallas_call(
        functools.partial(route_kernel, depth),
        name="route",
        in_specs=[whole(ids_t), whole(gates_t)],
        out_specs=[
            pl.BlockSpec((PARTS, part_slots, rows), lambda: (0, 0, 0)),
            pl.BlockSpec((PARTS, 2 * rows, part_slots), lambda: (0, 0, 0)),
        ],
        out_shape=[
            jax.ShapeDtypeStruct((PARTS, part_slots, rows), BF16),
            jax.ShapeDtypeStruct((PARTS, 2 * rows, part_slots), BF16),
        ],
        cost_estimate=cost(1e9, 2e6),
    )(ids_t, gates_t)

    moe_row = moe_gain[None, :]
    residual, mid, first_out = pl.pallas_call(
        functools.partial(attend_kernel, (nope + rope) ** (-0.5)),
        name="attend",
        grid=(steps,),
        in_specs=[
            SMEM, SMEM,
            pl.BlockSpec((pair, rows, width), lambda i: (i, 0, 0)),
            whole(cache_t), whole(cache_t), whole(cache_t), whole(cache_t), whole(near), whole(far),
            pl.BlockSpec((pair, lat, value), lambda i: (i, 0, 0)),
            pl.BlockSpec((pair * value, model), lambda i: (i, 0)),
            whole(tokens), whole(moe_row),
            pl.BlockSpec((None, part_slots, rows), lambda i: (0, 0, 0)),
        ],
        out_specs=[
            pl.BlockSpec((rows, model), lambda i: (0, 0)),
            pl.BlockSpec((rows, model), lambda i: (0, 0)),
            pl.BlockSpec((part_slots, model), lambda i: (0, 0)),
        ],
        out_shape=[
            jax.ShapeDtypeStruct((rows, model), F32),
            jax.ShapeDtypeStruct((rows, model), BF16),
            jax.ShapeDtypeStruct((part_slots, model), BF16),
        ],
        scratch_shapes=[
            pltpu.VMEM((width, prefix_len + rows * sub_count), BF16),
            pltpu.VMEM((rows, rows * sub_count), F32),
        ],
        cost_estimate=cost(8e9, 14e6),
    )(
        lengths, place_info, query_full, cache_t, *back, near, far,
        w_value_up, w_out, tokens, moe_row, placing,
    )

    def exchange(x):
        x = x.reshape(chips, depth, model)
        return lax.all_to_all(x, CHIP, split_axis=0, concat_axis=0, tiled=True).reshape(part_slots, model)

    def place(part):
        return pl.pallas_call(
            place_kernel,
            name="place",
            grid=(2,),
            in_specs=[
                pl.BlockSpec((None, part_slots // 2, rows), lambda i: (part, i, 0)), whole(mid),
            ],
            out_specs=pl.BlockSpec((part_slots // 2, model), lambda i: (i, 0)),
            out_shape=jax.ShapeDtypeStruct((part_slots, model), BF16),
            cost_estimate=cost(2 * part_slots * rows * model, 3e6),
        )(placing, mid)

    any_spec = pl.BlockSpec(memory_space=pl.ANY)

    def experts(x):
        return pl.pallas_call(
            expert_kernel,
            name="experts",
            in_specs=[whole(x)] + [any_spec] * 6,
            out_specs=pl.BlockSpec((part_slots, model), lambda: (0, 0)),
            out_shape=jax.ShapeDtypeStruct((part_slots, model), BF16),
            scratch_shapes=[
                pltpu.VMEM((6, hidden, model), BF16), pltpu.SemaphoreType.DMA((6,)),
            ],
            cost_estimate=cost(12 * part_slots * model * hidden, 21e6),
        )(x, gate_t, up_t, down, gate_far, up_far, down_far)

    blocks = 4

    def mix(base, part, x, dtype):
        return pl.pallas_call(
            mix_kernel,
            name="mix",
            grid=(blocks,),
            in_specs=[
                pl.BlockSpec((rows, model // blocks), lambda i: (0, i)),
                pl.BlockSpec((None, 2 * rows, part_slots), lambda i: (part, 0, 0)),
                pl.BlockSpec((part_slots, model // blocks), lambda i: (0, i)),
            ],
            out_specs=pl.BlockSpec((rows, model // blocks), lambda i: (0, i)),
            out_shape=jax.ShapeDtypeStruct((rows, model), dtype),
            cost_estimate=cost(4 * part_slots * rows * model, 5e6),
        )(base, mixing, x)

    outbound = [first_out] + [place(part) for part in range(1, PARTS)]
    arrived = [exchange(x) for x in outbound]
    returned = [exchange(experts(x)) for x in arrived]
    total = residual
    for part in range(PARTS):
        total = mix(total, part, returned[part], BF16 if part == PARTS - 1 else F32)
    return (total, cache_t.T)


def solution(mesh):
    split = Mesh(mesh.devices.reshape(mesh.devices.shape[0], -1, 2), ("req", "ylo", "core"))
    every = ("req", "ylo", "core")
    in_specs = (
        P(every, None), P(), P(), P(), P(), P(), P(), P(), P(),
        P(every, None, None), P(every, None, None), P(every, None, None),
        P(every, None), P(every, None), P("req", None), P("req"), P(), P("req", None, None),
    )
    out_specs = (P(every, None), P(every, None))
    return jax.shard_map(local, mesh=split, in_specs=in_specs, out_specs=out_specs, check_vma=False)
```

time: 724 us -> 223 us (0.31); the launches traced: 711 us -> 223 us
  waiting for transfers between devices: 328 us -> 73.9 us
  blocking collectives: 232 us -> 39 us
  Pallas kernels: 0 us -> 70.7 us
  matrix products: 54.1 us -> 0 us
  other arithmetic: 40.4 us -> 1.35 us
  local copies, waits for them, and re-layouts: 38.3 us -> 7.09 us
  starting transfers between devices: 0.04 us -> 29 us
  between operations: 18.1 us -> 1.49 us
    psum x1 -> x0, waiting for transfers between devices: 328 us -> none  [from_root(): return lax.psum(jnp.where(mine, x, jnp.zeros_like(x)), axis)]
    all_to_all x2, blocking collectives: 225 us -> 39 us  [the longest x1 21.9 us: local(): lax.all_to_all(jnp.concatenate([pieces, tag], axis=1), 'req', split_axis=...]
    pallas_call x0 -> x8, Pallas kernels: none -> 70.7 us  [the longest x2 35.6 us: experts(): pl.pallas_call(expert_kernel, name='experts', in_specs=[whole(x)] + [any_...]
    all_to_all x0 -> x4, waiting for transfers between devices: none -> 70.3 us  [exchange(): lax.all_to_all(x, CHIP, split_axis=0, concat_axis=0, tiled=True)]
    dot_general x14 -> x0, matrix products: 54.1 us -> none  [the longest x1 11.5 us: expert_half(): return jnp.dot(activated, down_half, preferred_element_type=jnp.float32)]
    all_to_all x0 -> x4, starting transfers between devices: none -> 25.1 us  [exchange(): lax.all_to_all(x, CHIP, split_axis=0, concat_axis=0, tiled=True)]
    convert_element_type x3 -> x0, local copies, waits for them, and re-layouts: 17.8 us -> none  [the longest x1 11.2 us: local(): partial_value.reshape(device_count, capacity, model_width)]
    reshape x1 -> x0, other arithmetic: 11.2 us -> none  [local(): merged = returned.reshape(expert_count, 2, capacity, model_width)]
  transfers between devices with their start and end apart: 1 -> 11, of which waited for: 1 -> 7; matrix products, arithmetic and copies ran while one was open for 5% -> 1% of each run, Pallas kernels for 0% -> 24%
where the time goes in v1:
time: 223 us
  waiting for transfers between devices  73.9 us (33%)
  Pallas kernels  70.7 us (32%)
  blocking collectives  39 us (17%)
  starting transfers between devices  29 us (13%)
  local copies, waits for them, and re-layouts  7.09 us (3%)
    all_to_all x4, waiting for transfers between devices, exchange(): lax.all_to_all(x, CHIP, split_axis=0, concat_axis=0, tiled=True)  70.3 us
    pallas_call x2, Pallas kernels, experts(): pl.pallas_call(expert_kernel, name='experts', in_specs=[whole(x)] + [any_...  35.6 us
    all_to_all x4, starting transfers between devices, exchange(): lax.all_to_all(x, CHIP, split_axis=0, concat_axis=0, tiled=True)  25.1 us
    all_to_all x1, blocking collectives, local(): lax.all_to_all(jnp.concatenate([pieces, tag], axis=1), 'req', split_axis=...  21.9 us
    all_to_all x1, blocking collectives, local(): lax.all_to_all(doubled.reshape((chips,) + picked.shape[1:]), CHIP, split_...  17.1 us
    pallas_call x1, Pallas kernels, local(): pl.pallas_call(functools.partial(attend_kernel, (nope + rope) ** (-0.5)),...  13.1 us
    pallas_call x2, Pallas kernels, mix(): pl.pallas_call(mix_kernel, name='mix', grid=(blocks,), in_specs=[pl.Block...  8.7 us
    pallas_call x1, Pallas kernels, local(): pl.pallas_call(project_kernel, name='project', grid=(steps,), in_specs=[S...  8.19 us
  transfers between devices with their start and end apart: 11, of which 7 were waited for; matrix products, arithmetic and copies ran while one was open for 1% of the time, Pallas kernels for 24%

profile of v1, /device:TPU:0, one launch (start us, length us, event | category | flops | bytes accessed | tf_op | source)
XLA Modules:
  0.0 222.5 jit_solution(7929780593227174379)
XLA Ops:
  0.7 1.2 copy-done
  2.8 21.9 %all_to_all.30 = bf16[32,40,128]{2,1,0:T(8,128)(2,1)S(1)} all-to-all(bf16[32,40,128]{2,1,0:T(8,128)(2,1)S(1)} %concatenate.3), channel_id=1, replica_groups=mesh['req'=32,'ylo'=2,'core'=2] {'req'}, dimensions={0} | all-to-all | bytes 655360 | tf_op jit(solution)/shard_map/all_to_all | solution.py:232
  26.2 17.1 %all_to_all.31 = bf16[64,40,128]{2,1,0:T(8,128)(2,1)S(1)} all-to-all(bf16[64,40,128]{2,1,0:T(8,128)(2,1)S(1)} %bitcast.36), channel_id=1, replica_groups=mesh['req'=32,'ylo'=2,'core'=2] {'req','ylo'}, dimensions={0} | all-to-all | bytes 1310720 | tf_op jit(solution)/shard_map/all_to_all | solution.py:245
  45.4 8.2 %project.1 = (bf16[576,128]{1,0:T(8,128)(2,1)}, bf16[8,128,576]{2,1,0:T(8,128)(2,1)}) custom-call(s32[1,3]{1,0:T(1,128)} %lengths_ref.3, s32[2]{0:T(128)} %pad_add_fusion.sub_ref, bf16[128,2048]{1,0:T(8,128)(2,1)} %tokens_ref.3, f32[1,2048]{1,0:T(1,128)} %bitcast.45, bf16[2048,1536]{1,0:T(8,128)(2,1)} %wq_ref.1, bf16[576,2048]{1,0:T(8,128)(2,1)} %bitcast.38, ...), custom_call_target="tpu_custom_call" | custom-call | flops 1107296256 | bytes 14000000 | tf_op jit(solution)/shard_map/project/pallas_call | solution.py:267
  55.8 2.1 route.1
  57.9 1.0 collective-permute-done.back_1_ref
  58.9 2.1 collective-permute-done.1.back_2_ref
  62.3 13.1 %attend.1 = (f32[128,2048]{1,0:T(8,128)}, bf16[128,2048]{1,0:T(8,128)(2,1)}, bf16[512,2048]{1,0:T(8,128)(2,1)}) custom-call(s32[1,3]{1,0:T(1,128)} %lengths_ref.3, s32[2]{0:T(128)} %pad_add_fusion.sub_ref, bf16[8,128,576]{2,1,0:T(8,128)(2,1)} %get-tuple-element.9.query_ref, bf16[576,128]{1,0:T(8,128)(2,1)} %get-tuple-element.10.own_ref, ...), custom_call_target="tpu_custom_call" | custom-call | flops 8000000000 | bytes 14000000 | tf_op jit(solution)/shard_map/attend/pallas_call | solution.py:316
  75.4 5.8 %all-to-all-start.2 = ((bf16[64,8,2048]{2,1,0:T(8,128)(2,1)}), bf16[64,8,2048]{2,1,0:T(8,128)(2,1)S(1)}, u32[]{:S(2)}, u32[]{:S(2)}) async-start(bf16[64,8,2048]{2,1,0:T(8,128)(2,1)} %bitcast.41), calls=%async_computation.2 | async-start | bytes 4194304 | tf_op jit(solution)/shard_map/all_to_all | solution.py:351
  81.3 1.2 collective-permute-start.4
  83.0 2.9 %place.1 = bf16[512,2048]{1,0:T(8,128)(2,1)} custom-call(bf16[2,512,128]{2,1,0:T(8,128)(2,1)} %get-tuple-element.11.place_ref, bf16[128,2048]{1,0:T(8,128)(2,1)} %get-tuple-element.15.mid_ref), custom_call_target="tpu_custom_call" | custom-call | flops 268435456 | bytes 3000000 | tf_op jit(solution)/shard_map/place/pallas_call | solution.py:354
  85.9 26.2 %all-to-all-done.2 = bf16[64,8,2048]{2,1,0:T(8,128)(2,1)S(1)} async-done(((bf16[64,8,2048]{2,1,0:T(8,128)(2,1)}), bf16[64,8,2048]{2,1,0:T(8,128)(2,1)S(1)}, u32[]{:S(2)}, u32[]{:S(2)}) %all-to-all-start.2) | async-done | bytes 2097184 | tf_op jit(solution)/shard_map/all_to_all | solution.py:351
  112.1 1.4 copy-done.2
  113.5 6.2 %all-to-all-start.4 = ((bf16[64,8,2048]{2,1,0:T(8,128)(2,1)}), bf16[64,8,2048]{2,1,0:T(8,128)(2,1)}, u32[]{:S(2)}, u32[]{:S(2)}) async-start(bf16[64,8,2048]{2,1,0:T(8,128)(2,1)} %bitcast.34), calls=%async_computation.4 | async-start | bytes 4194304 | tf_op jit(solution)/shard_map/all_to_all | solution.py:351
  119.8 17.8 %experts.2 = bf16[512,2048]{1,0:T(8,128)(2,1)} custom-call(bf16[512,2048]{1,0:T(8,128)(2,1)} %bitcast.40, bf16[704,2048]{1,0:T(8,128)(2,1)} %bitcast.48, bf16[704,2048]{1,0:T(8,128)(2,1)} %bitcast.51, bf16[704,2048]{1,0:T(8,128)(2,1)} %bitcast.54, bf16[704,2048]{1,0:T(8,128)(2,1)} %collective-permute-done.4.g1, bf16[704,2048]{1,0:T(8,128)(2,1)} %collective-permute-done.5.u1, ...), custom_call_target="tpu_custom_call" | custom-call | flops 8858370048 | bytes 21000000 | tf_op jit(solution)/shard_map/experts/pallas_call | solution.py:369
  137.6 11.2 %all-to-all-done.4 = bf16[64,8,2048]{2,1,0:T(8,128)(2,1)} async-done(((bf16[64,8,2048]{2,1,0:T(8,128)(2,1)}), bf16[64,8,2048]{2,1,0:T(8,128)(2,1)}, u32[]{:S(2)}, u32[]{:S(2)}) %all-to-all-start.4) | async-done | bytes 2097184 | tf_op jit(solution)/shard_map/all_to_all | solution.py:351
  148.8 6.4 %all-to-all-start.3 = ((bf16[64,8,2048]{2,1,0:T(8,128)(2,1)}), bf16[64,8,2048]{2,1,0:T(8,128)(2,1)S(1)}, u32[]{:S(2)}, u32[]{:S(2)}) async-start(bf16[64,8,2048]{2,1,0:T(8,128)(2,1)} %bitcast.43), calls=%async_computation.3 | async-start | bytes 4194304 | tf_op jit(solution)/shard_map/all_to_all | solution.py:351
  155.2 17.9 %experts.3 = bf16[512,2048]{1,0:T(8,128)(2,1)} custom-call(bf16[512,2048]{1,0:T(8,128)(2,1)} %bitcast.26.x_ref, bf16[704,2048]{1,0:T(8,128)(2,1)} %bitcast.49, bf16[704,2048]{1,0:T(8,128)(2,1)} %bitcast.52, bf16[704,2048]{1,0:T(8,128)(2,1)} %bitcast.55, bf16[704,2048]{1,0:T(8,128)(2,1)} %collective-permute-done.4.g1, ...), custom_call_target="tpu_custom_call" | custom-call | flops 8858370048 | bytes 21000000 | tf_op jit(solution)/shard_map/experts/pallas_call | solution.py:369
  173.1 10.1 %all-to-all-done.3 = bf16[64,8,2048]{2,1,0:T(8,128)(2,1)S(1)} async-done(((bf16[64,8,2048]{2,1,0:T(8,128)(2,1)}), bf16[64,8,2048]{2,1,0:T(8,128)(2,1)S(1)}, u32[]{:S(2)}, u32[]{:S(2)}) %all-to-all-start.3) | async-done | bytes 2097184 | tf_op jit(solution)/shard_map/all_to_all | solution.py:351
  183.1 1.3 copy-done.1
  184.4 6.6 %all-to-all-start.5 = ((bf16[64,8,2048]{2,1,0:T(8,128)(2,1)}), bf16[64,8,2048]{2,1,0:T(8,128)(2,1)}, u32[]{:S(2)}, u32[]{:S(2)}) async-start(bf16[64,8,2048]{2,1,0:T(8,128)(2,1)} %bitcast.42), calls=%async_computation.5 | async-start | bytes 4194304 | tf_op jit(solution)/shard_map/all_to_all | solution.py:351
  191.1 4.4 %mix.2.base_ref = f32[128,2048]{1,0:T(8,128)} custom-call(f32[128,2048]{1,0:T(8,128)} %get-tuple-element.12.base_ref, bf16[2,256,512]{2,1,0:T(8,128)(2,1)} %get-tuple-element.13.mix_ref, bf16[512,2048]{1,0:T(8,128)(2,1)} %bitcast.35), custom_call_target="tpu_custom_call" | custom-call | flops 536870912 | bytes 5000000 | tf_op jit(solution)/shard_map/mix/pallas_call | solution.py:384
  195.5 22.8 %all-to-all-done.5 = bf16[64,8,2048]{2,1,0:T(8,128)(2,1)} async-done(((bf16[64,8,2048]{2,1,0:T(8,128)(2,1)}), bf16[64,8,2048]{2,1,0:T(8,128)(2,1)}, u32[]{:S(2)}, u32[]{:S(2)}) %all-to-all-start.5) | async-done | bytes 2097184 | tf_op jit(solution)/shard_map/all_to_all | solution.py:351
  218.2 4.3 %mix.3 = bf16[128,2048]{1,0:T(8,128)(2,1)} custom-call(f32[128,2048]{1,0:T(8,128)} %mix.2.base_ref, bf16[2,256,512]{2,1,0:T(8,128)(2,1)} %get-tuple-element.13.mix_ref, bf16[512,2048]{1,0:T(8,128)(2,1)} %bitcast.28.rows_ref), custom_call_target="tpu_custom_call" | custom-call | flops 536870912 | bytes 5000000 | tf_op jit(solution)/shard_map/mix/pallas_call | solution.py:384
  (43 shorter events, 7.7 us)
Async XLA Ops:
  0.6 1.3 copy-start
  0.6 24.7 %copy-start.9 = (s32[4]{0:T(128)S(1)}, s32[4]{0:T(128)}, u32[]{:S(2)}) copy-start(s32[4]{0:T(128)} %param.35) | copy-start | bytes 52
  43.3 1.4 copy-start.4
  44.0 9.6 %copy-start.3 = (bf16[4,576,128]{2,1,0:T(8,128)(2,1)}, bf16[4,576,128]{2,1,0:T(8,128)(2,1)S(1)}, u32[]{:S(2)}) copy-start(bf16[4,576,128]{2,1,0:T(8,128)(2,1)S(1)} %reshape.62.near_ref) | copy-start | bytes 1769476
  44.0 17.4 %collective-permute-start.3 = (bf16[4,576,128]{2,1,0:T(8,128)(2,1)S(1)}, bf16[4,576,128]{2,1,0:T(8,128)(2,1)S(1)}, u32[]{:S(2)}, u32[]{:S(2)}) collective-permute-start(bf16[4,576,128]{2,1,0:T(8,128)(2,1)S(1)} %reshape.62.near_ref), channel_id=1, source_target_pairs={{0,1},{1,0},{2,3},{3,2},{4,5},{5,4},{6,7},{7,6},{8,9},{9,8},{10,11... | collective-permute-start | bytes 1769480 | tf_op jit(solution)/shard_map/ppermute | solution.py:251
  53.5 5.4 %collective-permute-start = (bf16[576,128]{1,0:T(8,128)(2,1)}, bf16[576,128]{1,0:T(8,128)(2,1)S(1)}, u32[]{:S(2)}, u32[]{:S(2)}) collective-permute-start(bf16[576,128]{1,0:T(8,128)(2,1)} %get-tuple-element.10.own_ref), channel_id=1, source_target_pairs={{0,1},{1,2},{2,3},{3,0},{4,5},{5,6},{6,7},{7,4},{8,9},{9,10},{10,1... | collective-permute-start | bytes 442376 | tf_op jit(solution)/shard_map/ppermute | solution.py:291
  54.1 6.9 %collective-permute-start.1 = (bf16[576,128]{1,0:T(8,128)(2,1)}, bf16[576,128]{1,0:T(8,128)(2,1)S(1)}, u32[]{:S(2)}, u32[]{:S(2)}) collective-permute-start(bf16[576,128]{1,0:T(8,128)(2,1)} %get-tuple-element.10.own_ref), channel_id=1, source_target_pairs={{0,2},{1,3},{2,0},{3,1},{4,6},{5,7},{6,4},{7,5},{8,10},{9,11},{10,... | collective-permute-start | bytes 442376 | tf_op jit(solution)/shard_map/ppermute | solution.py:291
  54.8 6.7 %collective-permute-start.2 = (bf16[576,128]{1,0:T(8,128)(2,1)}, bf16[576,128]{1,0:T(8,128)(2,1)S(1)}, u32[]{:S(2)}, u32[]{:S(2)}) collective-permute-start(bf16[576,128]{1,0:T(8,128)(2,1)} %get-tuple-element.10.own_ref), channel_id=1, source_target_pairs={{0,3},{1,0},{2,1},{3,2},{4,7},{5,4},{6,5},{7,6},{8,11},{9,8},{10,9... | collective-permute-start | bytes 442376 | tf_op jit(solution)/shard_map/ppermute | solution.py:291
  58.9 2.5 %copy-start.6 = (bf16[576,128]{1,0:T(8,128)(2,1)}, bf16[576,128]{1,0:T(8,128)(2,1)S(1)}, u32[]{:S(2)}) copy-start(bf16[576,128]{1,0:T(8,128)(2,1)S(1)} %collective-permute-done.back_1_ref) | copy-start | bytes 442372
  61.0 0.7 copy-start.7
  61.4 0.7 copy-start.8
  61.4 0.9 copy-start.5
  75.4 36.7 %all-to-all-start.2 = ((bf16[64,8,2048]{2,1,0:T(8,128)(2,1)}), bf16[64,8,2048]{2,1,0:T(8,128)(2,1)S(1)}, u32[]{:S(2)}, u32[]{:S(2)}) async-start(bf16[64,8,2048]{2,1,0:T(8,128)(2,1)} %bitcast.41), calls=%async_computation.2 | async-start | bytes 4194304 | tf_op jit(solution)/shard_map/all_to_all | solution.py:351
  81.3 38.5 %collective-permute-start.4 = (bf16[704,2048]{1,0:T(8,128)(2,1)}, bf16[704,2048]{1,0:T(8,128)(2,1)}, u32[]{:S(2)}, u32[]{:S(2)}) collective-permute-start(bf16[704,2048]{1,0:T(8,128)(2,1)} %bitcast.47), channel_id=1, source_target_pairs={{0,1},{1,0},{2,3},{3,2},{4,5},{5,4},{6,7},{7,6},{8,9},{9,8},{10,11... | collective-permute-start | bytes 8650760 | tf_op jit(solution)/shard_map/ppermute | solution.py:256
  82.5 37.3 %collective-permute-start.5 = (bf16[704,2048]{1,0:T(8,128)(2,1)}, bf16[704,2048]{1,0:T(8,128)(2,1)}, u32[]{:S(2)}, u32[]{:S(2)}) collective-permute-start(bf16[704,2048]{1,0:T(8,128)(2,1)} %bitcast.50), channel_id=1, source_target_pairs={{0,1},{1,0},{2,3},{3,2},{4,5},{5,4},{6,7},{7,6},{8,9},{9,8},{10,11... | collective-permute-start | bytes 8650760 | tf_op jit(solution)/shard_map/ppermute | solution.py:257
  82.6 37.2 %collective-permute-start.6 = (bf16[704,2048]{1,0:T(8,128)(2,1)}, bf16[704,2048]{1,0:T(8,128)(2,1)}, u32[]{:S(2)}, u32[]{:S(2)}) collective-permute-start(bf16[704,2048]{1,0:T(8,128)(2,1)} %bitcast.53), channel_id=1, source_target_pairs={{0,1},{1,0},{2,3},{3,2},{4,5},{5,4},{6,7},{7,6},{8,9},{9,8},{10,11... | collective-permute-start | bytes 8650760 | tf_op jit(solution)/shard_map/ppermute | solution.py:258
  112.1 1.4 copy-start.2
  113.5 35.3 %all-to-all-start.4 = ((bf16[64,8,2048]{2,1,0:T(8,128)(2,1)}), bf16[64,8,2048]{2,1,0:T(8,128)(2,1)}, u32[]{:S(2)}, u32[]{:S(2)}) async-start(bf16[64,8,2048]{2,1,0:T(8,128)(2,1)} %bitcast.34), calls=%async_computation.4 | async-start | bytes 4194304 | tf_op jit(solution)/shard_map/all_to_all | solution.py:351
  148.8 34.3 %all-to-all-start.3 = ((bf16[64,8,2048]{2,1,0:T(8,128)(2,1)}), bf16[64,8,2048]{2,1,0:T(8,128)(2,1)S(1)}, u32[]{:S(2)}, u32[]{:S(2)}) async-start(bf16[64,8,2048]{2,1,0:T(8,128)(2,1)} %bitcast.43), calls=%async_computation.3 | async-start | bytes 4194304 | tf_op jit(solution)/shard_map/all_to_all | solution.py:351
  183.1 1.3 copy-start.1
  184.4 33.8 %all-to-all-start.5 = ((bf16[64,8,2048]{2,1,0:T(8,128)(2,1)}), bf16[64,8,2048]{2,1,0:T(8,128)(2,1)}, u32[]{:S(2)}, u32[]{:S(2)}) async-start(bf16[64,8,2048]{2,1,0:T(8,128)(2,1)} %bitcast.42), calls=%async_computation.5 | async-start | bytes 4194304 | tf_op jit(solution)/shard_map/all_to_all | solution.py:351

commit v2 on v1

v2 whole, which is shorter than its diff:
```python
import functools
import math

import jax
import jax.numpy as jnp
import numpy as np
from jax import lax
from jax.experimental import pallas as pl
from jax.experimental.pallas import tpu as pltpu
from jax.sharding import Mesh
from jax.sharding import PartitionSpec as P


EPSILON = 1e-06
FLOOR_SCORE = -1e30
PARTS = 2
CHIP = ("req", "ylo")
BF16 = jnp.bfloat16
F32 = jnp.float32
NT = (((1,), (1,)), ((), ()))


def dot(a, b):
    return jnp.dot(a, b, preferred_element_type=F32)


def dot_nt(a, b):
    return lax.dot_general(a, b, NT, preferred_element_type=F32)


def iota(shape, axis):
    return lax.broadcasted_iota(jnp.int32, shape, axis)


def seg_starts(lengths_ref, pos):
    end_0 = lengths_ref[0, 0]
    end_1 = end_0 + lengths_ref[0, 1]
    return jnp.where(pos >= end_1, end_1, jnp.where(pos >= end_0, end_0, 0))


def spread_matrix(part_slots, experts):
    owner = iota((part_slots, experts), 0) // (part_slots // experts)
    return jnp.where(owner == iota((part_slots, experts), 1), 1.0, 0.0).astype(BF16)


def route_kernel(depth, ids_ref, place_ref):
    top, rows = ids_ref.shape
    parts, part_slots, _ = place_ref.shape
    experts = part_slots // depth
    e_iota = iota((experts, rows), 0)
    named = jnp.zeros((experts, rows), F32)
    for k in range(top):
        named = named + jnp.where(ids_ref[k : k + 1, :] == e_iota, 1.0, 0.0)
    before = jnp.where(iota((rows, rows), 0) < iota((rows, rows), 1), 1.0, 0.0).astype(BF16)
    rank = dot(named.astype(BF16), before)
    order = (named * (rank + 1.0)).astype(BF16)
    order_at = dot(spread_matrix(part_slots, experts), order)
    level = (iota((part_slots, rows), 0) % depth).astype(F32)
    for part in range(parts):
        put = order_at == level + (1.0 + part * depth)
        place_ref[part] = jnp.where(put, 1.0, 0.0).astype(BF16)


def gate_kernel(depth, part, ids_ref, gates_ref, place_ref, mix_ref):
    top, rows = ids_ref.shape
    part_slots = place_ref.shape[1]
    experts = part_slots // depth
    e_iota = iota((experts, rows), 0)
    gate = jnp.zeros((experts, rows), F32)
    for k in range(top):
        gate = gate + jnp.where(ids_ref[k : k + 1, :] == e_iota, gates_ref[k : k + 1, :], 0.0)
    gate_high = gate.astype(BF16)
    gate_low = (gate - gate_high.astype(F32)).astype(BF16)
    spread = spread_matrix(part_slots, experts)
    put = place_ref[part].astype(F32) > 0.5
    mix_ref[:rows] = jnp.where(put, dot(spread, gate_high), 0.0).T.astype(BF16)
    mix_ref[rows:] = jnp.where(put, dot(spread, gate_low), 0.0).T.astype(BF16)


def project_kernel(
    lengths_ref, sub_ref, tokens_ref, gain_ref, wq_ref, wl_ref, lgain_ref, wk_ref, inverse_ref,
    cache_ref, query_ref, normed, angle,
):
    rows = tokens_ref.shape[0]
    heads, nope, lat = wk_ref.shape
    rope = wl_ref.shape[0] - lat
    half = rope // 2

    @pl.when(pl.program_id(0) == 0)
    def _():
        x = tokens_ref[...].astype(F32)
        scale = lax.rsqrt(jnp.mean(x * x, axis=-1, keepdims=True) + EPSILON)
        normed[...] = (x * scale * gain_ref[...]).astype(BF16)
        pos = sub_ref[0] * rows + iota((half, rows), 1)
        offset = sub_ref[1] + pos - seg_starts(lengths_ref, pos)
        angles = offset.astype(F32) * inverse_ref[...]
        cos_part = jnp.cos(angles)
        sin_part = jnp.sin(angles)
        angle[...] = jnp.concatenate([cos_part, sin_part], axis=0).T
        latent = dot_nt(wl_ref[...], normed[...])
        low = latent[:lat]
        scale = lax.rsqrt(jnp.mean(low * low, axis=0, keepdims=True) + EPSILON)
        gain = jnp.broadcast_to(lgain_ref[...], (rows, lat)).T
        cache_ref[:lat] = (low * scale * gain).astype(BF16)
        first = latent[lat : lat + half]
        second = latent[lat + half :]
        cache_ref[lat : lat + half] = (first * cos_part - second * sin_part).astype(BF16)
        cache_ref[lat + half :] = (second * cos_part + first * sin_part).astype(BF16)

    queries = dot(normed[...], wq_ref[...]).astype(BF16)
    cos_part = angle[:, :half]
    sin_part = angle[:, half:]
    for h in range(heads):
        base = h * (nope + rope)
        at = pl.program_id(0) * heads + h
        query_ref[at, :, :lat] = dot(queries[:, base : base + nope], wk_ref[h]).astype(BF16)
        first = queries[:, base + nope : base + nope + half].astype(F32)
        second = queries[:, base + nope + half : base + nope + rope].astype(F32)
        query_ref[at, :, lat:] = jnp.concatenate(
            [first * cos_part - second * sin_part, second * cos_part + first * sin_part], axis=1
        ).astype(BF16)


def attend_kernel(
    score_scale, lengths_ref, sub_ref, query_ref, own_ref, back_1_ref, back_2_ref, back_3_ref,
    near_ref, far_ref, gain_ref, wv_hbm, wo_hbm, tokens_hbm, place_hbm,
    residual_ref, mid_ref, out_ref,
    keys, bias, query_buf, wv_ref, wo_ref, tokens_ref, place_ref, sems,
):
    copies = [
        pltpu.make_async_copy(src, dst, sems.at[i])
        for i, (src, dst) in enumerate((
            (query_ref, query_buf), (wv_hbm, wv_ref), (wo_hbm, wo_ref), (tokens_hbm, tokens_ref),
            (place_hbm.at[0], place_ref),
        ))
    ]
    for copy in copies:
        copy.start()
    rows = tokens_ref.shape[0]
    heads, lat, _ = wv_ref.shape
    width = query_ref.shape[2]
    near_tiles = near_ref.shape[0]
    tiles = near_tiles + far_ref.shape[0]
    suffix = (own_ref, back_1_ref, back_2_ref, back_3_ref)
    for i in range(near_tiles):
        keys[:, i * rows : (i + 1) * rows] = near_ref[i]
        keys[:, (near_tiles + i) * rows : (near_tiles + i + 1) * rows] = far_ref[i]
    pos = sub_ref[0] * rows + iota((rows, rows), 0)
    start = seg_starts(lengths_ref, pos)
    for d, ref in enumerate(suffix):
        keys[:, (tiles + d) * rows : (tiles + d + 1) * rows] = ref[...]
        key_pos = ((sub_ref[0] + len(suffix) - d) % len(suffix)) * rows + iota((rows, rows), 1)
        allowed = (key_pos >= start) & (key_pos <= pos)
        bias[:, d * rows : (d + 1) * rows] = jnp.where(allowed, 0.0, FLOOR_SCORE)
    cut = tiles * rows
    pair = 2
    mask = jnp.concatenate([bias[...]] * pair, axis=0)

    def score(i):
        query = query_buf[i * pair : (i + 1) * pair].reshape(pair * rows, width)
        return dot(query, keys[:, :cut]), dot(query, keys[:, cut:]) + mask

    def attend(early, late):
        row_top = jnp.maximum(
            jnp.max(early, axis=1, keepdims=True), jnp.max(late, axis=1, keepdims=True)
        )
        early = jnp.exp2((early - row_top) * score_scale)
        late = jnp.exp2((late - row_top) * score_scale)
        denominator = jnp.sum(early, axis=1, keepdims=True) + jnp.sum(late, axis=1, keepdims=True)
        weighted = dot_nt(early.astype(BF16), keys[:lat, :cut]) + dot_nt(
            late.astype(BF16), keys[:lat, cut:]
        )
        return (weighted / denominator).astype(BF16)

    latent_out = []
    copies[0].wait()
    current = score(0)
    for i in range(heads // pair):
        following = score(i + 1) if i + 1 < heads // pair else None
        latent_out.append(attend(*current))
        current = following
    copies[1].wait()
    head_out = jnp.concatenate(
        [
            dot(latent_out[h // pair][h % pair * rows : (h % pair + 1) * rows], wv_ref[h]).astype(BF16)
            for h in range(heads)
        ],
        axis=1,
    )
    copies[2].wait()
    copies[3].wait()
    x = tokens_ref[...].astype(F32) + dot(head_out, wo_ref[...])
    residual_ref[...] = x
    scale = lax.rsqrt(jnp.mean(x * x, axis=-1, keepdims=True) + EPSILON)
    mid = (x * scale * gain_ref[...]).astype(BF16)
    mid_ref[...] = mid
    copies[4].wait()
    out_ref[...] = dot(place_ref[...], mid).astype(BF16)


def place_kernel(place_ref, mid_ref, out_ref):
    out_ref[...] = dot(place_ref[...], mid_ref[...]).astype(BF16)


def expert_kernel(x_ref, g0, u0, d0, g1, u1, d1, out_ref, buf, activated, sems):
    copies = [
        pltpu.make_async_copy(src, buf.at[i], sems.at[i])
        for i, src in enumerate((g0, u0, g1, u1, d0, d1))
    ]
    for copy in copies:
        copy.start()
    step = 256
    blocks = x_ref.shape[0] // step
    for half in range(2):
        copies[2 * half].wait()
        copies[2 * half + 1].wait()

        @pl.loop(0, blocks)
        def _(i):
            at = pl.ds(pl.multiple_of(i * step, step), step)
            gate = dot_nt(x_ref[at], buf[2 * half])
            up = dot_nt(x_ref[at], buf[2 * half + 1])
            activated[half, at] = (gate / (1.0 + jnp.exp(-gate)) * up).astype(BF16)

    copies[4].wait()
    copies[5].wait()

    @pl.loop(0, blocks)
    def _(i):
        at = pl.ds(pl.multiple_of(i * step, step), step)
        total = dot(activated[0, at], buf[4])
        out_ref[at] = (total + dot(activated[1, at], buf[5])).astype(BF16)


def mix_kernel(base_ref, mix_ref, rows_ref, out_ref):
    rows = base_ref.shape[0]
    both = dot(mix_ref[...], rows_ref[...])
    out_ref[...] = (base_ref[...] + (both[:rows] + both[rows:])).astype(out_ref.dtype)


def cost(flops, moved):
    return pl.CostEstimate(flops=int(flops), bytes_accessed=int(moved), transcendentals=0)


SMEM = pl.BlockSpec(memory_space=pltpu.SMEM)
VMEM = pl.BlockSpec(memory_space=pltpu.VMEM)
HBM = pl.BlockSpec(memory_space=pltpu.HBM)


def near_core(x):
    return pltpu.with_memory_space_constraint(x, pltpu.VMEM)


def limit(mebibytes):
    return pltpu.CompilerParams(vmem_limit_bytes=mebibytes << 20)


def whole(array):
    return pl.BlockSpec(array.shape, lambda *_: (0,) * array.ndim)


def layer(
    tokens, attn_gain, w_query, w_latent, latent_gain, w_key_up, w_value_up, w_out, moe_gain,
    w_gate, w_up, w_down, expert_ids, gate_weights, lengths, slab_group, owners, prefix_pool,
):
    rows, model = tokens.shape
    head_count, nope, lat = w_key_up.shape
    width = w_latent.shape[1]
    rope = width - lat
    prefix_len = prefix_pool.shape[1]
    hidden = w_down.shape[1]
    top = expert_ids.shape[1]
    req_count = lax.axis_size("req")
    core_count = lax.axis_size("core")
    sub_count = lax.axis_size("ylo") * core_count
    chips = req_count * lax.axis_size("ylo")
    sub = lax.axis_index("ylo") * core_count + lax.axis_index("core")
    place_info = jnp.stack([sub, jnp.int32(prefix_len)]).astype(jnp.int32)

    quarter_len = prefix_len // sub_count
    quarter = lax.dynamic_slice(prefix_pool[0].T, (0, sub * quarter_len), (width, quarter_len))
    lanes = 128
    piece = width * quarter_len // lanes // req_count
    pieces = (
        quarter.reshape(width, quarter_len // lanes, lanes).transpose(1, 0, 2)
        .reshape(req_count, piece, lanes)
    )
    tag_rows = -piece % 8 or 8
    tag = jnp.broadcast_to(slab_group[0].astype(BF16), (req_count, tag_rows, lanes))
    spread = lax.all_to_all(
        jnp.concatenate([pieces, tag], axis=1), "req", split_axis=0, concat_axis=0, tiled=True
    )
    groups = spread[:, piece, 0].astype(jnp.int32)
    slots = jnp.sum(
        jnp.where(
            groups[:, None] == jnp.arange(owners.shape[0], dtype=jnp.int32)[None, :], owners[None, :], 0
        ),
        axis=1,
    )
    picked = jnp.take(spread, slots, axis=0, mode="clip")
    ylo_count = lax.axis_size("ylo")
    doubled = jnp.broadcast_to(picked[:, None], (req_count, ylo_count) + picked.shape[1:])
    near = lax.all_to_all(
        doubled.reshape((chips,) + picked.shape[1:]), CHIP, split_axis=0, concat_axis=0, tiled=True
    )
    near = near[:, :piece].reshape(req_count, ylo_count, piece, lanes).transpose(1, 0, 2, 3)
    near = near.reshape(ylo_count * quarter_len // lanes, width, lanes)
    swap = [(0, 1), (1, 0)]
    far = lax.ppermute(near, "core", swap)

    gate_t = w_gate[0].T
    up_t = w_up[0].T
    down = w_down[0]
    gate_far = lax.ppermute(gate_t, "core", swap)
    up_far = lax.ppermute(up_t, "core", swap)
    down_far = lax.ppermute(down, "core", swap)

    pair = 2
    steps = head_count // pair
    inverse = (10000.0 ** (-np.arange(rope // 2) / (rope // 2))).astype(np.float32)
    inverse = jnp.broadcast_to(jnp.asarray(inverse)[:, None], (rope // 2, rows))
    w_latent_t = w_latent.T
    gain_row = attn_gain[None, :]
    lgain_row = latent_gain[None, :]
    cache_t, query_full = pl.pallas_call(
        project_kernel,
        name="project",
        grid=(steps,),
        in_specs=[
            SMEM, SMEM, whole(tokens), whole(gain_row),
            pl.BlockSpec((model, pair * (nope + rope)), lambda i: (0, i)),
            whole(w_latent_t), whole(lgain_row),
            pl.BlockSpec((pair, nope, lat), lambda i: (i, 0, 0)),
            whole(inverse),
        ],
        out_specs=[VMEM, VMEM],
        out_shape=[
            pltpu.HBM((width, rows), BF16),
            pltpu.HBM((head_count, rows, width), BF16),
        ],
        scratch_shapes=[pltpu.VMEM((rows, model), BF16), pltpu.VMEM((rows, rope), F32)],
        cost_estimate=cost(2 * rows * model * (w_query.shape[1] + width), 14e6),
    )(lengths, place_info, tokens, gain_row, w_query, w_latent_t, lgain_row, w_key_up, inverse)

    back = [
        lax.ppermute(cache_t, ("ylo", "core"), [(k, (k + d) % sub_count) for k in range(sub_count)])
        for d in range(1, sub_count)
    ]

    slot_count = 4 * rows * top // 3
    part_slots = slot_count // PARTS
    depth = part_slots // chips
    ids_t = expert_ids.T
    gates_t = gate_weights.T
    placing = pl.pallas_call(
        functools.partial(route_kernel, depth),
        name="route",
        in_specs=[whole(ids_t)],
        out_specs=VMEM,
        out_shape=pltpu.HBM((PARTS, part_slots, rows), BF16),
        cost_estimate=cost(1e9, 2e6),
    )(ids_t)
    mixing = []
    for part in range(PARTS):
        mixing.append(pl.pallas_call(
            functools.partial(gate_kernel, depth, part),
            name="gates",
            in_specs=[whole(ids_t), whole(gates_t), VMEM],
            out_specs=VMEM,
            out_shape=pltpu.HBM((2 * rows, part_slots), BF16),
            cost_estimate=cost(1e9, 2e6),
        )(ids_t, gates_t, placing))

    moe_row = moe_gain[None, :]
    residual, mid, first_out = pl.pallas_call(
        functools.partial(attend_kernel, (nope + rope) ** (-0.5) * math.log2(math.e)),
        name="attend",
        in_specs=[SMEM, SMEM, HBM] + [VMEM] * 7 + [HBM] * 4,
        out_specs=[VMEM, VMEM, VMEM],
        out_shape=[
            pltpu.HBM((rows, model), F32),
            pltpu.HBM((rows, model), BF16),
            pltpu.HBM((part_slots, model), BF16),
        ],
        scratch_shapes=[
            pltpu.VMEM((width, prefix_len + rows * sub_count), BF16),
            pltpu.VMEM((rows, rows * sub_count), F32),
            pltpu.VMEM(query_full.shape, BF16),
            pltpu.VMEM(w_value_up.shape, BF16),
            pltpu.VMEM(w_out.shape, BF16),
            pltpu.VMEM(tokens.shape, BF16),
            pltpu.VMEM((part_slots, rows), BF16),
            pltpu.SemaphoreType.DMA((5,)),
        ],
        compiler_params=limit(54),
        cost_estimate=cost(5e9, 6e6),
    )(
        lengths, place_info, query_full, cache_t, *map(near_core, (*back, near, far)),
        moe_row, w_value_up, w_out, tokens, placing,
    )

    def exchange(x):
        x = x.reshape(chips, depth, model)
        x = lax.all_to_all(x, CHIP, split_axis=0, concat_axis=0, tiled=True)
        return x.reshape(part_slots, model)

    def place(part):
        return pl.pallas_call(
            place_kernel,
            name="place",
            grid=(2,),
            in_specs=[
                pl.BlockSpec((None, part_slots // 2, rows), lambda i: (part, i, 0)), VMEM,
            ],
            out_specs=pl.BlockSpec((part_slots // 2, model), lambda i: (i, 0)),
            out_shape=pltpu.HBM((part_slots, model), BF16),
            cost_estimate=cost(2 * part_slots * rows * model, 3e6),
        )(placing, mid)

    def experts(x):
        return pl.pallas_call(
            expert_kernel,
            name="experts",
            in_specs=[VMEM] + [HBM] * 6,
            out_specs=pl.BlockSpec((part_slots, model), lambda: (0, 0)),
            out_shape=pltpu.HBM((part_slots, model), BF16),
            scratch_shapes=[
                pltpu.VMEM((6, hidden, model), BF16), pltpu.VMEM((2, part_slots, hidden), BF16),
                pltpu.SemaphoreType.DMA((6,)),
            ],
            compiler_params=limit(54),
            cost_estimate=cost(12 * part_slots * model * hidden, 21e6),
        )(near_core(x), gate_t, up_t, down, gate_far, up_far, down_far)

    def mix(base, part, x, last):
        shape = (rows, model)
        return pl.pallas_call(
            mix_kernel,
            name="mix",
            in_specs=[VMEM] * 3,
            out_specs=VMEM,
            out_shape=pltpu.HBM(shape, BF16 if last else F32),
            compiler_params=limit(54),
            cost_estimate=cost(4 * part_slots * rows * model, 3e6),
        )(base, mixing[part], near_core(x))

    outbound = [first_out] + [place(part) for part in range(1, PARTS)]
    arrived = [exchange(x) for x in outbound]
    returned = [exchange(experts(x)) for x in arrived]
    total = residual
    for part in range(PARTS):
        total = mix(total, part, returned[part], part == PARTS - 1)
    return (total, cache_t.T)


def solution(mesh):
    split = Mesh(mesh.devices.reshape(mesh.devices.shape[0], -1, 2), ("req", "ylo", "core"))
    every = ("req", "ylo", "core")
    in_specs = (
        P(every, None), P(), P(), P(), P(), P(), P(), P(), P(),
        P(every, None, None), P(every, None, None), P(every, None, None),
        P(every, None), P(every, None), P("req", None), P("req"), P(), P("req", None, None),
    )
    out_specs = (P(every, None), P(every, None))
    return jax.shard_map(layer, mesh=split, in_specs=in_specs, out_specs=out_specs, check_vma=False)
```

time: 223 us -> 216 us (0.969)
  Pallas kernels: 70.7 us -> 65.4 us
  local copies, waits for them, and re-layouts: 7.09 us -> 3.53 us
    pallas_call x7 -> x9, Pallas kernels: 67.8 us -> 62.5 us  [the longest x2 31.6 us: experts(): pl.pallas_call(expert_kernel, name='experts', in_specs=[VMEM] + [HBM] * 6...]
    unnamed x21 -> x7, local copies, waits for them, and re-layouts: 4.95 us -> 1.39 us
where the time goes in v2:
time: 216 us; the launch traced here: 215 us
  waiting for transfers between devices  75.3 us (35%)
  Pallas kernels  65.4 us (30%)
  blocking collectives  39 us (18%)
  starting transfers between devices  29.1 us (13%)
  local copies, waits for them, and re-layouts  3.53 us (2%)
    all_to_all x4, waiting for transfers between devices, exchange(): x = lax.all_to_all(x, CHIP, split_axis=0, concat_axis=0, tiled=True)  71.3 us
    pallas_call x2, Pallas kernels, experts(): pl.pallas_call(expert_kernel, name='experts', in_specs=[VMEM] + [HBM] * 6...  31.6 us
    all_to_all x4, starting transfers between devices, exchange(): x = lax.all_to_all(x, CHIP, split_axis=0, concat_axis=0, tiled=True)  25.2 us
    all_to_all x1, blocking collectives, layer(): lax.all_to_all(jnp.concatenate([pieces, tag], axis=1), 'req', split_axis=...  21.9 us
    all_to_all x1, blocking collectives, layer(): lax.all_to_all(doubled.reshape((chips,) + picked.shape[1:]), CHIP, split_...  17.1 us
    pallas_call x1, Pallas kernels, layer(): pl.pallas_call(functools.partial(attend_kernel, (nope + rope) ** (-0.5) *...  10.2 us
    pallas_call x1, Pallas kernels, layer(): pl.pallas_call(project_kernel, name='project', grid=(steps,), in_specs=[S...  8.41 us
    pallas_call x2, Pallas kernels, mix(): pl.pallas_call(mix_kernel, name='mix', in_specs=[VMEM] * 3, out_specs=VME...  6.47 us
  transfers between devices with their start and end apart: 11, of which 7 were waited for; matrix products, arithmetic and copies ran while one was open for 1% of the time, Pallas kernels for 24%

profile of v2, /device:TPU:0, one launch (start us, length us, event | category | flops | bytes accessed | tf_op | source)
XLA Modules:
  0.0 215.2 jit_solution(12940800326808820950)
XLA Ops:
  0.7 1.2 copy-done
  2.8 21.9 %all_to_all.30 = bf16[32,40,128]{2,1,0:T(8,128)(2,1)S(1)} all-to-all(bf16[32,40,128]{2,1,0:T(8,128)(2,1)S(1)} %concatenate.3), channel_id=1, replica_groups=mesh['req'=32,'ylo'=2,'core'=2] {'req'}, dimensions={0} | all-to-all | bytes 655360 | tf_op jit(solution)/shard_map/all_to_all | solution.py:290
  26.2 17.1 %all_to_all.31 = bf16[64,40,128]{2,1,0:T(8,128)(2,1)S(1)} all-to-all(bf16[64,40,128]{2,1,0:T(8,128)(2,1)S(1)} %bitcast.37), channel_id=1, replica_groups=mesh['req'=32,'ylo'=2,'core'=2] {'req','ylo'}, dimensions={0} | all-to-all | bytes 1310720 | tf_op jit(solution)/shard_map/all_to_all | solution.py:303
  45.3 8.4 %project.1 = (bf16[576,128]{1,0:T(8,128)(2,1)}, bf16[8,128,576]{2,1,0:T(8,128)(2,1)}) custom-call(s32[1,3]{1,0:T(1,128)} %lengths_ref.3, s32[2]{0:T(128)} %pad_add_fusion.sub_ref, bf16[128,2048]{1,0:T(8,128)(2,1)} %tokens_hbm.1, f32[1,2048]{1,0:T(1,128)} %bitcast.45, bf16[2048,1536]{1,0:T(8,128)(2,1)} %wq_ref.1, bf16[576,2048]{1,0:T(8,128)(2,1)} %bitcast.39, ...), custom_call_target="tpu_custom_call" | custom-call | flops 1107296256 | bytes 14000000 | tf_op jit(solution)/shard_map/project/pallas_call | solution.py:325
  55.9 1.7 route.1.place_hbm.place_ref
  57.6 1.4 collective-permute-done.back_1_ref
  59.0 2.2 %collective-permute-done.1.back_2_ref = bf16[576,128]{1,0:T(8,128)(2,1)S(1)} collective-permute-done((bf16[576,128]{1,0:T(8,128)(2,1)}, bf16[576,128]{1,0:T(8,128)(2,1)S(1)}, u32[]{:S(2)}, u32[]{:S(2)}) %collective-permute-start.1) | collective-permute-done | bytes 147488 | tf_op jit(solution)/shard_map/ppermute | solution.py:346
  61.6 10.2 %attend.1 = (f32[128,2048]{1,0:T(8,128)}, bf16[128,2048]{1,0:T(8,128)(2,1)}, bf16[512,2048]{1,0:T(8,128)(2,1)}) custom-call(s32[1,3]{1,0:T(1,128)} %lengths_ref.3, s32[2]{0:T(128)} %pad_add_fusion.sub_ref, bf16[8,128,576]{2,1,0:T(8,128)(2,1)} %get-tuple-element.7.query_ref, bf16[576,128]{1,0:T(8,128)(2,1)} %get-tuple-element.8.own_ref, ...), custom_call_target="tpu_custom_call" | custom-call | flops 5000000000 | bytes 6000000 | tf_op jit(solution)/shard_map/attend/pallas_call | solution.py:375
  71.8 5.9 %all-to-all-start.2 = ((bf16[64,8,2048]{2,1,0:T(8,128)(2,1)}), bf16[64,8,2048]{2,1,0:T(8,128)(2,1)S(1)}, u32[]{:S(2)}, u32[]{:S(2)}) async-start(bf16[64,8,2048]{2,1,0:T(8,128)(2,1)} %bitcast.41), calls=%async_computation.2 | async-start | bytes 4194304 | tf_op jit(solution)/shard_map/all_to_all | solution.py:404
  77.7 1.2 collective-permute-start.4
  79.4 2.9 %place.1 = bf16[512,2048]{1,0:T(8,128)(2,1)} custom-call(bf16[2,512,128]{2,1,0:T(8,128)(2,1)} %route.1.place_hbm.place_ref, bf16[128,2048]{1,0:T(8,128)(2,1)} %get-tuple-element.11.mid_ref), custom_call_target="tpu_custom_call" | custom-call | flops 268435456 | bytes 3000000 | tf_op jit(solution)/shard_map/place/pallas_call | solution.py:408
  82.3 26.2 %all-to-all-done.2 = bf16[64,8,2048]{2,1,0:T(8,128)(2,1)S(1)} async-done(((bf16[64,8,2048]{2,1,0:T(8,128)(2,1)}), bf16[64,8,2048]{2,1,0:T(8,128)(2,1)S(1)}, u32[]{:S(2)}, u32[]{:S(2)}) %all-to-all-start.2) | async-done | bytes 2097184 | tf_op jit(solution)/shard_map/all_to_all | solution.py:404
  108.5 6.4 %all-to-all-start.4 = ((bf16[64,8,2048]{2,1,0:T(8,128)(2,1)}), bf16[64,8,2048]{2,1,0:T(8,128)(2,1)}, u32[]{:S(2)}, u32[]{:S(2)}) async-start(bf16[64,8,2048]{2,1,0:T(8,128)(2,1)} %bitcast.36), calls=%async_computation.4 | async-start | bytes 4194304 | tf_op jit(solution)/shard_map/all_to_all | solution.py:404
  114.9 15.0 %experts.2 = bf16[512,2048]{1,0:T(8,128)(2,1)} custom-call(bf16[512,2048]{1,0:T(8,128)(2,1)S(1)} %bitcast.35, bf16[704,2048]{1,0:T(8,128)(2,1)} %bitcast.48, bf16[704,2048]{1,0:T(8,128)(2,1)} %bitcast.51, bf16[704,2048]{1,0:T(8,128)(2,1)} %bitcast.54, bf16[704,2048]{1,0:T(8,128)(2,1)} %collective-permute-done.4.g1, ...), custom_call_target="tpu_custom_call" | custom-call | flops 8858370048 | bytes 21000000 | tf_op jit(solution)/shard_map/experts/pallas_call | solution.py:421
  129.9 13.8 %all-to-all-done.4 = bf16[64,8,2048]{2,1,0:T(8,128)(2,1)} async-done(((bf16[64,8,2048]{2,1,0:T(8,128)(2,1)}), bf16[64,8,2048]{2,1,0:T(8,128)(2,1)}, u32[]{:S(2)}, u32[]{:S(2)}) %all-to-all-start.4) | async-done | bytes 2097184 | tf_op jit(solution)/shard_map/all_to_all | solution.py:404
  143.7 6.2 %all-to-all-start.3 = ((bf16[64,8,2048]{2,1,0:T(8,128)(2,1)}), bf16[64,8,2048]{2,1,0:T(8,128)(2,1)S(1)}, u32[]{:S(2)}, u32[]{:S(2)}) async-start(bf16[64,8,2048]{2,1,0:T(8,128)(2,1)} %bitcast.43), calls=%async_computation.3 | async-start | bytes 4194304 | tf_op jit(solution)/shard_map/all_to_all | solution.py:404
  149.8 16.6 %experts.3 = bf16[512,2048]{1,0:T(8,128)(2,1)} custom-call(bf16[512,2048]{1,0:T(8,128)(2,1)} %bitcast.26.x_ref, bf16[704,2048]{1,0:T(8,128)(2,1)} %bitcast.49, bf16[704,2048]{1,0:T(8,128)(2,1)} %bitcast.52, bf16[704,2048]{1,0:T(8,128)(2,1)} %bitcast.55, bf16[704,2048]{1,0:T(8,128)(2,1)} %collective-permute-done.4.g1, ...), custom_call_target="tpu_custom_call" | custom-call | flops 8858370048 | bytes 21000000 | tf_op jit(solution)/shard_map/experts/pallas_call | solution.py:421
  166.5 11.4 %all-to-all-done.3 = bf16[64,8,2048]{2,1,0:T(8,128)(2,1)S(1)} async-done(((bf16[64,8,2048]{2,1,0:T(8,128)(2,1)}), bf16[64,8,2048]{2,1,0:T(8,128)(2,1)S(1)}, u32[]{:S(2)}, u32[]{:S(2)}) %all-to-all-start.3) | async-done | bytes 2097184 | tf_op jit(solution)/shard_map/all_to_all | solution.py:404
  177.9 6.8 %all-to-all-start.5 = ((bf16[64,8,2048]{2,1,0:T(8,128)(2,1)}), bf16[64,8,2048]{2,1,0:T(8,128)(2,1)}, u32[]{:S(2)}, u32[]{:S(2)}) async-start(bf16[64,8,2048]{2,1,0:T(8,128)(2,1)} %bitcast.42), calls=%async_computation.5 | async-start | bytes 4194304 | tf_op jit(solution)/shard_map/all_to_all | solution.py:404
  184.6 2.0 gates.2.mix_ref
  186.7 2.0 gates.3.mix_ref
  188.7 3.0 %mix.2.base_ref = f32[128,2048]{1,0:T(8,128)} custom-call(f32[128,2048]{1,0:T(8,128)} %get-tuple-element.9.base_ref, bf16[256,512]{1,0:T(8,128)(2,1)} %gates.2.mix_ref, bf16[512,2048]{1,0:T(8,128)(2,1)S(1)} %bitcast.34), custom_call_target="tpu_custom_call" | custom-call | flops 536870912 | bytes 3000000 | tf_op jit(solution)/shard_map/mix/pallas_call | solution.py:437
  191.7 20.0 %all-to-all-done.5 = bf16[64,8,2048]{2,1,0:T(8,128)(2,1)} async-done(((bf16[64,8,2048]{2,1,0:T(8,128)(2,1)}), bf16[64,8,2048]{2,1,0:T(8,128)(2,1)}, u32[]{:S(2)}, u32[]{:S(2)}) %all-to-all-start.5) | async-done | bytes 2097184 | tf_op jit(solution)/shard_map/all_to_all | solution.py:404
  211.6 3.5 %mix.3 = bf16[128,2048]{1,0:T(8,128)(2,1)} custom-call(f32[128,2048]{1,0:T(8,128)} %mix.2.base_ref, bf16[256,512]{1,0:T(8,128)(2,1)} %gates.3.mix_ref, bf16[512,2048]{1,0:T(8,128)(2,1)} %bitcast.28.rows_ref), custom_call_target="tpu_custom_call" | custom-call | flops 536870912 | bytes 3000000 | tf_op jit(solution)/shard_map/mix/pallas_call | solution.py:437
  (31 shorter events, 6.7 us)
Async XLA Ops:
  0.6 1.3 copy-start
  0.6 24.7 %copy-start.2 = (s32[4]{0:T(128)S(1)}, s32[4]{0:T(128)}, u32[]{:S(2)}) copy-start(s32[4]{0:T(128)} %param.35) | copy-start | bytes 52
  43.3 1.3 copy-start.1
  44.0 17.6 %collective-permute-start.3 = (bf16[4,576,128]{2,1,0:T(8,128)(2,1)S(1)}, bf16[4,576,128]{2,1,0:T(8,128)(2,1)S(1)}, u32[]{:S(2)}, u32[]{:S(2)}) collective-permute-start(bf16[4,576,128]{2,1,0:T(8,128)(2,1)S(1)} %reshape.62.near_ref), channel_id=1, source_target_pairs={{0,1},{1,0},{2,3},{3,2},{4,5},{5,4},{6,7},{7,6},{8,9},{9,8},{10,11... | collective-permute-start | bytes 1769480 | tf_op jit(solution)/shard_map/ppermute | solution.py:309
  53.7 5.3 %collective-permute-start = (bf16[576,128]{1,0:T(8,128)(2,1)}, bf16[576,128]{1,0:T(8,128)(2,1)S(1)}, u32[]{:S(2)}, u32[]{:S(2)}) collective-permute-start(bf16[576,128]{1,0:T(8,128)(2,1)} %get-tuple-element.8.own_ref), channel_id=1, source_target_pairs={{0,1},{1,2},{2,3},{3,0},{4,5},{5,6},{6,7},{7,4},{8,9},{9,10},{10,1... | collective-permute-start | bytes 442376 | tf_op jit(solution)/shard_map/ppermute | solution.py:346
  54.2 6.9 %collective-permute-start.1 = (bf16[576,128]{1,0:T(8,128)(2,1)}, bf16[576,128]{1,0:T(8,128)(2,1)S(1)}, u32[]{:S(2)}, u32[]{:S(2)}) collective-permute-start(bf16[576,128]{1,0:T(8,128)(2,1)} %get-tuple-element.8.own_ref), channel_id=1, source_target_pairs={{0,2},{1,3},{2,0},{3,1},{4,6},{5,7},{6,4},{7,5},{8,10},{9,11},{10,... | collective-permute-start | bytes 442376 | tf_op jit(solution)/shard_map/ppermute | solution.py:346
  54.9 6.6 %collective-permute-start.2 = (bf16[576,128]{1,0:T(8,128)(2,1)}, bf16[576,128]{1,0:T(8,128)(2,1)S(1)}, u32[]{:S(2)}, u32[]{:S(2)}) collective-permute-start(bf16[576,128]{1,0:T(8,128)(2,1)} %get-tuple-element.8.own_ref), channel_id=1, source_target_pairs={{0,3},{1,0},{2,1},{3,2},{4,7},{5,4},{6,5},{7,6},{8,11},{9,8},{10,9... | collective-permute-start | bytes 442376 | tf_op jit(solution)/shard_map/ppermute | solution.py:346
  71.8 36.7 %all-to-all-start.2 = ((bf16[64,8,2048]{2,1,0:T(8,128)(2,1)}), bf16[64,8,2048]{2,1,0:T(8,128)(2,1)S(1)}, u32[]{:S(2)}, u32[]{:S(2)}) async-start(bf16[64,8,2048]{2,1,0:T(8,128)(2,1)} %bitcast.41), calls=%async_computation.2 | async-start | bytes 4194304 | tf_op jit(solution)/shard_map/all_to_all | solution.py:404
  77.7 37.2 %collective-permute-start.4 = (bf16[704,2048]{1,0:T(8,128)(2,1)}, bf16[704,2048]{1,0:T(8,128)(2,1)}, u32[]{:S(2)}, u32[]{:S(2)}) collective-permute-start(bf16[704,2048]{1,0:T(8,128)(2,1)} %bitcast.47), channel_id=1, source_target_pairs={{0,1},{1,0},{2,3},{3,2},{4,5},{5,4},{6,7},{7,6},{8,9},{9,8},{10,11... | collective-permute-start | bytes 8650760 | tf_op jit(solution)/shard_map/ppermute | solution.py:314
  78.9 36.0 %collective-permute-start.5 = (bf16[704,2048]{1,0:T(8,128)(2,1)}, bf16[704,2048]{1,0:T(8,128)(2,1)}, u32[]{:S(2)}, u32[]{:S(2)}) collective-permute-start(bf16[704,2048]{1,0:T(8,128)(2,1)} %bitcast.50), channel_id=1, source_target_pairs={{0,1},{1,0},{2,3},{3,2},{4,5},{5,4},{6,7},{7,6},{8,9},{9,8},{10,11... | collective-permute-start | bytes 8650760 | tf_op jit(solution)/shard_map/ppermute | solution.py:315
  79.0 35.9 %collective-permute-start.6 = (bf16[704,2048]{1,0:T(8,128)(2,1)}, bf16[704,2048]{1,0:T(8,128)(2,1)}, u32[]{:S(2)}, u32[]{:S(2)}) collective-permute-start(bf16[704,2048]{1,0:T(8,128)(2,1)} %bitcast.53), channel_id=1, source_target_pairs={{0,1},{1,0},{2,3},{3,2},{4,5},{5,4},{6,7},{7,6},{8,9},{9,8},{10,11... | collective-permute-start | bytes 8650760 | tf_op jit(solution)/shard_map/ppermute | solution.py:316
  108.5 35.2 %all-to-all-start.4 = ((bf16[64,8,2048]{2,1,0:T(8,128)(2,1)}), bf16[64,8,2048]{2,1,0:T(8,128)(2,1)}, u32[]{:S(2)}, u32[]{:S(2)}) async-start(bf16[64,8,2048]{2,1,0:T(8,128)(2,1)} %bitcast.36), calls=%async_computation.4 | async-start | bytes 4194304 | tf_op jit(solution)/shard_map/all_to_all | solution.py:404
  143.7 34.2 %all-to-all-start.3 = ((bf16[64,8,2048]{2,1,0:T(8,128)(2,1)}), bf16[64,8,2048]{2,1,0:T(8,128)(2,1)S(1)}, u32[]{:S(2)}, u32[]{:S(2)}) async-start(bf16[64,8,2048]{2,1,0:T(8,128)(2,1)} %bitcast.43), calls=%async_computation.3 | async-start | bytes 4194304 | tf_op jit(solution)/shard_map/all_to_all | solution.py:404
  177.9 33.8 %all-to-all-start.5 = ((bf16[64,8,2048]{2,1,0:T(8,128)(2,1)}), bf16[64,8,2048]{2,1,0:T(8,128)(2,1)}, u32[]{:S(2)}, u32[]{:S(2)}) async-start(bf16[64,8,2048]{2,1,0:T(8,128)(2,1)} %bitcast.42), calls=%async_computation.5 | async-start | bytes 4194304 | tf_op jit(solution)/shard_map/all_to_all | solution.py:404

commit v3 on v2

--- a/solution.py
+++ b/solution.py
@@ -77,46 +77,47 @@
     mix_ref[rows:] = jnp.where(put, dot(spread, gate_low), 0.0).T.astype(BF16)
 
 
-def project_kernel(
-    lengths_ref, sub_ref, tokens_ref, gain_ref, wq_ref, wl_ref, lgain_ref, wk_ref, inverse_ref,
-    cache_ref, query_ref, normed, angle,
+def cache_kernel(
+    lengths_ref, sub_ref, tokens_ref, gain_ref, wl_ref, lgain_ref, inverse_ref,
+    cache_ref, normed_ref, angle_ref,
 ):
     rows = tokens_ref.shape[0]
+    lat = lgain_ref.shape[1]
+    half = (wl_ref.shape[0] - lat) // 2
+    x = tokens_ref[...].astype(F32)
+    scale = lax.rsqrt(jnp.mean(x * x, axis=-1, keepdims=True) + EPSILON)
+    normed = (x * scale * gain_ref[...]).astype(BF16)
+    normed_ref[...] = normed
+    pos = sub_ref[0] * rows + iota((half, rows), 1)
+    offset = sub_ref[1] + pos - seg_starts(lengths_ref, pos)
+    angles = offset.astype(F32) * inverse_ref[...]
+    cos_part = jnp.cos(angles)
+    sin_part = jnp.sin(angles)
+    angle_ref[...] = jnp.concatenate([cos_part, sin_part], axis=0).T
+    latent = dot_nt(wl_ref[...], normed)
+    low = latent[:lat]
+    scale = lax.rsqrt(jnp.mean(low * low, axis=0, keepdims=True) + EPSILON)
+    gain = jnp.broadcast_to(lgain_ref[...], (rows, lat)).T
+    cache_ref[:lat] = (low * scale * gain).astype(BF16)
+    first = latent[lat : lat + half]
+    second = latent[lat + half :]
+    cache_ref[lat : lat + half] = (first * cos_part - second * sin_part).astype(BF16)
+    cache_ref[lat + half :] = (second * cos_part + first * sin_part).astype(BF16)
+
+
+def query_kernel(normed_ref, angle_ref, wq_ref, wk_ref, query_ref):
     heads, nope, lat = wk_ref.shape
-    rope = wl_ref.shape[0] - lat
+    rope = angle_ref.shape[1]
     half = rope // 2
-
-    @pl.when(pl.program_id(0) == 0)
-    def _():
-        x = tokens_ref[...].astype(F32)
-        scale = lax.rsqrt(jnp.mean(x * x, axis=-1, keepdims=True) + EPSILON)
-        normed[...] = (x * scale * gain_ref[...]).astype(BF16)
-        pos = sub_ref[0] * rows + iota((half, rows), 1)
-        offset = sub_ref[1] + pos - seg_starts(lengths_ref, pos)
-        angles = offset.astype(F32) * inverse_ref[...]
-        cos_part = jnp.cos(angles)
-        sin_part = jnp.sin(angles)
-        angle[...] = jnp.concatenate([cos_part, sin_part], axis=0).T
-        latent = dot_nt(wl_ref[...], normed[...])
-        low = latent[:lat]
-        scale = lax.rsqrt(jnp.mean(low * low, axis=0, keepdims=True) + EPSILON)
-        gain = jnp.broadcast_to(lgain_ref[...], (rows, lat)).T
-        cache_ref[:lat] = (low * scale * gain).astype(BF16)
-        first = latent[lat : lat + half]
-        second = latent[lat + half :]
-        cache_ref[lat : lat + half] = (first * cos_part - second * sin_part).astype(BF16)
-        cache_ref[lat + half :] = (second * cos_part + first * sin_part).astype(BF16)
-
-    queries = dot(normed[...], wq_ref[...]).astype(BF16)
-    cos_part = angle[:, :half]
-    sin_part = angle[:, half:]
+    queries = dot(normed_ref[...], wq_ref[...]).astype(BF16)
+    cos_part = angle_ref[:, :half]
+    sin_part = angle_ref[:, half:]
     for h in range(heads):
         base = h * (nope + rope)
-        at = pl.program_id(0) * heads + h
-        query_ref[at, :, :lat] = dot(queries[:, base : base + nope], wk_ref[h]).astype(BF16)
+        query_ref[h, :, :lat] = dot(queries[:, base : base + nope], wk_ref[h]).astype(BF16)
         first = queries[:, base + nope : base + nope + half].astype(F32)
         second = queries[:, base + nope + half : base + nope + rope].astype(F32)
-        query_ref[at, :, lat:] = jnp.concatenate(
+        query_ref[h, :, lat:] = jnp.concatenate(
             [first * cos_part - second * sin_part, second * cos_part + first * sin_part], axis=1
         ).astype(BF16)
 
@@ -234,7 +235,9 @@
 
 def mix_kernel(base_ref, mix_ref, rows_ref, out_ref):
     rows = base_ref.shape[0]
-    both = dot(mix_ref[...], rows_ref[...])
+    width = base_ref.shape[1]
+    columns = pl.ds(pl.multiple_of(pl.program_id(0) * width, width), width)
+    both = dot(mix_ref[...], rows_ref[:, columns])
     out_ref[...] = (base_ref[...] + (both[:rows] + both[rows:])).astype(out_ref.dtype)
 
 
@@ -322,25 +325,31 @@
     w_latent_t = w_latent.T
     gain_row = attn_gain[None, :]
     lgain_row = latent_gain[None, :]
-    cache_t, query_full = pl.pallas_call(
-        project_kernel,
-        name="project",
+    cache_t, normed, angle = pl.pallas_call(
+        cache_kernel,
+        name="cache",
+        in_specs=[SMEM, SMEM] + [VMEM] * 5,
+        out_specs=[VMEM, VMEM, VMEM],
+        out_shape=[
+            pltpu.HBM((width, rows), BF16),
+            pltpu.HBM((rows, model), BF16),
+            pltpu.HBM((rows, rope), F32),
+        ],
+        cost_estimate=cost(2 * rows * model * width, 4e6),
+    )(lengths, place_info, tokens, gain_row, w_latent_t, lgain_row, inverse)
+    query_full = pl.pallas_call(
+        query_kernel,
+        name="query",
         grid=(steps,),
         in_specs=[
-            SMEM, SMEM, whole(tokens), whole(gain_row),
+            whole(normed), whole(angle),
             pl.BlockSpec((model, pair * (nope + rope)), lambda i: (0, i)),
-            whole(w_latent_t), whole(lgain_row),
             pl.BlockSpec((pair, nope, lat), lambda i: (i, 0, 0)),
-            whole(inverse),
         ],
-        out_specs=[VMEM, VMEM],
-        out_shape=[
-            pltpu.HBM((width, rows), BF16),
-            pltpu.HBM((head_count, rows, width), BF16),
-        ],
-        scratch_shapes=[pltpu.VMEM((rows, model), BF16), pltpu.VMEM((rows, rope), F32)],
-        cost_estimate=cost(2 * rows * model * (w_query.shape[1] + width), 14e6),
-    )(lengths, place_info, tokens, gain_row, w_query, w_latent_t, lgain_row, w_key_up, inverse)
+        out_specs=pl.BlockSpec((pair, rows, width), lambda i: (i, 0, 0)),
+        out_shape=pltpu.HBM((head_count, rows, width), BF16),
+        cost_estimate=cost(2 * rows * model * w_query.shape[1], 9e6),
+    )(normed, angle, w_query, w_key_up)
 
     back = [
         lax.ppermute(cache_t, ("ylo", "core"), [(k, (k + d) % sub_count) for k in range(sub_count)])
@@ -432,13 +441,16 @@
             cost_estimate=cost(12 * part_slots * model * hidden, 21e6),
         )(near_core(x), gate_t, up_t, down, gate_far, up_far, down_far)
 
+    blocks = 4
+
     def mix(base, part, x, last):
         shape = (rows, model)
         return pl.pallas_call(
             mix_kernel,
             name="mix",
-            in_specs=[VMEM] * 3,
-            out_specs=VMEM,
+            grid=(blocks,),
+            in_specs=[pl.BlockSpec((rows, model // blocks), lambda i: (0, i)), VMEM, VMEM],
+            out_specs=pl.BlockSpec((rows, model // blocks), lambda i: (0, i)),
             out_shape=pltpu.HBM(shape, BF16 if last else F32),
             compiler_params=limit(54),
             cost_estimate=cost(4 * part_slots * rows * model, 3e6),

time: 216 us -> 211 us (0.977)
  waiting for transfers between devices: 75.3 us -> 67.6 us
  Pallas kernels: 65.4 us -> 69.1 us
    ppermute x3, waiting for transfers between devices: 3.95 us -> 0.01 us  [layer(): lax.ppermute(cache_t, ('ylo', 'core'), [(k, (k + d) % sub_count) for k in...]
    pallas_call x3 -> x4, Pallas kernels: 14.9 us -> 18.6 us  [the longest x2 8.72 us: mix(): pl.pallas_call(mix_kernel, name='mix', grid=(blocks,), in_specs=[pl.Block...]
    all_to_all x4, waiting for transfers between devices: 71.3 us -> 67.6 us  [exchange(): x = lax.all_to_all(x, CHIP, split_axis=0, concat_axis=0, tiled=True)]
  transfers between devices with their start and end apart: 11 -> 11, of which waited for: 7 -> 4; matrix products, arithmetic and copies ran while one was open for 1% -> 1% of each run, Pallas kernels for 24% -> 26%
where the time goes in v3:
time: 211 us; the launch traced here: 210 us
  Pallas kernels  69.1 us (33%)
  waiting for transfers between devices  67.6 us (32%)
  blocking collectives  39 us (18%)
  starting transfers between devices  28.3 us (13%)
  local copies, waits for them, and re-layouts  3.52 us (2%)
    all_to_all x4, waiting for transfers between devices, exchange(): x = lax.all_to_all(x, CHIP, split_axis=0, concat_axis=0, tiled=True)  67.6 us
    pallas_call x2, Pallas kernels, experts(): pl.pallas_call(expert_kernel, name='experts', in_specs=[VMEM] + [HBM] * 6...  31.5 us
    all_to_all x4, starting transfers between devices, exchange(): x = lax.all_to_all(x, CHIP, split_axis=0, concat_axis=0, tiled=True)  25.4 us
    all_to_all x1, blocking collectives, layer(): lax.all_to_all(jnp.concatenate([pieces, tag], axis=1), 'req', split_axis=...  21.9 us
    all_to_all x1, blocking collectives, layer(): lax.all_to_all(doubled.reshape((chips,) + picked.shape[1:]), CHIP, split_...  17.1 us
    pallas_call x1, Pallas kernels, layer(): pl.pallas_call(functools.partial(attend_kernel, (nope + rope) ** (-0.5) *...  10.2 us
    pallas_call x2, Pallas kernels, mix(): pl.pallas_call(mix_kernel, name='mix', grid=(blocks,), in_specs=[pl.Block...  8.72 us
    pallas_call x1, Pallas kernels, layer(): pl.pallas_call(query_kernel, name='query', grid=(steps,), in_specs=[whole...  6.36 us
  transfers between devices with their start and end apart: 11, of which 4 were waited for; matrix products, arithmetic and copies ran while one was open for 1% of the time, Pallas kernels for 26%

profile of v3, /device:TPU:0, one launch (start us, length us, event | category | flops | bytes accessed | tf_op | source)
XLA Modules:
  0.0 210.4 jit_solution(10540521479250787394)
XLA Ops:
  0.7 1.2 copy-done
  2.8 21.9 %all_to_all.30 = bf16[32,40,128]{2,1,0:T(8,128)(2,1)S(1)} all-to-all(bf16[32,40,128]{2,1,0:T(8,128)(2,1)S(1)} %concatenate.3), channel_id=1, replica_groups=mesh['req'=32,'ylo'=2,'core'=2] {'req'}, dimensions={0} | all-to-all | bytes 655360 | tf_op jit(solution)/shard_map/all_to_all | solution.py:293
  26.2 17.1 %all_to_all.31 = bf16[64,40,128]{2,1,0:T(8,128)(2,1)S(1)} all-to-all(bf16[64,40,128]{2,1,0:T(8,128)(2,1)S(1)} %bitcast.37), channel_id=1, replica_groups=mesh['req'=32,'ylo'=2,'core'=2] {'req','ylo'}, dimensions={0} | all-to-all | bytes 1310720 | tf_op jit(solution)/shard_map/all_to_all | solution.py:306
  45.3 3.5 %cache.1 = (bf16[576,128]{1,0:T(8,128)(2,1)}, bf16[128,2048]{1,0:T(8,128)(2,1)}, f32[128,64]{1,0:T(8,128)}) custom-call(s32[1,3]{1,0:T(1,128)} %lengths_ref.3, s32[2]{0:T(128)} %pad_add_fusion.sub_ref, bf16[128,2048]{1,0:T(8,128)(2,1)} %tokens_hbm.1, f32[1,2048]{1,0:T(1,128)} %bitcast.45, bf16[576,2048]{1,0:T(8,128)(2,1)} %bitcast.39, f32[1,512]{1,0:T(1,128)} %bitcast.46, ...), custom_call_target="tpu_custom_call" | custom-call | flops 301989888 | bytes 4000000 | tf_op jit(solution)/shard_map/cache/pallas_call | solution.py:328
  49.3 0.7 collective-permute-start.1
  50.0 1.0 collective-permute-start.2
  51.0 6.4 %query.1.query_ref = bf16[8,128,576]{2,1,0:T(8,128)(2,1)} custom-call(bf16[128,2048]{1,0:T(8,128)(2,1)} %get-tuple-element.8.normed_ref, f32[128,64]{1,0:T(8,128)} %get-tuple-element.9.angle_ref, bf16[2048,1536]{1,0:T(8,128)(2,1)} %wq_ref.1, bf16[8,128,512]{2,1,0:T(8,128)(2,1)} %wk_ref.1), custom_call_target="tpu_custom_call" | custom-call | flops 805306368 | bytes 9000000 | tf_op jit(solution)/shard_map/query/pallas_call | solution.py:340
  57.3 1.7 route.1.place_hbm.place_ref
  59.1 10.2 %attend.1 = (f32[128,2048]{1,0:T(8,128)}, bf16[128,2048]{1,0:T(8,128)(2,1)}, bf16[512,2048]{1,0:T(8,128)(2,1)}) custom-call(s32[1,3]{1,0:T(1,128)} %lengths_ref.3, s32[2]{0:T(128)} %pad_add_fusion.sub_ref, bf16[8,128,576]{2,1,0:T(8,128)(2,1)} %query.1.query_ref, bf16[576,128]{1,0:T(8,128)(2,1)} %get-tuple-element.10.own_ref, ...), custom_call_target="tpu_custom_call" | custom-call | flops 5000000000 | bytes 6000000 | tf_op jit(solution)/shard_map/attend/pallas_call | solution.py:384
  69.3 5.9 %all-to-all-start.2 = ((bf16[64,8,2048]{2,1,0:T(8,128)(2,1)}), bf16[64,8,2048]{2,1,0:T(8,128)(2,1)S(1)}, u32[]{:S(2)}, u32[]{:S(2)}) async-start(bf16[64,8,2048]{2,1,0:T(8,128)(2,1)} %bitcast.41), calls=%async_computation.2 | async-start | bytes 4194304 | tf_op jit(solution)/shard_map/all_to_all | solution.py:413
  75.9 2.9 %place.1 = bf16[512,2048]{1,0:T(8,128)(2,1)} custom-call(bf16[2,512,128]{2,1,0:T(8,128)(2,1)} %route.1.place_hbm.place_ref, bf16[128,2048]{1,0:T(8,128)(2,1)} %get-tuple-element.13.mid_ref), custom_call_target="tpu_custom_call" | custom-call | flops 268435456 | bytes 3000000 | tf_op jit(solution)/shard_map/place/pallas_call | solution.py:417
  78.8 24.9 %all-to-all-done.2 = bf16[64,8,2048]{2,1,0:T(8,128)(2,1)S(1)} async-done(((bf16[64,8,2048]{2,1,0:T(8,128)(2,1)}), bf16[64,8,2048]{2,1,0:T(8,128)(2,1)S(1)}, u32[]{:S(2)}, u32[]{:S(2)}) %all-to-all-start.2) | async-done | bytes 2097184 | tf_op jit(solution)/shard_map/all_to_all | solution.py:413
  103.7 7.3 %all-to-all-start.4 = ((bf16[64,8,2048]{2,1,0:T(8,128)(2,1)}), bf16[64,8,2048]{2,1,0:T(8,128)(2,1)}, u32[]{:S(2)}, u32[]{:S(2)}) async-start(bf16[64,8,2048]{2,1,0:T(8,128)(2,1)} %bitcast.36), calls=%async_computation.4 | async-start | bytes 4194304 | tf_op jit(solution)/shard_map/all_to_all | solution.py:413
  111.0 15.0 %experts.2 = bf16[512,2048]{1,0:T(8,128)(2,1)} custom-call(bf16[512,2048]{1,0:T(8,128)(2,1)S(1)} %bitcast.35, bf16[704,2048]{1,0:T(8,128)(2,1)} %bitcast.48, bf16[704,2048]{1,0:T(8,128)(2,1)} %bitcast.51, bf16[704,2048]{1,0:T(8,128)(2,1)} %bitcast.54, bf16[704,2048]{1,0:T(8,128)(2,1)} %collective-permute-done.4.g1, ...), custom_call_target="tpu_custom_call" | custom-call | flops 8858370048 | bytes 21000000 | tf_op jit(solution)/shard_map/experts/pallas_call | solution.py:430
  126.0 12.2 %all-to-all-done.4 = bf16[64,8,2048]{2,1,0:T(8,128)(2,1)} async-done(((bf16[64,8,2048]{2,1,0:T(8,128)(2,1)}), bf16[64,8,2048]{2,1,0:T(8,128)(2,1)}, u32[]{:S(2)}, u32[]{:S(2)}) %all-to-all-start.4) | async-done | bytes 2097184 | tf_op jit(solution)/shard_map/all_to_all | solution.py:413
  138.2 6.0 %all-to-all-start.3 = ((bf16[64,8,2048]{2,1,0:T(8,128)(2,1)}), bf16[64,8,2048]{2,1,0:T(8,128)(2,1)S(1)}, u32[]{:S(2)}, u32[]{:S(2)}) async-start(bf16[64,8,2048]{2,1,0:T(8,128)(2,1)} %bitcast.43), calls=%async_computation.3 | async-start | bytes 4194304 | tf_op jit(solution)/shard_map/all_to_all | solution.py:413
  144.3 16.5 %experts.3 = bf16[512,2048]{1,0:T(8,128)(2,1)} custom-call(bf16[512,2048]{1,0:T(8,128)(2,1)} %bitcast.26.x_ref, bf16[704,2048]{1,0:T(8,128)(2,1)} %bitcast.49, bf16[704,2048]{1,0:T(8,128)(2,1)} %bitcast.52, bf16[704,2048]{1,0:T(8,128)(2,1)} %bitcast.55, bf16[704,2048]{1,0:T(8,128)(2,1)} %collective-permute-done.4.g1, ...), custom_call_target="tpu_custom_call" | custom-call | flops 8858370048 | bytes 21000000 | tf_op jit(solution)/shard_map/experts/pallas_call | solution.py:430
  160.8 11.3 %all-to-all-done.3 = bf16[64,8,2048]{2,1,0:T(8,128)(2,1)S(1)} async-done(((bf16[64,8,2048]{2,1,0:T(8,128)(2,1)}), bf16[64,8,2048]{2,1,0:T(8,128)(2,1)S(1)}, u32[]{:S(2)}, u32[]{:S(2)}) %all-to-all-start.3) | async-done | bytes 2097184 | tf_op jit(solution)/shard_map/all_to_all | solution.py:413
  172.1 6.2 %all-to-all-start.5 = ((bf16[64,8,2048]{2,1,0:T(8,128)(2,1)}), bf16[64,8,2048]{2,1,0:T(8,128)(2,1)}, u32[]{:S(2)}, u32[]{:S(2)}) async-start(bf16[64,8,2048]{2,1,0:T(8,128)(2,1)} %bitcast.42), calls=%async_computation.5 | async-start | bytes 4194304 | tf_op jit(solution)/shard_map/all_to_all | solution.py:413
  178.3 2.0 gates.2.mix_ref
  180.4 2.0 gates.3.mix_ref
  182.4 4.1 %mix.2.base_ref = f32[128,2048]{1,0:T(8,128)} custom-call(f32[128,2048]{1,0:T(8,128)} %get-tuple-element.11.base_ref, bf16[256,512]{1,0:T(8,128)(2,1)} %gates.2.mix_ref, bf16[512,2048]{1,0:T(8,128)(2,1)S(1)} %bitcast.34), custom_call_target="tpu_custom_call" | custom-call | flops 536870912 | bytes 3000000 | tf_op jit(solution)/shard_map/mix/pallas_call | solution.py:448
  186.5 19.3 %all-to-all-done.5 = bf16[64,8,2048]{2,1,0:T(8,128)(2,1)} async-done(((bf16[64,8,2048]{2,1,0:T(8,128)(2,1)}), bf16[64,8,2048]{2,1,0:T(8,128)(2,1)}, u32[]{:S(2)}, u32[]{:S(2)}) %all-to-all-start.5) | async-done | bytes 2097184 | tf_op jit(solution)/shard_map/all_to_all | solution.py:413
  205.8 4.7 %mix.3 = bf16[128,2048]{1,0:T(8,128)(2,1)} custom-call(f32[128,2048]{1,0:T(8,128)} %mix.2.base_ref, bf16[256,512]{1,0:T(8,128)(2,1)} %gates.3.mix_ref, bf16[512,2048]{1,0:T(8,128)(2,1)} %bitcast.28.rows_ref), custom_call_target="tpu_custom_call" | custom-call | flops 536870912 | bytes 3000000 | tf_op jit(solution)/shard_map/mix/pallas_call | solution.py:448
  (32 shorter events, 4.9 us)
Async XLA Ops:
  0.6 1.3 copy-start
  0.6 24.7 %copy-start.2 = (s32[4]{0:T(128)S(1)}, s32[4]{0:T(128)}, u32[]{:S(2)}) copy-start(s32[4]{0:T(128)} %param.35) | copy-start | bytes 52
  43.3 1.3 copy-start.1
  44.0 15.1 %collective-permute-start.3 = (bf16[4,576,128]{2,1,0:T(8,128)(2,1)S(1)}, bf16[4,576,128]{2,1,0:T(8,128)(2,1)S(1)}, u32[]{:S(2)}, u32[]{:S(2)}) collective-permute-start(bf16[4,576,128]{2,1,0:T(8,128)(2,1)S(1)} %reshape.62.near_ref), channel_id=1, source_target_pairs={{0,1},{1,0},{2,3},{3,2},{4,5},{5,4},{6,7},{7,6},{8,9},{9,8},{10,11... | collective-permute-start | bytes 1769480 | tf_op jit(solution)/shard_map/ppermute | solution.py:312
  48.8 10.2 %collective-permute-start = (bf16[576,128]{1,0:T(8,128)(2,1)}, bf16[576,128]{1,0:T(8,128)(2,1)S(1)}, u32[]{:S(2)}, u32[]{:S(2)}) collective-permute-start(bf16[576,128]{1,0:T(8,128)(2,1)} %get-tuple-element.10.own_ref), channel_id=1, source_target_pairs={{0,1},{1,2},{2,3},{3,0},{4,5},{5,6},{6,7},{7,4},{8,9},{9,10},{10,1... | collective-permute-start | bytes 442376 | tf_op jit(solution)/shard_map/ppermute | solution.py:355
  49.3 9.7 %collective-permute-start.1 = (bf16[576,128]{1,0:T(8,128)(2,1)}, bf16[576,128]{1,0:T(8,128)(2,1)S(1)}, u32[]{:S(2)}, u32[]{:S(2)}) collective-permute-start(bf16[576,128]{1,0:T(8,128)(2,1)} %get-tuple-element.10.own_ref), channel_id=1, source_target_pairs={{0,2},{1,3},{2,0},{3,1},{4,6},{5,7},{6,4},{7,5},{8,10},{9,11},{10,... | collective-permute-start | bytes 442376 | tf_op jit(solution)/shard_map/ppermute | solution.py:355
  50.0 9.1 %collective-permute-start.2 = (bf16[576,128]{1,0:T(8,128)(2,1)}, bf16[576,128]{1,0:T(8,128)(2,1)S(1)}, u32[]{:S(2)}, u32[]{:S(2)}) collective-permute-start(bf16[576,128]{1,0:T(8,128)(2,1)} %get-tuple-element.10.own_ref), channel_id=1, source_target_pairs={{0,3},{1,0},{2,1},{3,2},{4,7},{5,4},{6,5},{7,6},{8,11},{9,8},{10,9... | collective-permute-start | bytes 442376 | tf_op jit(solution)/shard_map/ppermute | solution.py:355
  69.3 34.4 %all-to-all-start.2 = ((bf16[64,8,2048]{2,1,0:T(8,128)(2,1)}), bf16[64,8,2048]{2,1,0:T(8,128)(2,1)S(1)}, u32[]{:S(2)}, u32[]{:S(2)}) async-start(bf16[64,8,2048]{2,1,0:T(8,128)(2,1)} %bitcast.41), calls=%async_computation.2 | async-start | bytes 4194304 | tf_op jit(solution)/shard_map/all_to_all | solution.py:413
  75.2 35.8 %collective-permute-start.4 = (bf16[704,2048]{1,0:T(8,128)(2,1)}, bf16[704,2048]{1,0:T(8,128)(2,1)}, u32[]{:S(2)}, u32[]{:S(2)}) collective-permute-start(bf16[704,2048]{1,0:T(8,128)(2,1)} %bitcast.47), channel_id=1, source_target_pairs={{0,1},{1,0},{2,3},{3,2},{4,5},{5,4},{6,7},{7,6},{8,9},{9,8},{10,11... | collective-permute-start | bytes 8650760 | tf_op jit(solution)/shard_map/ppermute | solution.py:317
  75.3 35.7 %collective-permute-start.5 = (bf16[704,2048]{1,0:T(8,128)(2,1)}, bf16[704,2048]{1,0:T(8,128)(2,1)}, u32[]{:S(2)}, u32[]{:S(2)}) collective-permute-start(bf16[704,2048]{1,0:T(8,128)(2,1)} %bitcast.50), channel_id=1, source_target_pairs={{0,1},{1,0},{2,3},{3,2},{4,5},{5,4},{6,7},{7,6},{8,9},{9,8},{10,11... | collective-permute-start | bytes 8650760 | tf_op jit(solution)/shard_map/ppermute | solution.py:318
  75.8 35.2 %collective-permute-start.6 = (bf16[704,2048]{1,0:T(8,128)(2,1)}, bf16[704,2048]{1,0:T(8,128)(2,1)}, u32[]{:S(2)}, u32[]{:S(2)}) collective-permute-start(bf16[704,2048]{1,0:T(8,128)(2,1)} %bitcast.53), channel_id=1, source_target_pairs={{0,1},{1,0},{2,3},{3,2},{4,5},{5,4},{6,7},{7,6},{8,9},{9,8},{10,11... | collective-permute-start | bytes 8650760 | tf_op jit(solution)/shard_map/ppermute | solution.py:319
  103.7 34.5 %all-to-all-start.4 = ((bf16[64,8,2048]{2,1,0:T(8,128)(2,1)}), bf16[64,8,2048]{2,1,0:T(8,128)(2,1)}, u32[]{:S(2)}, u32[]{:S(2)}) async-start(bf16[64,8,2048]{2,1,0:T(8,128)(2,1)} %bitcast.36), calls=%async_computation.4 | async-start | bytes 4194304 | tf_op jit(solution)/shard_map/all_to_all | solution.py:413
  138.2 33.9 %all-to-all-start.3 = ((bf16[64,8,2048]{2,1,0:T(8,128)(2,1)}), bf16[64,8,2048]{2,1,0:T(8,128)(2,1)S(1)}, u32[]{:S(2)}, u32[]{:S(2)}) async-start(bf16[64,8,2048]{2,1,0:T(8,128)(2,1)} %bitcast.43), calls=%async_computation.3 | async-start | bytes 4194304 | tf_op jit(solution)/shard_map/all_to_all | solution.py:413
  172.1 33.7 %all-to-all-start.5 = ((bf16[64,8,2048]{2,1,0:T(8,128)(2,1)}), bf16[64,8,2048]{2,1,0:T(8,128)(2,1)}, u32[]{:S(2)}, u32[]{:S(2)}) async-start(bf16[64,8,2048]{2,1,0:T(8,128)(2,1)} %bitcast.42), calls=%async_computation.5 | async-start | bytes 4194304 | tf_op jit(solution)/shard_map/all_to_all | solution.py:413

commit v4 on v3

--- a/solution.py
+++ b/solution.py
@@ -122,17 +122,56 @@
         ).astype(BF16)
 
 
+PAIR = 2
+
+
+def late_kernel(
+    score_scale, lengths_ref, sub_ref, query_ref, own_ref, back_1_ref, back_2_ref, back_3_ref,
+    weighted_ref, stats_ref, keys, bias,
+):
+    heads, rows, width = query_ref.shape
+    lat = weighted_ref.shape[1]
+    suffix = (own_ref, back_1_ref, back_2_ref, back_3_ref)
+    pos = sub_ref[0] * rows + iota((rows, rows), 0)
+    start = seg_starts(lengths_ref, pos)
+    for d, ref in enumerate(suffix):
+        at = slice(d * rows, (d + 1) * rows)
+        keys[:, at] = ref[...]
+        key_pos = ((sub_ref[0] + len(suffix) - d) % len(suffix)) * rows + iota((rows, rows), 1)
+        allowed = (key_pos >= start) & (key_pos <= pos)
+        bias[:, at] = jnp.where(allowed, 0.0, FLOOR_SCORE)
+    mask = jnp.concatenate([bias[...]] * PAIR, axis=0)
+    count = PAIR * rows
+    lane = iota((count, stats_ref.shape[1]), 1)
+
+    def score(i):
+        query = query_ref[i * PAIR : (i + 1) * PAIR].reshape(count, width)
+        return dot(query, keys[...]) + mask
+
+    current = score(0)
+    for i in range(heads // PAIR):
+        following = score(i + 1) if i + 1 < heads // PAIR else None
+        at = slice(i * count, (i + 1) * count)
+        row_top = jnp.max(current, axis=1, keepdims=True)
+        weights = jnp.exp2((current - row_top) * score_scale)
+        denominator = jnp.sum(weights, axis=1, keepdims=True)
+        weighted_ref[at] = dot_nt(weights.astype(BF16), keys[:lat])
+        stats_ref[at] = jnp.where(lane == 0, row_top, denominator)
+        current = following
+
+
 def attend_kernel(
-    score_scale, lengths_ref, sub_ref, query_ref, own_ref, back_1_ref, back_2_ref, back_3_ref,
-    near_ref, far_ref, gain_ref, wv_hbm, wo_hbm, tokens_hbm, place_hbm,
-    residual_ref, mid_ref, out_ref,
-    keys, bias, query_buf, wv_ref, wo_ref, tokens_ref, place_ref, sems,
+    score_scale, query_hbm, late_hbm, stats_hbm, near_ref, far_ref, gain_ref,
+    wv_hbm, wo_hbm, tokens_hbm, place_hbm,
+    residual_hbm, mid_hbm, out_hbm,
+    keys, query_ref, late_ref, stats_ref, wv_ref, wo_ref, tokens_ref, place_ref,
+    residual_ref, mid_ref, out_ref, sems,
 ):
     copies = [
         pltpu.make_async_copy(src, dst, sems.at[i])
         for i, (src, dst) in enumerate((
-            (query_ref, query_buf), (wv_hbm, wv_ref), (wo_hbm, wo_ref), (tokens_hbm, tokens_ref),
-            (place_hbm.at[0], place_ref),
+            (query_hbm, query_ref), (stats_hbm, stats_ref), (late_hbm, late_ref), (wv_hbm, wv_ref),
+            (wo_hbm, wo_ref), (tokens_hbm, tokens_ref), (place_hbm.at[0], place_ref),
         ))
     ]
     for copy in copies:
@@ -141,62 +180,65 @@
     heads, lat, _ = wv_ref.shape
     width = query_ref.shape[2]
     near_tiles = near_ref.shape[0]
-    tiles = near_tiles + far_ref.shape[0]
-    suffix = (own_ref, back_1_ref, back_2_ref, back_3_ref)
     for i in range(near_tiles):
         keys[:, i * rows : (i + 1) * rows] = near_ref[i]
         keys[:, (near_tiles + i) * rows : (near_tiles + i + 1) * rows] = far_ref[i]
-    pos = sub_ref[0] * rows + iota((rows, rows), 0)
-    start = seg_starts(lengths_ref, pos)
-    for d, ref in enumerate(suffix):
-        keys[:, (tiles + d) * rows : (tiles + d + 1) * rows] = ref[...]
-        key_pos = ((sub_ref[0] + len(suffix) - d) % len(suffix)) * rows + iota((rows, rows), 1)
-        allowed = (key_pos >= start) & (key_pos <= pos)
-        bias[:, d * rows : (d + 1) * rows] = jnp.where(allowed, 0.0, FLOOR_SCORE)
-    cut = tiles * rows
-    pair = 2
-    mask = jnp.concatenate([bias[...]] * pair, axis=0)
+    count = PAIR * rows
 
     def score(i):
-        query = query_buf[i * pair : (i + 1) * pair].reshape(pair * rows, width)
-        return dot(query, keys[:, :cut]), dot(query, keys[:, cut:]) + mask
-
-    def attend(early, late):
-        row_top = jnp.maximum(
-            jnp.max(early, axis=1, keepdims=True), jnp.max(late, axis=1, keepdims=True)
-        )
+        query = query_ref[i * PAIR : (i + 1) * PAIR].reshape(count, width)
+        return dot(query, keys[...])
+
+    def attend(i, early):
+        at = slice(i * count, (i + 1) * count)
+        late_top = stats_ref[at, 0:1]
+        row_top = jnp.maximum(jnp.max(early, axis=1, keepdims=True), late_top)
         early = jnp.exp2((early - row_top) * score_scale)
-        late = jnp.exp2((late - row_top) * score_scale)
-        denominator = jnp.sum(early, axis=1, keepdims=True) + jnp.sum(late, axis=1, keepdims=True)
-        weighted = dot_nt(early.astype(BF16), keys[:lat, :cut]) + dot_nt(
-            late.astype(BF16), keys[:lat, cut:]
-        )
+        share = jnp.exp2((late_top - row_top) * score_scale)
+        denominator = jnp.sum(early, axis=1, keepdims=True) + share * stats_ref[at, 1:2]
+        weighted = dot_nt(early.astype(BF16), keys[:lat]) + late_ref[at] * share
         return (weighted / denominator).astype(BF16)
 
     latent_out = []
     copies[0].wait()
     current = score(0)
-    for i in range(heads // pair):
-        following = score(i + 1) if i + 1 < heads // pair else None
-        latent_out.append(attend(*current))
+    copies[1].wait()
+    copies[2].wait()
+    for i in range(heads // PAIR):
+        following = score(i + 1) if i + 1 < heads // PAIR else None
+        latent_out.append(attend(i, current))
         current = following
-    copies[1].wait()
+    copies[3].wait()
     head_out = jnp.concatenate(
         [
-            dot(latent_out[h // pair][h % pair * rows : (h % pair + 1) * rows], wv_ref[h]).astype(BF16)
+            dot(latent_out[h // PAIR][h % PAIR * rows : (h % PAIR + 1) * rows], wv_ref[h]).astype(BF16)
             for h in range(heads)
         ],
         axis=1,
     )
-    copies[2].wait()
-    copies[3].wait()
+    copies[4].wait()
+    copies[5].wait()
     x = tokens_ref[...].astype(F32) + dot(head_out, wo_ref[...])
     residual_ref[...] = x
+    base = len(copies)
+    writes = [pltpu.make_async_copy(residual_ref, residual_hbm, sems.at[base])]
+    writes[0].start()
     scale = lax.rsqrt(jnp.mean(x * x, axis=-1, keepdims=True) + EPSILON)
     mid = (x * scale * gain_ref[...]).astype(BF16)
     mid_ref[...] = mid
-    copies[4].wait()
-    out_ref[...] = dot(place_ref[...], mid).astype(BF16)
+    writes.append(pltpu.make_async_copy(mid_ref, mid_hbm, sems.at[base + 1]))
+    writes[1].start()
+    copies[6].wait()
+    step = out_ref.shape[0] // 2
+    for i in range(2):
+        at = slice(i * step, (i + 1) * step)
+        out_ref[at] = dot(place_ref[at], mid).astype(BF16)
+        writes.append(
+            pltpu.make_async_copy(out_ref.at[at], out_hbm.at[at], sems.at[base + 2 + i])
+        )
+        writes[-1].start()
+    for write in writes:
+        write.wait()
 
 
 def place_kernel(place_ref, mid_ref, out_ref):
@@ -235,9 +277,7 @@
 
 def mix_kernel(base_ref, mix_ref, rows_ref, out_ref):
     rows = base_ref.shape[0]
-    width = base_ref.shape[1]
-    columns = pl.ds(pl.multiple_of(pl.program_id(0) * width, width), width)
-    both = dot(mix_ref[...], rows_ref[:, columns])
+    both = dot(mix_ref[...], rows_ref[...])
     out_ref[...] = (base_ref[...] + (both[:rows] + both[rows:])).astype(out_ref.dtype)
 
 
@@ -293,6 +333,7 @@
     spread = lax.all_to_all(
         jnp.concatenate([pieces, tag], axis=1), "req", split_axis=0, concat_axis=0, tiled=True
     )
+    ylo_count = lax.axis_size("ylo")
     groups = spread[:, piece, 0].astype(jnp.int32)
     slots = jnp.sum(
         jnp.where(
@@ -300,12 +341,8 @@
         ),
         axis=1,
     )
-    picked = jnp.take(spread, slots, axis=0, mode="clip")
-    ylo_count = lax.axis_size("ylo")
-    doubled = jnp.broadcast_to(picked[:, None], (req_count, ylo_count) + picked.shape[1:])
-    near = lax.all_to_all(
-        doubled.reshape((chips,) + picked.shape[1:]), CHIP, split_axis=0, concat_axis=0, tiled=True
-    )
+    picked = jnp.take(spread, jnp.repeat(slots, ylo_count), axis=0, mode="clip")
+    near = lax.all_to_all(picked, CHIP, split_axis=0, concat_axis=0, tiled=True)
     near = near[:, :piece].reshape(req_count, ylo_count, piece, lanes).transpose(1, 0, 2, 3)
     near = near.reshape(ylo_count * quarter_len // lanes, width, lanes)
     swap = [(0, 1), (1, 0)]
@@ -381,30 +418,48 @@
         )(ids_t, gates_t, placing))
 
     moe_row = moe_gain[None, :]
+    score_scale = (nope + rope) ** (-0.5) * math.log2(math.e)
+    lines = head_count * rows
+    late, stats = pl.pallas_call(
+        functools.partial(late_kernel, score_scale),
+        name="late",
+        in_specs=[SMEM, SMEM] + [VMEM] * 5,
+        out_specs=[VMEM, VMEM],
+        out_shape=[pltpu.HBM((lines, lat), F32), pltpu.HBM((lines, 128), F32)],
+        scratch_shapes=[
+            pltpu.VMEM((width, rows * sub_count), BF16), pltpu.VMEM((rows, rows * sub_count), F32),
+        ],
+        compiler_params=limit(54),
+        cost_estimate=cost(1e9, 6e6),
+    )(lengths, place_info, query_full, cache_t, *map(near_core, back))
     residual, mid, first_out = pl.pallas_call(
-        functools.partial(attend_kernel, (nope + rope) ** (-0.5) * math.log2(math.e)),
+        functools.partial(attend_kernel, score_scale),
         name="attend",
-        in_specs=[SMEM, SMEM, HBM] + [VMEM] * 7 + [HBM] * 4,
-        out_specs=[VMEM, VMEM, VMEM],
+        in_specs=[HBM] * 3 + [VMEM] * 3 + [HBM] * 4,
+        out_specs=[HBM, HBM, HBM],
         out_shape=[
             pltpu.HBM((rows, model), F32),
             pltpu.HBM((rows, model), BF16),
             pltpu.HBM((part_slots, model), BF16),
         ],
         scratch_shapes=[
-            pltpu.VMEM((width, prefix_len + rows * sub_count), BF16),
-            pltpu.VMEM((rows, rows * sub_count), F32),
+            pltpu.VMEM((width, prefix_len), BF16),
             pltpu.VMEM(query_full.shape, BF16),
+            pltpu.VMEM((lines, lat), F32),
+            pltpu.VMEM((lines, 128), F32),
             pltpu.VMEM(w_value_up.shape, BF16),
             pltpu.VMEM(w_out.shape, BF16),
             pltpu.VMEM(tokens.shape, BF16),
             pltpu.VMEM((part_slots, rows), BF16),
-            pltpu.SemaphoreType.DMA((5,)),
+            pltpu.VMEM((rows, model), F32),
+            pltpu.VMEM((rows, model), BF16),
+            pltpu.VMEM((part_slots, model), BF16),
+            pltpu.SemaphoreType.DMA((11,)),
         ],
         compiler_params=limit(54),
         cost_estimate=cost(5e9, 6e6),
     )(
-        lengths, place_info, query_full, cache_t, *map(near_core, (*back, near, far)),
+        query_full, late, stats, near_core(near), near_core(far),
         moe_row, w_value_up, w_out, tokens, placing,
     )
 
@@ -441,16 +496,13 @@
             cost_estimate=cost(12 * part_slots * model * hidden, 21e6),
         )(near_core(x), gate_t, up_t, down, gate_far, up_far, down_far)
 
-    blocks = 4
-
     def mix(base, part, x, last):
         shape = (rows, model)
         return pl.pallas_call(
             mix_kernel,
             name="mix",
-            grid=(blocks,),
-            in_specs=[pl.BlockSpec((rows, model // blocks), lambda i: (0, i)), VMEM, VMEM],
-            out_specs=pl.BlockSpec((rows, model // blocks), lambda i: (0, i)),
+            in_specs=[VMEM] * 3,
+            out_specs=VMEM,
             out_shape=pltpu.HBM(shape, BF16 if last else F32),
             compiler_params=limit(54),
             cost_estimate=cost(4 * part_slots * rows * model, 3e6),

time: 211 us -> 213 us (level)
    pallas_call x3 -> x4, Pallas kernels: 19 us -> 19.7 us  [the longest x1 8.88 us: layer(): pl.pallas_call(functools.partial(attend_kernel, score_scale), name='atten...]
  transfers between devices with their start and end apart: 11 -> 11, of which waited for: 4 -> 4; matrix products, arithmetic and copies ran while one was open for 1% -> 1% of each run, Pallas kernels for 26% -> 27%
where the time goes in v4:
time: 213 us; the launch traced here: 212 us
  Pallas kernels  69.9 us (33%)
  waiting for transfers between devices  68.7 us (32%)
  blocking collectives  39 us (18%)
  starting transfers between devices  28.3 us (13%)
  local copies, waits for them, and re-layouts  3.69 us (2%)
    all_to_all x4, waiting for transfers between devices, exchange(): x = lax.all_to_all(x, CHIP, split_axis=0, concat_axis=0, tiled=True)  68.7 us
    pallas_call x2, Pallas kernels, experts(): pl.pallas_call(expert_kernel, name='experts', in_specs=[VMEM] + [HBM] * 6...  31.6 us
    all_to_all x4, starting transfers between devices, exchange(): x = lax.all_to_all(x, CHIP, split_axis=0, concat_axis=0, tiled=True)  25.4 us
    all_to_all x1, blocking collectives, layer(): lax.all_to_all(jnp.concatenate([pieces, tag], axis=1), 'req', split_axis=...  21.9 us
    all_to_all x1, blocking collectives, layer(): near = lax.all_to_all(picked, CHIP, split_axis=0, concat_axis=0, tiled=True)  17.1 us
    pallas_call x1, Pallas kernels, layer(): pl.pallas_call(functools.partial(attend_kernel, score_scale), name='atten...  8.88 us
    pallas_call x2, Pallas kernels, mix(): pl.pallas_call(mix_kernel, name='mix', in_specs=[VMEM] * 3, out_specs=VME...  6.47 us
    pallas_call x1, Pallas kernels, layer(): pl.pallas_call(query_kernel, name='query', grid=(steps,), in_specs=[whole...  6.37 us
  transfers between devices with their start and end apart: 11, of which 4 were waited for; matrix products, arithmetic and copies ran while one was open for 1% of the time, Pallas kernels for 27%

profile of v4, /device:TPU:0, one launch (start us, length us, event | category | flops | bytes accessed | tf_op | source)
XLA Modules:
  0.0 212.4 jit_solution(7677502939577643440)
XLA Ops:
  0.7 1.2 copy-done
  2.8 21.9 %all_to_all.30 = bf16[32,40,128]{2,1,0:T(8,128)(2,1)S(1)} all-to-all(bf16[32,40,128]{2,1,0:T(8,128)(2,1)S(1)} %concatenate.3), channel_id=1, replica_groups=mesh['req'=32,'ylo'=2,'core'=2] {'req'}, dimensions={0} | all-to-all | bytes 655360 | tf_op jit(solution)/shard_map/all_to_all | solution.py:333
  26.4 17.1 %all_to_all.31 = bf16[64,40,128]{2,1,0:T(8,128)(2,1)S(1)} all-to-all(bf16[64,40,128]{2,1,0:T(8,128)(2,1)S(1)} %gather_fusion), channel_id=1, replica_groups=mesh['req'=32,'ylo'=2,'core'=2] {'req','ylo'}, dimensions={0} | all-to-all | bytes 1310720 | tf_op jit(solution)/shard_map/all_to_all | solution.py:345
  45.5 3.5 %cache.1 = (bf16[576,128]{1,0:T(8,128)(2,1)}, bf16[128,2048]{1,0:T(8,128)(2,1)}, f32[128,64]{1,0:T(8,128)}) custom-call(s32[1,3]{1,0:T(1,128)} %lengths_ref.3, s32[2]{0:T(128)} %pad_add_fusion.sub_ref, bf16[128,2048]{1,0:T(8,128)(2,1)} %tokens_hbm.1, f32[1,2048]{1,0:T(1,128)} %bitcast.43, bf16[576,2048]{1,0:T(8,128)(2,1)} %bitcast.37, f32[1,512]{1,0:T(1,128)} %bitcast.44, ...), custom_call_target="tpu_custom_call" | custom-call | flops 301989888 | bytes 4000000 | tf_op jit(solution)/shard_map/cache/pallas_call | solution.py:365
  50.2 1.0 collective-permute-start.2
  51.1 6.4 %query.1.query_ref.query_hbm = bf16[8,128,576]{2,1,0:T(8,128)(2,1)} custom-call(bf16[128,2048]{1,0:T(8,128)(2,1)} %get-tuple-element.10.normed_ref, f32[128,64]{1,0:T(8,128)} %get-tuple-element.11.angle_ref, bf16[2048,1536]{1,0:T(8,128)(2,1)} %wq_ref.1, bf16[8,128,512]{2,1,0:T(8,128)(2,1)} %wk_ref.1), custom_call_target="tpu_custom_call" | custom-call | flops 805306368 | bytes 9000000 | tf_op jit(solution)/shard_map/query/pallas_call | solution.py:377
  57.5 1.7 route.1.place_hbm.place_ref
  59.3 4.4 %late.1 = (f32[1024,512]{1,0:T(8,128)}, f32[1024,128]{1,0:T(8,128)}) custom-call(s32[1,3]{1,0:T(1,128)} %lengths_ref.3, s32[2]{0:T(128)} %pad_add_fusion.sub_ref, bf16[8,128,576]{2,1,0:T(8,128)(2,1)} %query.1.query_ref.query_hbm, bf16[576,128]{1,0:T(8,128)(2,1)} %get-tuple-element.12.own_ref, bf16[576,128]{1,0:T(8,128)(2,1)S(1)} %collective-permute-done.back_1_ref, ...), custom_call_target="tpu_custom_call" | custom-call | flops 1000000000 | bytes 6000000 | tf_op jit(solution)/shard_map/late/pallas_call | solution.py:423
  63.6 8.9 %attend.1 = (f32[128,2048]{1,0:T(8,128)}, bf16[128,2048]{1,0:T(8,128)(2,1)}, bf16[512,2048]{1,0:T(8,128)(2,1)}) custom-call(bf16[8,128,576]{2,1,0:T(8,128)(2,1)} %query.1.query_ref.query_hbm, f32[1024,512]{1,0:T(8,128)} %get-tuple-element.13.late_hbm, f32[1024,128]{1,0:T(8,128)} %get-tuple-element.14.stats_hbm, bf16[4,576,128]{2,1,0:T(8,128)(2,1)S(1)} %reshape.59.near_ref, ...), custom_call_target="tpu_custom_call" | custom-call | flops 5000000000 | bytes 6000000 | tf_op jit(solution)/shard_map/attend/pallas_call | solution.py:435
  72.5 5.9 %all-to-all-start.2 = ((bf16[64,8,2048]{2,1,0:T(8,128)(2,1)}), bf16[64,8,2048]{2,1,0:T(8,128)(2,1)S(1)}, u32[]{:S(2)}, u32[]{:S(2)}) async-start(bf16[64,8,2048]{2,1,0:T(8,128)(2,1)} %bitcast.39), calls=%async_computation.2 | async-start | bytes 4194304 | tf_op jit(solution)/shard_map/all_to_all | solution.py:468
  79.1 2.9 %place.1 = bf16[512,2048]{1,0:T(8,128)(2,1)} custom-call(bf16[2,512,128]{2,1,0:T(8,128)(2,1)} %route.1.place_hbm.place_ref, bf16[128,2048]{1,0:T(8,128)(2,1)} %get-tuple-element.17.mid_ref), custom_call_target="tpu_custom_call" | custom-call | flops 268435456 | bytes 3000000 | tf_op jit(solution)/shard_map/place/pallas_call | solution.py:472
  82.0 24.9 %all-to-all-done.2 = bf16[64,8,2048]{2,1,0:T(8,128)(2,1)S(1)} async-done(((bf16[64,8,2048]{2,1,0:T(8,128)(2,1)}), bf16[64,8,2048]{2,1,0:T(8,128)(2,1)S(1)}, u32[]{:S(2)}, u32[]{:S(2)}) %all-to-all-start.2) | async-done | bytes 2097184 | tf_op jit(solution)/shard_map/all_to_all | solution.py:468
  106.9 7.3 %all-to-all-start.4 = ((bf16[64,8,2048]{2,1,0:T(8,128)(2,1)}), bf16[64,8,2048]{2,1,0:T(8,128)(2,1)}, u32[]{:S(2)}, u32[]{:S(2)}) async-start(bf16[64,8,2048]{2,1,0:T(8,128)(2,1)} %bitcast.35), calls=%async_computation.4 | async-start | bytes 4194304 | tf_op jit(solution)/shard_map/all_to_all | solution.py:468
  114.2 15.0 %experts.2 = bf16[512,2048]{1,0:T(8,128)(2,1)} custom-call(bf16[512,2048]{1,0:T(8,128)(2,1)S(1)} %bitcast.34, bf16[704,2048]{1,0:T(8,128)(2,1)} %bitcast.46, bf16[704,2048]{1,0:T(8,128)(2,1)} %bitcast.49, bf16[704,2048]{1,0:T(8,128)(2,1)} %bitcast.52, bf16[704,2048]{1,0:T(8,128)(2,1)} %collective-permute-done.4.g1, ...), custom_call_target="tpu_custom_call" | custom-call | flops 8858370048 | bytes 21000000 | tf_op jit(solution)/shard_map/experts/pallas_call | solution.py:485
  129.2 12.2 %all-to-all-done.4 = bf16[64,8,2048]{2,1,0:T(8,128)(2,1)} async-done(((bf16[64,8,2048]{2,1,0:T(8,128)(2,1)}), bf16[64,8,2048]{2,1,0:T(8,128)(2,1)}, u32[]{:S(2)}, u32[]{:S(2)}) %all-to-all-start.4) | async-done | bytes 2097184 | tf_op jit(solution)/shard_map/all_to_all | solution.py:468
  141.4 6.0 %all-to-all-start.3 = ((bf16[64,8,2048]{2,1,0:T(8,128)(2,1)}), bf16[64,8,2048]{2,1,0:T(8,128)(2,1)S(1)}, u32[]{:S(2)}, u32[]{:S(2)}) async-start(bf16[64,8,2048]{2,1,0:T(8,128)(2,1)} %bitcast.41), calls=%async_computation.3 | async-start | bytes 4194304 | tf_op jit(solution)/shard_map/all_to_all | solution.py:468
  147.4 16.6 %experts.3 = bf16[512,2048]{1,0:T(8,128)(2,1)} custom-call(bf16[512,2048]{1,0:T(8,128)(2,1)} %bitcast.25.x_ref, bf16[704,2048]{1,0:T(8,128)(2,1)} %bitcast.47, bf16[704,2048]{1,0:T(8,128)(2,1)} %bitcast.50, bf16[704,2048]{1,0:T(8,128)(2,1)} %bitcast.53, bf16[704,2048]{1,0:T(8,128)(2,1)} %collective-permute-done.4.g1, ...), custom_call_target="tpu_custom_call" | custom-call | flops 8858370048 | bytes 21000000 | tf_op jit(solution)/shard_map/experts/pallas_call | solution.py:485
  164.1 11.2 %all-to-all-done.3 = bf16[64,8,2048]{2,1,0:T(8,128)(2,1)S(1)} async-done(((bf16[64,8,2048]{2,1,0:T(8,128)(2,1)}), bf16[64,8,2048]{2,1,0:T(8,128)(2,1)S(1)}, u32[]{:S(2)}, u32[]{:S(2)}) %all-to-all-start.3) | async-done | bytes 2097184 | tf_op jit(solution)/shard_map/all_to_all | solution.py:468
  175.3 6.2 %all-to-all-start.5 = ((bf16[64,8,2048]{2,1,0:T(8,128)(2,1)}), bf16[64,8,2048]{2,1,0:T(8,128)(2,1)}, u32[]{:S(2)}, u32[]{:S(2)}) async-start(bf16[64,8,2048]{2,1,0:T(8,128)(2,1)} %bitcast.40), calls=%async_computation.5 | async-start | bytes 4194304 | tf_op jit(solution)/shard_map/all_to_all | solution.py:468
  181.5 2.0 gates.2.mix_ref
  183.6 2.0 gates.3.mix_ref
  185.6 3.0 %mix.2.base_ref = f32[128,2048]{1,0:T(8,128)} custom-call(f32[128,2048]{1,0:T(8,128)} %get-tuple-element.15.base_ref, bf16[256,512]{1,0:T(8,128)(2,1)} %gates.2.mix_ref, bf16[512,2048]{1,0:T(8,128)(2,1)S(1)} %bitcast.33), custom_call_target="tpu_custom_call" | custom-call | flops 536870912 | bytes 3000000 | tf_op jit(solution)/shard_map/mix/pallas_call | solution.py:501
  188.5 20.4 %all-to-all-done.5 = bf16[64,8,2048]{2,1,0:T(8,128)(2,1)} async-done(((bf16[64,8,2048]{2,1,0:T(8,128)(2,1)}), bf16[64,8,2048]{2,1,0:T(8,128)(2,1)}, u32[]{:S(2)}, u32[]{:S(2)}) %all-to-all-start.5) | async-done | bytes 2097184 | tf_op jit(solution)/shard_map/all_to_all | solution.py:468
  208.9 3.5 %mix.3 = bf16[128,2048]{1,0:T(8,128)(2,1)} custom-call(f32[128,2048]{1,0:T(8,128)} %mix.2.base_ref, bf16[256,512]{1,0:T(8,128)(2,1)} %gates.3.mix_ref, bf16[512,2048]{1,0:T(8,128)(2,1)} %bitcast.27.rows_ref), custom_call_target="tpu_custom_call" | custom-call | flops 536870912 | bytes 3000000 | tf_op jit(solution)/shard_map/mix/pallas_call | solution.py:501
  (34 shorter events, 5.7 us)
Async XLA Ops:
  0.6 1.3 copy-start
  0.6 24.7 %copy-start.2 = (s32[4]{0:T(128)S(1)}, s32[4]{0:T(128)}, u32[]{:S(2)}) copy-start(s32[4]{0:T(128)} %param.35) | copy-start | bytes 52
  43.5 1.3 copy-start.1
  44.1 19.5 %collective-permute-start.3 = (bf16[4,576,128]{2,1,0:T(8,128)(2,1)S(1)}, bf16[4,576,128]{2,1,0:T(8,128)(2,1)S(1)}, u32[]{:S(2)}, u32[]{:S(2)}) collective-permute-start(bf16[4,576,128]{2,1,0:T(8,128)(2,1)S(1)} %reshape.59.near_ref), channel_id=1, source_target_pairs={{0,1},{1,0},{2,3},{3,2},{4,5},{5,4},{6,7},{7,6},{8,9},{9,8},{10,11... | collective-permute-start | bytes 1769480 | tf_op jit(solution)/shard_map/ppermute | solution.py:349
  49.0 10.2 %collective-permute-start = (bf16[576,128]{1,0:T(8,128)(2,1)}, bf16[576,128]{1,0:T(8,128)(2,1)S(1)}, u32[]{:S(2)}, u32[]{:S(2)}) collective-permute-start(bf16[576,128]{1,0:T(8,128)(2,1)} %get-tuple-element.12.own_ref), channel_id=1, source_target_pairs={{0,1},{1,2},{2,3},{3,0},{4,5},{5,6},{6,7},{7,4},{8,9},{9,10},{10,1... | collective-permute-start | bytes 442376 | tf_op jit(solution)/shard_map/ppermute | solution.py:392
  49.5 9.7 %collective-permute-start.1 = (bf16[576,128]{1,0:T(8,128)(2,1)}, bf16[576,128]{1,0:T(8,128)(2,1)S(1)}, u32[]{:S(2)}, u32[]{:S(2)}) collective-permute-start(bf16[576,128]{1,0:T(8,128)(2,1)} %get-tuple-element.12.own_ref), channel_id=1, source_target_pairs={{0,2},{1,3},{2,0},{3,1},{4,6},{5,7},{6,4},{7,5},{8,10},{9,11},{10,... | collective-permute-start | bytes 442376 | tf_op jit(solution)/shard_map/ppermute | solution.py:392
  50.2 9.1 %collective-permute-start.2 = (bf16[576,128]{1,0:T(8,128)(2,1)}, bf16[576,128]{1,0:T(8,128)(2,1)S(1)}, u32[]{:S(2)}, u32[]{:S(2)}) collective-permute-start(bf16[576,128]{1,0:T(8,128)(2,1)} %get-tuple-element.12.own_ref), channel_id=1, source_target_pairs={{0,3},{1,0},{2,1},{3,2},{4,7},{5,4},{6,5},{7,6},{8,11},{9,8},{10,9... | collective-permute-start | bytes 442376 | tf_op jit(solution)/shard_map/ppermute | solution.py:392
  72.5 34.4 %all-to-all-start.2 = ((bf16[64,8,2048]{2,1,0:T(8,128)(2,1)}), bf16[64,8,2048]{2,1,0:T(8,128)(2,1)S(1)}, u32[]{:S(2)}, u32[]{:S(2)}) async-start(bf16[64,8,2048]{2,1,0:T(8,128)(2,1)} %bitcast.39), calls=%async_computation.2 | async-start | bytes 4194304 | tf_op jit(solution)/shard_map/all_to_all | solution.py:468
  78.4 35.8 %collective-permute-start.4 = (bf16[704,2048]{1,0:T(8,128)(2,1)}, bf16[704,2048]{1,0:T(8,128)(2,1)}, u32[]{:S(2)}, u32[]{:S(2)}) collective-permute-start(bf16[704,2048]{1,0:T(8,128)(2,1)} %bitcast.45), channel_id=1, source_target_pairs={{0,1},{1,0},{2,3},{3,2},{4,5},{5,4},{6,7},{7,6},{8,9},{9,8},{10,11... | collective-permute-start | bytes 8650760 | tf_op jit(solution)/shard_map/ppermute | solution.py:354
  78.5 35.7 %collective-permute-start.5 = (bf16[704,2048]{1,0:T(8,128)(2,1)}, bf16[704,2048]{1,0:T(8,128)(2,1)}, u32[]{:S(2)}, u32[]{:S(2)}) collective-permute-start(bf16[704,2048]{1,0:T(8,128)(2,1)} %bitcast.48), channel_id=1, source_target_pairs={{0,1},{1,0},{2,3},{3,2},{4,5},{5,4},{6,7},{7,6},{8,9},{9,8},{10,11... | collective-permute-start | bytes 8650760 | tf_op jit(solution)/shard_map/ppermute | solution.py:355
  79.0 35.2 %collective-permute-start.6 = (bf16[704,2048]{1,0:T(8,128)(2,1)}, bf16[704,2048]{1,0:T(8,128)(2,1)}, u32[]{:S(2)}, u32[]{:S(2)}) collective-permute-start(bf16[704,2048]{1,0:T(8,128)(2,1)} %bitcast.51), channel_id=1, source_target_pairs={{0,1},{1,0},{2,3},{3,2},{4,5},{5,4},{6,7},{7,6},{8,9},{9,8},{10,11... | collective-permute-start | bytes 8650760 | tf_op jit(solution)/shard_map/ppermute | solution.py:356
  106.9 34.5 %all-to-all-start.4 = ((bf16[64,8,2048]{2,1,0:T(8,128)(2,1)}), bf16[64,8,2048]{2,1,0:T(8,128)(2,1)}, u32[]{:S(2)}, u32[]{:S(2)}) async-start(bf16[64,8,2048]{2,1,0:T(8,128)(2,1)} %bitcast.35), calls=%async_computation.4 | async-start | bytes 4194304 | tf_op jit(solution)/shard_map/all_to_all | solution.py:468
  141.4 33.9 %all-to-all-start.3 = ((bf16[64,8,2048]{2,1,0:T(8,128)(2,1)}), bf16[64,8,2048]{2,1,0:T(8,128)(2,1)S(1)}, u32[]{:S(2)}, u32[]{:S(2)}) async-start(bf16[64,8,2048]{2,1,0:T(8,128)(2,1)} %bitcast.41), calls=%async_computation.3 | async-start | bytes 4194304 | tf_op jit(solution)/shard_map/all_to_all | solution.py:468
  175.3 33.7 %all-to-all-start.5 = ((bf16[64,8,2048]{2,1,0:T(8,128)(2,1)}), bf16[64,8,2048]{2,1,0:T(8,128)(2,1)}, u32[]{:S(2)}, u32[]{:S(2)}) async-start(bf16[64,8,2048]{2,1,0:T(8,128)(2,1)} %bitcast.40), calls=%async_computation.5 | async-start | bytes 4194304 | tf_op jit(solution)/shard_map/all_to_all | solution.py:468

commit v5 on v4

--- a/solution.py
+++ b/solution.py
@@ -36,6 +36,22 @@
     end_0 = lengths_ref[0, 0]
     end_1 = end_0 + lengths_ref[0, 1]
     return jnp.where(pos >= end_1, end_1, jnp.where(pos >= end_0, end_0, 0))
+
+
+def pack_kernel(sub_ref, tag_ref, pool_hbm, out_ref, quarter, sem):
+    width, quarter_len = quarter.shape
+    count, held, lanes = out_ref.shape
+    start = pl.multiple_of(sub_ref[0] * quarter_len, quarter_len)
+    copy = pltpu.make_async_copy(pool_hbm.at[:, pl.ds(start, quarter_len)], quarter, sem)
+    copy.start()
+    piece = width * quarter_len // lanes // count
+    tag = jnp.full((held - piece, lanes), tag_ref[0].astype(F32), F32)
+    copy.wait()
+    rows = jnp.concatenate(
+        [quarter[:, i * lanes : (i + 1) * lanes] for i in range(quarter_len // lanes)], axis=0
+    ).astype(F32)
+    for j in range(count):
+        out_ref[j] = jnp.concatenate([rows[j * piece : (j + 1) * piece], tag], axis=0).astype(BF16)
 
 
 def spread_matrix(part_slots, experts):
@@ -78,7 +94,7 @@
 
 
 def cache_kernel(
-    lengths_ref, sub_ref, tokens_ref, gain_ref, wl_ref, lgain_ref, inverse_ref,
+    prefix_len, lengths_ref, sub_ref, tokens_ref, gain_ref, wl_ref, lgain_ref, inverse_ref,
     cache_ref, normed_ref, angle_ref,
 ):
     rows = tokens_ref.shape[0]
@@ -89,7 +105,7 @@
     normed = (x * scale * gain_ref[...]).astype(BF16)
     normed_ref[...] = normed
     pos = sub_ref[0] * rows + iota((half, rows), 1)
-    offset = sub_ref[1] + pos - seg_starts(lengths_ref, pos)
+    offset = prefix_len + pos - seg_starts(lengths_ref, pos)
     angles = offset.astype(F32) * inverse_ref[...]
     cos_part = jnp.cos(angles)
     sin_part = jnp.sin(angles)
@@ -105,10 +121,30 @@
     cache_ref[lat + half :] = (second * cos_part + first * sin_part).astype(BF16)
 
 
-def query_kernel(normed_ref, angle_ref, wq_ref, wk_ref, query_ref):
+def query_kernel(
+    score_scale, lengths_ref, sub_ref, normed_ref, angle_ref, wq_ref, wk_ref,
+    own_ref, back_1_ref, back_2_ref, back_3_ref,
+    query_ref, weighted_ref, stats_ref, keys, mask,
+):
     heads, nope, lat = wk_ref.shape
-    rope = angle_ref.shape[1]
+    rows, rope = angle_ref.shape
     half = rope // 2
+    count = heads * rows
+
+    @pl.when(pl.program_id(0) == 0)
+    def _():
+        suffix = (own_ref, back_1_ref, back_2_ref, back_3_ref)
+        pos = sub_ref[0] * rows + iota((rows, rows), 0)
+        start = seg_starts(lengths_ref, pos)
+        for d, ref in enumerate(suffix):
+            at = slice(d * rows, (d + 1) * rows)
+            keys[:, at] = ref[...]
+            key_pos = ((sub_ref[0] + len(suffix) - d) % len(suffix)) * rows + iota((rows, rows), 1)
+            allowed = (key_pos >= start) & (key_pos <= pos)
+            floor = jnp.where(allowed, 0.0, FLOOR_SCORE)
+            for h in range(heads):
+                mask[h * rows : (h + 1) * rows, at] = floor
+
     queries = dot(normed_ref[...], wq_ref[...]).astype(BF16)
     cos_part = angle_ref[:, :half]
     sin_part = angle_ref[:, half:]
@@ -120,44 +156,15 @@
         query_ref[h, :, lat:] = jnp.concatenate(
             [first * cos_part - second * sin_part, second * cos_part + first * sin_part], axis=1
         ).astype(BF16)
+    scores = dot(query_ref[...].reshape(count, lat + rope), keys[...]) + mask[...]
+    row_top = jnp.max(scores, axis=1, keepdims=True)
+    weights = jnp.exp2((scores - row_top) * score_scale)
+    denominator = jnp.sum(weights, axis=1, keepdims=True)
+    weighted_ref[...] = dot_nt(weights.astype(BF16), keys[:lat])
+    stats_ref[...] = jnp.where(iota(stats_ref.shape, 1) == 0, row_top, denominator)
 
 
 PAIR = 2
-
-
-def late_kernel(
-    score_scale, lengths_ref, sub_ref, query_ref, own_ref, back_1_ref, back_2_ref, back_3_ref,
-    weighted_ref, stats_ref, keys, bias,
-):
-    heads, rows, width = query_ref.shape
-    lat = weighted_ref.shape[1]
-    suffix = (own_ref, back_1_ref, back_2_ref, back_3_ref)
-    pos = sub_ref[0] * rows + iota((rows, rows), 0)
-    start = seg_starts(lengths_ref, pos)
-    for d, ref in enumerate(suffix):
-        at = slice(d * rows, (d + 1) * rows)
-        keys[:, at] = ref[...]
-        key_pos = ((sub_ref[0] + len(suffix) - d) % len(suffix)) * rows + iota((rows, rows), 1)
-        allowed = (key_pos >= start) & (key_pos <= pos)
-        bias[:, at] = jnp.where(allowed, 0.0, FLOOR_SCORE)
-    mask = jnp.concatenate([bias[...]] * PAIR, axis=0)
-    count = PAIR * rows
-    lane = iota((count, stats_ref.shape[1]), 1)
-
-    def score(i):
-        query = query_ref[i * PAIR : (i + 1) * PAIR].reshape(count, width)
-        return dot(query, keys[...]) + mask
-
-    current = score(0)
-    for i in range(heads // PAIR):
-        following = score(i + 1) if i + 1 < heads // PAIR else None
-        at = slice(i * count, (i + 1) * count)
-        row_top = jnp.max(current, axis=1, keepdims=True)
-        weights = jnp.exp2((current - row_top) * score_scale)
-        denominator = jnp.sum(weights, axis=1, keepdims=True)
-        weighted_ref[at] = dot_nt(weights.astype(BF16), keys[:lat])
-        stats_ref[at] = jnp.where(lane == 0, row_top, denominator)
-        current = following
 
 
 def attend_kernel(
@@ -318,20 +325,21 @@
     sub_count = lax.axis_size("ylo") * core_count
     chips = req_count * lax.axis_size("ylo")
     sub = lax.axis_index("ylo") * core_count + lax.axis_index("core")
-    place_info = jnp.stack([sub, jnp.int32(prefix_len)]).astype(jnp.int32)
+    place_info = jnp.reshape(sub, (1,)).astype(jnp.int32)
 
     quarter_len = prefix_len // sub_count
-    quarter = lax.dynamic_slice(prefix_pool[0].T, (0, sub * quarter_len), (width, quarter_len))
     lanes = 128
     piece = width * quarter_len // lanes // req_count
-    pieces = (
-        quarter.reshape(width, quarter_len // lanes, lanes).transpose(1, 0, 2)
-        .reshape(req_count, piece, lanes)
-    )
-    tag_rows = -piece % 8 or 8
-    tag = jnp.broadcast_to(slab_group[0].astype(BF16), (req_count, tag_rows, lanes))
+    packed = pl.pallas_call(
+        pack_kernel,
+        name="pack",
+        in_specs=[SMEM, SMEM, HBM],
+        out_specs=VMEM,
+        out_shape=pltpu.HBM((req_count, piece + (-piece % 8 or 8), lanes), BF16),
+        scratch_shapes=[pltpu.VMEM((width, quarter_len), BF16), pltpu.SemaphoreType.DMA],
+    )(place_info, slab_group, prefix_pool[0].T)
     spread = lax.all_to_all(
-        jnp.concatenate([pieces, tag], axis=1), "req", split_axis=0, concat_axis=0, tiled=True
+        packed, "req", split_axis=0, concat_axis=0, tiled=True
     )
     ylo_count = lax.axis_size("ylo")
     groups = spread[:, piece, 0].astype(jnp.int32)
@@ -358,12 +366,12 @@
     pair = 2
     steps = head_count // pair
     inverse = (10000.0 ** (-np.arange(rope // 2) / (rope // 2))).astype(np.float32)
-    inverse = jnp.broadcast_to(jnp.asarray(inverse)[:, None], (rope // 2, rows))
+    inverse = jnp.asarray(np.ascontiguousarray(np.broadcast_to(inverse[:, None], (rope // 2, rows))))
     w_latent_t = w_latent.T
     gain_row = attn_gain[None, :]
     lgain_row = latent_gain[None, :]
     cache_t, normed, angle = pl.pallas_call(
-        cache_kernel,
+        functools.partial(cache_kernel, prefix_len),
         name="cache",
         in_specs=[SMEM, SMEM] + [VMEM] * 5,
         out_specs=[VMEM, VMEM, VMEM],
@@ -374,24 +382,42 @@
         ],
         cost_estimate=cost(2 * rows * model * width, 4e6),
     )(lengths, place_info, tokens, gain_row, w_latent_t, lgain_row, inverse)
-    query_full = pl.pallas_call(
-        query_kernel,
-        name="query",
-        grid=(steps,),
-        in_specs=[
-            whole(normed), whole(angle),
-            pl.BlockSpec((model, pair * (nope + rope)), lambda i: (0, i)),
-            pl.BlockSpec((pair, nope, lat), lambda i: (i, 0, 0)),
-        ],
-        out_specs=pl.BlockSpec((pair, rows, width), lambda i: (i, 0, 0)),
-        out_shape=pltpu.HBM((head_count, rows, width), BF16),
-        cost_estimate=cost(2 * rows * model * w_query.shape[1], 9e6),
-    )(normed, angle, w_query, w_key_up)
-
     back = [
         lax.ppermute(cache_t, ("ylo", "core"), [(k, (k + d) % sub_count) for k in range(sub_count)])
         for d in range(1, sub_count)
     ]
+
+    score_scale = (nope + rope) ** (-0.5) * math.log2(math.e)
+    lines = head_count * rows
+    query_full, late, stats = pl.pallas_call(
+        functools.partial(query_kernel, score_scale),
+        name="query",
+        grid=(steps,),
+        in_specs=[
+            SMEM, SMEM, whole(normed), whole(angle),
+            pl.BlockSpec((model, pair * (nope + rope)), lambda i: (0, i)),
+            pl.BlockSpec((pair, nope, lat), lambda i: (i, 0, 0)),
+            VMEM, VMEM, VMEM, VMEM,
+        ],
+        out_specs=[
+            pl.BlockSpec((pair, rows, width), lambda i: (i, 0, 0)),
+            pl.BlockSpec((pair * rows, lat), lambda i: (i, 0)),
+            pl.BlockSpec((pair * rows, 128), lambda i: (i, 0)),
+        ],
+        out_shape=[
+            pltpu.HBM((head_count, rows, width), BF16),
+            pltpu.HBM((lines, lat), F32),
+            pltpu.HBM((lines, 128), F32),
+        ],
+        scratch_shapes=[
+            pltpu.VMEM((width, rows * sub_count), BF16),
+            pltpu.VMEM((pair * rows, rows * sub_count), F32),
+        ],
+        compiler_params=limit(54),
+        cost_estimate=cost(3e9, 12e6),
+    )(
+        lengths, place_info, normed, angle, w_query, w_key_up, cache_t, *map(near_core, back),
+    )
 
     slot_count = 4 * rows * top // 3
     part_slots = slot_count // PARTS
@@ -418,20 +444,6 @@
         )(ids_t, gates_t, placing))
 
     moe_row = moe_gain[None, :]
-    score_scale = (nope + rope) ** (-0.5) * math.log2(math.e)
-    lines = head_count * rows
-    late, stats = pl.pallas_call(
-        functools.partial(late_kernel, score_scale),
-        name="late",
-        in_specs=[SMEM, SMEM] + [VMEM] * 5,
-        out_specs=[VMEM, VMEM],
-        out_shape=[pltpu.HBM((lines, lat), F32), pltpu.HBM((lines, 128), F32)],
-        scratch_shapes=[
-            pltpu.VMEM((width, rows * sub_count), BF16), pltpu.VMEM((rows, rows * sub_count), F32),
-        ],
-        compiler_params=limit(54),
-        cost_estimate=cost(1e9, 6e6),
-    )(lengths, place_info, query_full, cache_t, *map(near_core, back))
     residual, mid, first_out = pl.pallas_call(
         functools.partial(attend_kernel, score_scale),
         name="attend",

time: 213 us -> 217 us (1.019)
  waiting for transfers between devices: 68.7 us -> 75.6 us
  local copies, waits for them, and re-layouts: 3.69 us -> 1.05 us
    ppermute x3, waiting for transfers between devices: 0.01 us -> 3.96 us  [layer(): lax.ppermute(cache_t, ('ylo', 'core'), [(k, (k + d) % sub_count) for k in...]
    all_to_all x4, waiting for transfers between devices: 68.7 us -> 71.7 us  [exchange(): x = lax.all_to_all(x, CHIP, split_axis=0, concat_axis=0, tiled=True)]
  transfers between devices with their start and end apart: 11 -> 11, of which waited for: 4 -> 7; matrix products, arithmetic and copies ran while one was open for 1% -> 0% of each run, Pallas kernels for 27% -> 26%
where the time goes in v5:
time: 217 us; the launch traced here: 216 us
  waiting for transfers between devices  75.6 us (35%)
  Pallas kernels  69.3 us (32%)
  blocking collectives  39.2 us (18%)
  starting transfers between devices  28.8 us (13%)
    all_to_all x4, waiting for transfers between devices, exchange(): x = lax.all_to_all(x, CHIP, split_axis=0, concat_axis=0, tiled=True)  71.7 us
    pallas_call x2, Pallas kernels, experts(): pl.pallas_call(expert_kernel, name='experts', in_specs=[VMEM] + [HBM] * 6...  31.6 us
    all_to_all x4, starting transfers between devices, exchange(): x = lax.all_to_all(x, CHIP, split_axis=0, concat_axis=0, tiled=True)  24.7 us
    all_to_all x1, blocking collectives, layer(): lax.all_to_all(packed, 'req', split_axis=0, concat_axis=0, tiled=True)  22.1 us
    all_to_all x1, blocking collectives, layer(): near = lax.all_to_all(picked, CHIP, split_axis=0, concat_axis=0, tiled=True)  17.1 us
    pallas_call x1, Pallas kernels, layer(): pl.pallas_call(functools.partial(attend_kernel, score_scale), name='atten...  8.86 us
    pallas_call x1, Pallas kernels, layer(): pl.pallas_call(functools.partial(query_kernel, score_scale), name='query'...  8.41 us
    pallas_call x2, Pallas kernels, mix(): pl.pallas_call(mix_kernel, name='mix', in_specs=[VMEM] * 3, out_specs=VME...  6.46 us
  transfers between devices with their start and end apart: 11, of which 7 were waited for; matrix products, arithmetic and copies ran while one was open for 0% of the time, Pallas kernels for 26%

profile of v5, /device:TPU:0, one launch (start us, length us, event | category | flops | bytes accessed | tf_op | source)
XLA Modules:
  0.0 216.2 jit_solution(10936926379674007946)
XLA Ops:
  1.3 1.7 pack.1
  3.1 22.1 %all_to_all.30 = bf16[32,40,128]{2,1,0:T(8,128)(2,1)S(1)} all-to-all(bf16[32,40,128]{2,1,0:T(8,128)(2,1)} %pack.1), channel_id=1, replica_groups=mesh['req'=32,'ylo'=2,'core'=2] {'req'}, dimensions={0} | all-to-all | bytes 655360 | tf_op jit(solution)/shard_map/all_to_all | solution.py:341
  26.8 17.1 %all_to_all.31 = bf16[64,40,128]{2,1,0:T(8,128)(2,1)S(1)} all-to-all(bf16[64,40,128]{2,1,0:T(8,128)(2,1)S(1)} %gather_fusion), channel_id=1, replica_groups=mesh['req'=32,'ylo'=2,'core'=2] {'req','ylo'}, dimensions={0} | all-to-all | bytes 1310720 | tf_op jit(solution)/shard_map/all_to_all | solution.py:353
  44.2 3.5 %cache.1 = (bf16[576,128]{1,0:T(8,128)(2,1)}, bf16[128,2048]{1,0:T(8,128)(2,1)}, f32[128,64]{1,0:T(8,128)}) custom-call(s32[1,3]{1,0:T(1,128)} %lengths_ref.3, s32[1]{0:T(128)} %bitcast.sub_ref, bf16[128,2048]{1,0:T(8,128)(2,1)} %tokens_hbm.1, f32[1,2048]{1,0:T(1,128)} %bitcast.41, bf16[576,2048]{1,0:T(8,128)(2,1)} %bitcast.36, f32[1,512]{1,0:T(1,128)} %bitcast.42, ...), custom_call_target="tpu_custom_call" | custom-call | flops 301989888 | bytes 4000000 | tf_op jit(solution)/shard_map/cache/pallas_call | solution.py:373
  49.9 1.7 route.1.place_hbm.place_ref
  51.6 1.4 collective-permute-done.back_1_ref
  53.0 2.1 collective-permute-done.1.back_2_ref
  55.5 8.4 %query.1 = (bf16[8,128,576]{2,1,0:T(8,128)(2,1)}, f32[1024,512]{1,0:T(8,128)}, f32[1024,128]{1,0:T(8,128)}) custom-call(s32[1,3]{1,0:T(1,128)} %lengths_ref.3, s32[1]{0:T(128)} %bitcast.sub_ref, bf16[128,2048]{1,0:T(8,128)(2,1)} %get-tuple-element.11.normed_ref, f32[128,64]{1,0:T(8,128)} %get-tuple-element.12.angle_ref, bf16[2048,1536]{1,0:T(8,128)(2,1)} %wq_ref.1, ...), custom_call_target="tpu_custom_call" | custom-call | flops 3000000000 | bytes 12000000 | tf_op jit(solution)/shard_map/query/pallas_call | solution.py:392
  63.9 8.9 %attend.1 = (f32[128,2048]{1,0:T(8,128)}, bf16[128,2048]{1,0:T(8,128)(2,1)}, bf16[512,2048]{1,0:T(8,128)(2,1)}) custom-call(bf16[8,128,576]{2,1,0:T(8,128)(2,1)} %get-tuple-element.14.query_hbm, f32[1024,512]{1,0:T(8,128)} %get-tuple-element.15.late_hbm, f32[1024,128]{1,0:T(8,128)} %get-tuple-element.16.stats_hbm, ...), custom_call_target="tpu_custom_call" | custom-call | flops 5000000000 | bytes 6000000 | tf_op jit(solution)/shard_map/attend/pallas_call | solution.py:447
  72.8 5.8 %all-to-all-start.2 = ((bf16[64,8,2048]{2,1,0:T(8,128)(2,1)}), bf16[64,8,2048]{2,1,0:T(8,128)(2,1)S(1)}, u32[]{:S(2)}, u32[]{:S(2)}) async-start(bf16[64,8,2048]{2,1,0:T(8,128)(2,1)} %bitcast.37), calls=%async_computation.2 | async-start | bytes 4194304 | tf_op jit(solution)/shard_map/all_to_all | solution.py:480
  80.6 2.9 %place.1 = bf16[512,2048]{1,0:T(8,128)(2,1)} custom-call(bf16[2,512,128]{2,1,0:T(8,128)(2,1)} %route.1.place_hbm.place_ref, bf16[128,2048]{1,0:T(8,128)(2,1)} %get-tuple-element.19.mid_ref), custom_call_target="tpu_custom_call" | custom-call | flops 268435456 | bytes 3000000 | tf_op jit(solution)/shard_map/place/pallas_call | solution.py:484
  83.5 26.0 %all-to-all-done.2 = bf16[64,8,2048]{2,1,0:T(8,128)(2,1)S(1)} async-done(((bf16[64,8,2048]{2,1,0:T(8,128)(2,1)}), bf16[64,8,2048]{2,1,0:T(8,128)(2,1)S(1)}, u32[]{:S(2)}, u32[]{:S(2)}) %all-to-all-start.2) | async-done | bytes 2097184 | tf_op jit(solution)/shard_map/all_to_all | solution.py:480
  109.5 6.1 %all-to-all-start.4 = ((bf16[64,8,2048]{2,1,0:T(8,128)(2,1)}), bf16[64,8,2048]{2,1,0:T(8,128)(2,1)}, u32[]{:S(2)}, u32[]{:S(2)}) async-start(bf16[64,8,2048]{2,1,0:T(8,128)(2,1)} %bitcast.33), calls=%async_computation.4 | async-start | bytes 4194304 | tf_op jit(solution)/shard_map/all_to_all | solution.py:480
  115.6 15.0 %experts.2 = bf16[512,2048]{1,0:T(8,128)(2,1)} custom-call(bf16[512,2048]{1,0:T(8,128)(2,1)S(1)} %bitcast.32, bf16[704,2048]{1,0:T(8,128)(2,1)} %bitcast.44, bf16[704,2048]{1,0:T(8,128)(2,1)} %bitcast.47, bf16[704,2048]{1,0:T(8,128)(2,1)} %bitcast.50, bf16[704,2048]{1,0:T(8,128)(2,1)} %collective-permute-done.4.g1, ...), custom_call_target="tpu_custom_call" | custom-call | flops 8858370048 | bytes 21000000 | tf_op jit(solution)/shard_map/experts/pallas_call | solution.py:497
  130.6 14.1 %all-to-all-done.4 = bf16[64,8,2048]{2,1,0:T(8,128)(2,1)} async-done(((bf16[64,8,2048]{2,1,0:T(8,128)(2,1)}), bf16[64,8,2048]{2,1,0:T(8,128)(2,1)}, u32[]{:S(2)}, u32[]{:S(2)}) %all-to-all-start.4) | async-done | bytes 2097184 | tf_op jit(solution)/shard_map/all_to_all | solution.py:480
  144.6 6.1 %all-to-all-start.3 = ((bf16[64,8,2048]{2,1,0:T(8,128)(2,1)}), bf16[64,8,2048]{2,1,0:T(8,128)(2,1)S(1)}, u32[]{:S(2)}, u32[]{:S(2)}) async-start(bf16[64,8,2048]{2,1,0:T(8,128)(2,1)} %bitcast.39), calls=%async_computation.3 | async-start | bytes 4194304 | tf_op jit(solution)/shard_map/all_to_all | solution.py:480
  150.8 16.6 %experts.3 = bf16[512,2048]{1,0:T(8,128)(2,1)} custom-call(bf16[512,2048]{1,0:T(8,128)(2,1)} %bitcast.23.x_ref, bf16[704,2048]{1,0:T(8,128)(2,1)} %bitcast.45, bf16[704,2048]{1,0:T(8,128)(2,1)} %bitcast.48, bf16[704,2048]{1,0:T(8,128)(2,1)} %bitcast.51, bf16[704,2048]{1,0:T(8,128)(2,1)} %collective-permute-done.4.g1, ...), custom_call_target="tpu_custom_call" | custom-call | flops 8858370048 | bytes 21000000 | tf_op jit(solution)/shard_map/experts/pallas_call | solution.py:497
  167.4 11.5 %all-to-all-done.3 = bf16[64,8,2048]{2,1,0:T(8,128)(2,1)S(1)} async-done(((bf16[64,8,2048]{2,1,0:T(8,128)(2,1)}), bf16[64,8,2048]{2,1,0:T(8,128)(2,1)S(1)}, u32[]{:S(2)}, u32[]{:S(2)}) %all-to-all-start.3) | async-done | bytes 2097184 | tf_op jit(solution)/shard_map/all_to_all | solution.py:480
  178.9 6.6 %all-to-all-start.5 = ((bf16[64,8,2048]{2,1,0:T(8,128)(2,1)}), bf16[64,8,2048]{2,1,0:T(8,128)(2,1)}, u32[]{:S(2)}, u32[]{:S(2)}) async-start(bf16[64,8,2048]{2,1,0:T(8,128)(2,1)} %bitcast.38), calls=%async_computation.5 | async-start | bytes 4194304 | tf_op jit(solution)/shard_map/all_to_all | solution.py:480
  185.5 2.0 gates.2.mix_ref
  187.6 2.0 gates.3.mix_ref
  189.6 2.9 %mix.2.base_ref = f32[128,2048]{1,0:T(8,128)} custom-call(f32[128,2048]{1,0:T(8,128)} %get-tuple-element.17.base_ref, bf16[256,512]{1,0:T(8,128)(2,1)} %gates.2.mix_ref, bf16[512,2048]{1,0:T(8,128)(2,1)S(1)} %bitcast.31), custom_call_target="tpu_custom_call" | custom-call | flops 536870912 | bytes 3000000 | tf_op jit(solution)/shard_map/mix/pallas_call | solution.py:513
  192.6 20.1 %all-to-all-done.5 = bf16[64,8,2048]{2,1,0:T(8,128)(2,1)} async-done(((bf16[64,8,2048]{2,1,0:T(8,128)(2,1)}), bf16[64,8,2048]{2,1,0:T(8,128)(2,1)}, u32[]{:S(2)}, u32[]{:S(2)}) %all-to-all-start.5) | async-done | bytes 2097184 | tf_op jit(solution)/shard_map/all_to_all | solution.py:480
  212.6 3.5 %mix.3 = bf16[128,2048]{1,0:T(8,128)(2,1)} custom-call(f32[128,2048]{1,0:T(8,128)} %mix.2.base_ref, bf16[256,512]{1,0:T(8,128)(2,1)} %gates.3.mix_ref, bf16[512,2048]{1,0:T(8,128)(2,1)} %bitcast.25.rows_ref), custom_call_target="tpu_custom_call" | custom-call | flops 536870912 | bytes 3000000 | tf_op jit(solution)/shard_map/mix/pallas_call | solution.py:513
  (22 shorter events, 6.3 us)
Async XLA Ops:
  0.6 25.2 %copy-start = (s32[4]{0:T(128)S(1)}, s32[4]{0:T(128)}, u32[]{:S(2)}) copy-start(s32[4]{0:T(128)} %param.35) | copy-start | bytes 52
  44.1 19.8 %collective-permute-start.3 = (bf16[4,576,128]{2,1,0:T(8,128)(2,1)S(1)}, bf16[4,576,128]{2,1,0:T(8,128)(2,1)S(1)}, u32[]{:S(2)}, u32[]{:S(2)}) collective-permute-start(bf16[4,576,128]{2,1,0:T(8,128)(2,1)S(1)} %reshape.49.near_ref), channel_id=1, source_target_pairs={{0,1},{1,0},{2,3},{3,2},{4,5},{5,4},{6,7},{7,6},{8,9},{9,8},{10,11... | collective-permute-start | bytes 1769480 | tf_op jit(solution)/shard_map/ppermute | solution.py:357
  47.7 5.3 %collective-permute-start = (bf16[576,128]{1,0:T(8,128)(2,1)}, bf16[576,128]{1,0:T(8,128)(2,1)S(1)}, u32[]{:S(2)}, u32[]{:S(2)}) collective-permute-start(bf16[576,128]{1,0:T(8,128)(2,1)} %get-tuple-element.13.own_ref), channel_id=1, source_target_pairs={{0,1},{1,2},{2,3},{3,0},{4,5},{5,6},{6,7},{7,4},{8,9},{9,10},{10,1... | collective-permute-start | bytes 442376 | tf_op jit(solution)/shard_map/ppermute | solution.py:386
  48.2 6.9 %collective-permute-start.1 = (bf16[576,128]{1,0:T(8,128)(2,1)}, bf16[576,128]{1,0:T(8,128)(2,1)S(1)}, u32[]{:S(2)}, u32[]{:S(2)}) collective-permute-start(bf16[576,128]{1,0:T(8,128)(2,1)} %get-tuple-element.13.own_ref), channel_id=1, source_target_pairs={{0,2},{1,3},{2,0},{3,1},{4,6},{5,7},{6,4},{7,5},{8,10},{9,11},{10,... | collective-permute-start | bytes 442376 | tf_op jit(solution)/shard_map/ppermute | solution.py:386
  48.9 6.7 %collective-permute-start.2 = (bf16[576,128]{1,0:T(8,128)(2,1)}, bf16[576,128]{1,0:T(8,128)(2,1)S(1)}, u32[]{:S(2)}, u32[]{:S(2)}) collective-permute-start(bf16[576,128]{1,0:T(8,128)(2,1)} %get-tuple-element.13.own_ref), channel_id=1, source_target_pairs={{0,3},{1,0},{2,1},{3,2},{4,7},{5,4},{6,5},{7,6},{8,11},{9,8},{10,9... | collective-permute-start | bytes 442376 | tf_op jit(solution)/shard_map/ppermute | solution.py:386
  72.8 36.7 %all-to-all-start.2 = ((bf16[64,8,2048]{2,1,0:T(8,128)(2,1)}), bf16[64,8,2048]{2,1,0:T(8,128)(2,1)S(1)}, u32[]{:S(2)}, u32[]{:S(2)}) async-start(bf16[64,8,2048]{2,1,0:T(8,128)(2,1)} %bitcast.37), calls=%async_computation.2 | async-start | bytes 4194304 | tf_op jit(solution)/shard_map/all_to_all | solution.py:480
  78.7 36.9 %collective-permute-start.4 = (bf16[704,2048]{1,0:T(8,128)(2,1)}, bf16[704,2048]{1,0:T(8,128)(2,1)}, u32[]{:S(2)}, u32[]{:S(2)}) collective-permute-start(bf16[704,2048]{1,0:T(8,128)(2,1)} %bitcast.43), channel_id=1, source_target_pairs={{0,1},{1,0},{2,3},{3,2},{4,5},{5,4},{6,7},{7,6},{8,9},{9,8},{10,11... | collective-permute-start | bytes 8650760 | tf_op jit(solution)/shard_map/ppermute | solution.py:362
  80.1 35.5 %collective-permute-start.5 = (bf16[704,2048]{1,0:T(8,128)(2,1)}, bf16[704,2048]{1,0:T(8,128)(2,1)}, u32[]{:S(2)}, u32[]{:S(2)}) collective-permute-start(bf16[704,2048]{1,0:T(8,128)(2,1)} %bitcast.46), channel_id=1, source_target_pairs={{0,1},{1,0},{2,3},{3,2},{4,5},{5,4},{6,7},{7,6},{8,9},{9,8},{10,11... | collective-permute-start | bytes 8650760 | tf_op jit(solution)/shard_map/ppermute | solution.py:363
  80.2 35.4 %collective-permute-start.6 = (bf16[704,2048]{1,0:T(8,128)(2,1)}, bf16[704,2048]{1,0:T(8,128)(2,1)}, u32[]{:S(2)}, u32[]{:S(2)}) collective-permute-start(bf16[704,2048]{1,0:T(8,128)(2,1)} %bitcast.49), channel_id=1, source_target_pairs={{0,1},{1,0},{2,3},{3,2},{4,5},{5,4},{6,7},{7,6},{8,9},{9,8},{10,11... | collective-permute-start | bytes 8650760 | tf_op jit(solution)/shard_map/ppermute | solution.py:364
  109.5 35.1 %all-to-all-start.4 = ((bf16[64,8,2048]{2,1,0:T(8,128)(2,1)}), bf16[64,8,2048]{2,1,0:T(8,128)(2,1)}, u32[]{:S(2)}, u32[]{:S(2)}) async-start(bf16[64,8,2048]{2,1,0:T(8,128)(2,1)} %bitcast.33), calls=%async_computation.4 | async-start | bytes 4194304 | tf_op jit(solution)/shard_map/all_to_all | solution.py:480
  144.6 34.3 %all-to-all-start.3 = ((bf16[64,8,2048]{2,1,0:T(8,128)(2,1)}), bf16[64,8,2048]{2,1,0:T(8,128)(2,1)S(1)}, u32[]{:S(2)}, u32[]{:S(2)}) async-start(bf16[64,8,2048]{2,1,0:T(8,128)(2,1)} %bitcast.39), calls=%async_computation.3 | async-start | bytes 4194304 | tf_op jit(solution)/shard_map/all_to_all | solution.py:480
  178.9 33.7 %all-to-all-start.5 = ((bf16[64,8,2048]{2,1,0:T(8,128)(2,1)}), bf16[64,8,2048]{2,1,0:T(8,128)(2,1)}, u32[]{:S(2)}, u32[]{:S(2)}) async-start(bf16[64,8,2048]{2,1,0:T(8,128)(2,1)} %bitcast.38), calls=%async_computation.5 | async-start | bytes 4194304 | tf_op jit(solution)/shard_map/all_to_all | solution.py:480

commit v6 on v5

--- a/solution.py
+++ b/solution.py
@@ -94,9 +94,11 @@
 
 
 def cache_kernel(
-    prefix_len, lengths_ref, sub_ref, tokens_ref, gain_ref, wl_ref, lgain_ref, inverse_ref,
-    cache_ref, normed_ref, angle_ref,
+    prefix_len, lengths_ref, sub_ref, tokens_ref, gain_ref, wl_hbm, lgain_ref, inverse_ref,
+    cache_ref, normed_ref, angle_ref, wl_ref, sem,
 ):
+    copy = pltpu.make_async_copy(wl_hbm, wl_ref, sem)
+    copy.start()
     rows = tokens_ref.shape[0]
     lat = lgain_ref.shape[1]
     half = (wl_ref.shape[0] - lat) // 2
@@ -110,6 +112,7 @@
     cos_part = jnp.cos(angles)
     sin_part = jnp.sin(angles)
     angle_ref[...] = jnp.concatenate([cos_part, sin_part], axis=0).T
+    copy.wait()
     latent = dot_nt(wl_ref[...], normed)
     low = latent[:lat]
     scale = lax.rsqrt(jnp.mean(low * low, axis=0, keepdims=True) + EPSILON)
@@ -282,10 +285,27 @@
         out_ref[at] = (total + dot(activated[1, at], buf[5])).astype(BF16)
 
 
-def mix_kernel(base_ref, mix_ref, rows_ref, out_ref):
-    rows = base_ref.shape[0]
-    both = dot(mix_ref[...], rows_ref[...])
-    out_ref[...] = (base_ref[...] + (both[:rows] + both[rows:])).astype(out_ref.dtype)
+def mix_kernel(base_hbm, mix_hbm, rows_ref, out_hbm, base_ref, mix_ref, out_ref, sems):
+    rows, model = base_ref.shape
+    mix_copy = pltpu.make_async_copy(mix_hbm, mix_ref, sems.at[0])
+    base_copy = pltpu.make_async_copy(base_hbm, base_ref, sems.at[1])
+    mix_copy.start()
+    base_copy.start()
+    blocks = 4
+    writes = []
+    mix_copy.wait()
+    for i in range(blocks):
+        at = slice(i * model // blocks, (i + 1) * model // blocks)
+        both = dot(mix_ref[...], rows_ref[:, at])
+        if i == 0:
+            base_copy.wait()
+        out_ref[:, at] = (base_ref[:, at] + (both[:rows] + both[rows:])).astype(out_ref.dtype)
+        writes.append(
+            pltpu.make_async_copy(out_ref.at[:, at], out_hbm.at[:, at], sems.at[2 + i])
+        )
+        writes[-1].start()
+    for write in writes:
+        write.wait()
 
 
 def cost(flops, moved):
@@ -373,13 +393,14 @@
     cache_t, normed, angle = pl.pallas_call(
         functools.partial(cache_kernel, prefix_len),
         name="cache",
-        in_specs=[SMEM, SMEM] + [VMEM] * 5,
+        in_specs=[SMEM, SMEM, VMEM, VMEM, HBM, VMEM, VMEM],
         out_specs=[VMEM, VMEM, VMEM],
         out_shape=[
             pltpu.HBM((width, rows), BF16),
             pltpu.HBM((rows, model), BF16),
             pltpu.HBM((rows, rope), F32),
         ],
+        scratch_shapes=[pltpu.VMEM((width, model), BF16), pltpu.SemaphoreType.DMA],
         cost_estimate=cost(2 * rows * model * width, 4e6),
     )(lengths, place_info, tokens, gain_row, w_latent_t, lgain_row, inverse)
     back = [
@@ -513,9 +534,13 @@
         return pl.pallas_call(
             mix_kernel,
             name="mix",
-            in_specs=[VMEM] * 3,
-            out_specs=VMEM,
+            in_specs=[HBM, HBM, VMEM],
+            out_specs=HBM,
             out_shape=pltpu.HBM(shape, BF16 if last else F32),
+            scratch_shapes=[
+                pltpu.VMEM(shape, F32), pltpu.VMEM((2 * rows, part_slots), BF16),
+                pltpu.VMEM(shape, BF16 if last else F32), pltpu.SemaphoreType.DMA((6,)),
+            ],
             compiler_params=limit(54),
             cost_estimate=cost(4 * part_slots * rows * model, 3e6),
         )(base, mixing[part], near_core(x))

time: 217 us -> 219 us (level)
  no operation moved by 1% of the time
where the time goes in v6:
time: 219 us; the launch traced here: 218 us
  waiting for transfers between devices  75.7 us (35%)
  Pallas kernels  70.4 us (32%)
  blocking collectives  39.2 us (18%)
  starting transfers between devices  29 us (13%)
    all_to_all x4, waiting for transfers between devices, exchange(): x = lax.all_to_all(x, CHIP, split_axis=0, concat_axis=0, tiled=True)  71.7 us
    pallas_call x2, Pallas kernels, experts(): pl.pallas_call(expert_kernel, name='experts', in_specs=[VMEM] + [HBM] * 6...  31.6 us
    all_to_all x4, starting transfers between devices, exchange(): x = lax.all_to_all(x, CHIP, split_axis=0, concat_axis=0, tiled=True)  24.8 us
    all_to_all x1, blocking collectives, layer(): lax.all_to_all(packed, 'req', split_axis=0, concat_axis=0, tiled=True)  22.1 us
    all_to_all x1, blocking collectives, layer(): near = lax.all_to_all(picked, CHIP, split_axis=0, concat_axis=0, tiled=True)  17.1 us
    pallas_call x1, Pallas kernels, layer(): pl.pallas_call(functools.partial(attend_kernel, score_scale), name='atten...  8.85 us
    pallas_call x1, Pallas kernels, layer(): pl.pallas_call(functools.partial(query_kernel, score_scale), name='query'...  8.41 us
    pallas_call x2, Pallas kernels, mix(): pl.pallas_call(mix_kernel, name='mix', in_specs=[HBM, HBM, VMEM], out_spe...  6.88 us
  transfers between devices with their start and end apart: 11, of which 7 were waited for; matrix products, arithmetic and copies ran while one was open for 0% of the time, Pallas kernels for 26%

profile of v6, /device:TPU:0, one launch (start us, length us, event | category | flops | bytes accessed | tf_op | source)
XLA Modules:
  0.0 217.7 jit_solution(9884654029188951346)
XLA Ops:
  1.3 1.7 pack.1
  3.1 22.1 %all_to_all.30 = bf16[32,40,128]{2,1,0:T(8,128)(2,1)S(1)} all-to-all(bf16[32,40,128]{2,1,0:T(8,128)(2,1)} %pack.1), channel_id=1, replica_groups=mesh['req'=32,'ylo'=2,'core'=2] {'req'}, dimensions={0} | all-to-all | bytes 655360 | tf_op jit(solution)/shard_map/all_to_all | solution.py:361
  26.8 17.1 %all_to_all.31 = bf16[64,40,128]{2,1,0:T(8,128)(2,1)S(1)} all-to-all(bf16[64,40,128]{2,1,0:T(8,128)(2,1)S(1)} %gather_fusion), channel_id=1, replica_groups=mesh['req'=32,'ylo'=2,'core'=2] {'req','ylo'}, dimensions={0} | all-to-all | bytes 1310720 | tf_op jit(solution)/shard_map/all_to_all | solution.py:373
  44.2 4.2 %cache.1 = (bf16[576,128]{1,0:T(8,128)(2,1)}, bf16[128,2048]{1,0:T(8,128)(2,1)}, f32[128,64]{1,0:T(8,128)}) custom-call(s32[1,3]{1,0:T(1,128)} %lengths_ref.3, s32[1]{0:T(128)} %bitcast.sub_ref, bf16[128,2048]{1,0:T(8,128)(2,1)} %tokens_hbm.1, f32[1,2048]{1,0:T(1,128)} %bitcast.41, bf16[576,2048]{1,0:T(8,128)(2,1)} %bitcast.36, f32[1,512]{1,0:T(1,128)} %bitcast.42, ...), custom_call_target="tpu_custom_call" | custom-call | flops 301989888 | bytes 4000000 | tf_op jit(solution)/shard_map/cache/pallas_call | solution.py:393
  50.6 1.7 route.1.place_hbm.place_ref
  52.3 1.4 collective-permute-done.back_1_ref
  53.8 2.1 collective-permute-done.1.back_2_ref
  56.3 8.4 %query.1 = (bf16[8,128,576]{2,1,0:T(8,128)(2,1)}, f32[1024,512]{1,0:T(8,128)}, f32[1024,128]{1,0:T(8,128)}) custom-call(s32[1,3]{1,0:T(1,128)} %lengths_ref.3, s32[1]{0:T(128)} %bitcast.sub_ref, bf16[128,2048]{1,0:T(8,128)(2,1)} %get-tuple-element.11.normed_ref, f32[128,64]{1,0:T(8,128)} %get-tuple-element.12.angle_ref, bf16[2048,1536]{1,0:T(8,128)(2,1)} %wq_ref.1, ...), custom_call_target="tpu_custom_call" | custom-call | flops 3000000000 | bytes 12000000 | tf_op jit(solution)/shard_map/query/pallas_call | solution.py:413
  64.7 8.9 %attend.1 = (f32[128,2048]{1,0:T(8,128)}, bf16[128,2048]{1,0:T(8,128)(2,1)}, bf16[512,2048]{1,0:T(8,128)(2,1)}) custom-call(bf16[8,128,576]{2,1,0:T(8,128)(2,1)} %get-tuple-element.14.query_hbm, f32[1024,512]{1,0:T(8,128)} %get-tuple-element.15.late_hbm, f32[1024,128]{1,0:T(8,128)} %get-tuple-element.16.stats_hbm, ...), custom_call_target="tpu_custom_call" | custom-call | flops 5000000000 | bytes 6000000 | tf_op jit(solution)/shard_map/attend/pallas_call | solution.py:468
  73.6 5.9 %all-to-all-start.2 = ((bf16[64,8,2048]{2,1,0:T(8,128)(2,1)}), bf16[64,8,2048]{2,1,0:T(8,128)(2,1)S(1)}, u32[]{:S(2)}, u32[]{:S(2)}) async-start(bf16[64,8,2048]{2,1,0:T(8,128)(2,1)} %bitcast.37), calls=%async_computation.2 | async-start | bytes 4194304 | tf_op jit(solution)/shard_map/all_to_all | solution.py:501
  81.3 2.9 %place.1 = bf16[512,2048]{1,0:T(8,128)(2,1)} custom-call(bf16[2,512,128]{2,1,0:T(8,128)(2,1)} %route.1.place_hbm.place_ref, bf16[128,2048]{1,0:T(8,128)(2,1)} %get-tuple-element.19.mid_ref), custom_call_target="tpu_custom_call" | custom-call | flops 268435456 | bytes 3000000 | tf_op jit(solution)/shard_map/place/pallas_call | solution.py:505
  84.2 26.0 %all-to-all-done.2 = bf16[64,8,2048]{2,1,0:T(8,128)(2,1)S(1)} async-done(((bf16[64,8,2048]{2,1,0:T(8,128)(2,1)}), bf16[64,8,2048]{2,1,0:T(8,128)(2,1)S(1)}, u32[]{:S(2)}, u32[]{:S(2)}) %all-to-all-start.2) | async-done | bytes 2097184 | tf_op jit(solution)/shard_map/all_to_all | solution.py:501
  110.3 6.1 %all-to-all-start.4 = ((bf16[64,8,2048]{2,1,0:T(8,128)(2,1)}), bf16[64,8,2048]{2,1,0:T(8,128)(2,1)}, u32[]{:S(2)}, u32[]{:S(2)}) async-start(bf16[64,8,2048]{2,1,0:T(8,128)(2,1)} %bitcast.33), calls=%async_computation.4 | async-start | bytes 4194304 | tf_op jit(solution)/shard_map/all_to_all | solution.py:501
  116.4 15.0 %experts.2 = bf16[512,2048]{1,0:T(8,128)(2,1)} custom-call(bf16[512,2048]{1,0:T(8,128)(2,1)S(1)} %bitcast.32, bf16[704,2048]{1,0:T(8,128)(2,1)} %bitcast.44, bf16[704,2048]{1,0:T(8,128)(2,1)} %bitcast.47, bf16[704,2048]{1,0:T(8,128)(2,1)} %bitcast.50, bf16[704,2048]{1,0:T(8,128)(2,1)} %collective-permute-done.4.g1, ...), custom_call_target="tpu_custom_call" | custom-call | flops 8858370048 | bytes 21000000 | tf_op jit(solution)/shard_map/experts/pallas_call | solution.py:518
  131.4 14.0 %all-to-all-done.4 = bf16[64,8,2048]{2,1,0:T(8,128)(2,1)} async-done(((bf16[64,8,2048]{2,1,0:T(8,128)(2,1)}), bf16[64,8,2048]{2,1,0:T(8,128)(2,1)}, u32[]{:S(2)}, u32[]{:S(2)}) %all-to-all-start.4) | async-done | bytes 2097184 | tf_op jit(solution)/shard_map/all_to_all | solution.py:501
  145.4 6.2 %all-to-all-start.3 = ((bf16[64,8,2048]{2,1,0:T(8,128)(2,1)}), bf16[64,8,2048]{2,1,0:T(8,128)(2,1)S(1)}, u32[]{:S(2)}, u32[]{:S(2)}) async-start(bf16[64,8,2048]{2,1,0:T(8,128)(2,1)} %bitcast.39), calls=%async_computation.3 | async-start | bytes 4194304 | tf_op jit(solution)/shard_map/all_to_all | solution.py:501
  151.5 16.6 %experts.3 = bf16[512,2048]{1,0:T(8,128)(2,1)} custom-call(bf16[512,2048]{1,0:T(8,128)(2,1)} %bitcast.23.x_ref, bf16[704,2048]{1,0:T(8,128)(2,1)} %bitcast.45, bf16[704,2048]{1,0:T(8,128)(2,1)} %bitcast.48, bf16[704,2048]{1,0:T(8,128)(2,1)} %bitcast.51, bf16[704,2048]{1,0:T(8,128)(2,1)} %collective-permute-done.4.g1, ...), custom_call_target="tpu_custom_call" | custom-call | flops 8858370048 | bytes 21000000 | tf_op jit(solution)/shard_map/experts/pallas_call | solution.py:518
  168.2 11.5 %all-to-all-done.3 = bf16[64,8,2048]{2,1,0:T(8,128)(2,1)S(1)} async-done(((bf16[64,8,2048]{2,1,0:T(8,128)(2,1)}), bf16[64,8,2048]{2,1,0:T(8,128)(2,1)S(1)}, u32[]{:S(2)}, u32[]{:S(2)}) %all-to-all-start.3) | async-done | bytes 2097184 | tf_op jit(solution)/shard_map/all_to_all | solution.py:501
  179.6 6.7 %all-to-all-start.5 = ((bf16[64,8,2048]{2,1,0:T(8,128)(2,1)}), bf16[64,8,2048]{2,1,0:T(8,128)(2,1)}, u32[]{:S(2)}, u32[]{:S(2)}) async-start(bf16[64,8,2048]{2,1,0:T(8,128)(2,1)} %bitcast.38), calls=%async_computation.5 | async-start | bytes 4194304 | tf_op jit(solution)/shard_map/all_to_all | solution.py:501
  186.4 2.0 gates.2.mix_hbm
  188.4 2.0 gates.3.mix_hbm
  190.4 2.7 %mix.2.base_hbm = f32[128,2048]{1,0:T(8,128)} custom-call(f32[128,2048]{1,0:T(8,128)} %get-tuple-element.17.base_hbm, bf16[256,512]{1,0:T(8,128)(2,1)} %gates.2.mix_hbm, bf16[512,2048]{1,0:T(8,128)(2,1)S(1)} %bitcast.31), custom_call_target="tpu_custom_call" | custom-call | flops 536870912 | bytes 3000000 | tf_op jit(solution)/shard_map/mix/pallas_call | solution.py:534
  193.1 20.2 %all-to-all-done.5 = bf16[64,8,2048]{2,1,0:T(8,128)(2,1)} async-done(((bf16[64,8,2048]{2,1,0:T(8,128)(2,1)}), bf16[64,8,2048]{2,1,0:T(8,128)(2,1)}, u32[]{:S(2)}, u32[]{:S(2)}) %all-to-all-start.5) | async-done | bytes 2097184 | tf_op jit(solution)/shard_map/all_to_all | solution.py:501
  213.3 4.2 %mix.3 = bf16[128,2048]{1,0:T(8,128)(2,1)} custom-call(f32[128,2048]{1,0:T(8,128)} %mix.2.base_hbm, bf16[256,512]{1,0:T(8,128)(2,1)} %gates.3.mix_hbm, bf16[512,2048]{1,0:T(8,128)(2,1)} %bitcast.25.rows_ref), custom_call_target="tpu_custom_call" | custom-call | flops 536870912 | bytes 3000000 | tf_op jit(solution)/shard_map/mix/pallas_call | solution.py:534
  (22 shorter events, 6.4 us)
Async XLA Ops:
  0.6 25.2 %copy-start = (s32[4]{0:T(128)S(1)}, s32[4]{0:T(128)}, u32[]{:S(2)}) copy-start(s32[4]{0:T(128)} %param.35) | copy-start | bytes 52
  44.1 20.6 %collective-permute-start.3 = (bf16[4,576,128]{2,1,0:T(8,128)(2,1)S(1)}, bf16[4,576,128]{2,1,0:T(8,128)(2,1)S(1)}, u32[]{:S(2)}, u32[]{:S(2)}) collective-permute-start(bf16[4,576,128]{2,1,0:T(8,128)(2,1)S(1)} %reshape.49.near_ref), channel_id=1, source_target_pairs={{0,1},{1,0},{2,3},{3,2},{4,5},{5,4},{6,7},{7,6},{8,9},{9,8},{10,11... | collective-permute-start | bytes 1769480 | tf_op jit(solution)/shard_map/ppermute | solution.py:377
  48.4 5.4 %collective-permute-start = (bf16[576,128]{1,0:T(8,128)(2,1)}, bf16[576,128]{1,0:T(8,128)(2,1)S(1)}, u32[]{:S(2)}, u32[]{:S(2)}) collective-permute-start(bf16[576,128]{1,0:T(8,128)(2,1)} %get-tuple-element.13.own_ref), channel_id=1, source_target_pairs={{0,1},{1,2},{2,3},{3,0},{4,5},{5,6},{6,7},{7,4},{8,9},{9,10},{10,1... | collective-permute-start | bytes 442376 | tf_op jit(solution)/shard_map/ppermute | solution.py:407
  49.0 6.9 %collective-permute-start.1 = (bf16[576,128]{1,0:T(8,128)(2,1)}, bf16[576,128]{1,0:T(8,128)(2,1)S(1)}, u32[]{:S(2)}, u32[]{:S(2)}) collective-permute-start(bf16[576,128]{1,0:T(8,128)(2,1)} %get-tuple-element.13.own_ref), channel_id=1, source_target_pairs={{0,2},{1,3},{2,0},{3,1},{4,6},{5,7},{6,4},{7,5},{8,10},{9,11},{10,... | collective-permute-start | bytes 442376 | tf_op jit(solution)/shard_map/ppermute | solution.py:407
  49.6 6.7 %collective-permute-start.2 = (bf16[576,128]{1,0:T(8,128)(2,1)}, bf16[576,128]{1,0:T(8,128)(2,1)S(1)}, u32[]{:S(2)}, u32[]{:S(2)}) collective-permute-start(bf16[576,128]{1,0:T(8,128)(2,1)} %get-tuple-element.13.own_ref), channel_id=1, source_target_pairs={{0,3},{1,0},{2,1},{3,2},{4,7},{5,4},{6,5},{7,6},{8,11},{9,8},{10,9... | collective-permute-start | bytes 442376 | tf_op jit(solution)/shard_map/ppermute | solution.py:407
  73.6 36.7 %all-to-all-start.2 = ((bf16[64,8,2048]{2,1,0:T(8,128)(2,1)}), bf16[64,8,2048]{2,1,0:T(8,128)(2,1)S(1)}, u32[]{:S(2)}, u32[]{:S(2)}) async-start(bf16[64,8,2048]{2,1,0:T(8,128)(2,1)} %bitcast.37), calls=%async_computation.2 | async-start | bytes 4194304 | tf_op jit(solution)/shard_map/all_to_all | solution.py:501
  79.4 36.9 %collective-permute-start.4 = (bf16[704,2048]{1,0:T(8,128)(2,1)}, bf16[704,2048]{1,0:T(8,128)(2,1)}, u32[]{:S(2)}, u32[]{:S(2)}) collective-permute-start(bf16[704,2048]{1,0:T(8,128)(2,1)} %bitcast.43), channel_id=1, source_target_pairs={{0,1},{1,0},{2,3},{3,2},{4,5},{5,4},{6,7},{7,6},{8,9},{9,8},{10,11... | collective-permute-start | bytes 8650760 | tf_op jit(solution)/shard_map/ppermute | solution.py:382
  80.8 35.6 %collective-permute-start.5 = (bf16[704,2048]{1,0:T(8,128)(2,1)}, bf16[704,2048]{1,0:T(8,128)(2,1)}, u32[]{:S(2)}, u32[]{:S(2)}) collective-permute-start(bf16[704,2048]{1,0:T(8,128)(2,1)} %bitcast.46), channel_id=1, source_target_pairs={{0,1},{1,0},{2,3},{3,2},{4,5},{5,4},{6,7},{7,6},{8,9},{9,8},{10,11... | collective-permute-start | bytes 8650760 | tf_op jit(solution)/shard_map/ppermute | solution.py:383
  80.9 35.5 %collective-permute-start.6 = (bf16[704,2048]{1,0:T(8,128)(2,1)}, bf16[704,2048]{1,0:T(8,128)(2,1)}, u32[]{:S(2)}, u32[]{:S(2)}) collective-permute-start(bf16[704,2048]{1,0:T(8,128)(2,1)} %bitcast.49), channel_id=1, source_target_pairs={{0,1},{1,0},{2,3},{3,2},{4,5},{5,4},{6,7},{7,6},{8,9},{9,8},{10,11... | collective-permute-start | bytes 8650760 | tf_op jit(solution)/shard_map/ppermute | solution.py:384
  110.3 35.1 %all-to-all-start.4 = ((bf16[64,8,2048]{2,1,0:T(8,128)(2,1)}), bf16[64,8,2048]{2,1,0:T(8,128)(2,1)}, u32[]{:S(2)}, u32[]{:S(2)}) async-start(bf16[64,8,2048]{2,1,0:T(8,128)(2,1)} %bitcast.33), calls=%async_computation.4 | async-start | bytes 4194304 | tf_op jit(solution)/shard_map/all_to_all | solution.py:501
  145.4 34.3 %all-to-all-start.3 = ((bf16[64,8,2048]{2,1,0:T(8,128)(2,1)}), bf16[64,8,2048]{2,1,0:T(8,128)(2,1)S(1)}, u32[]{:S(2)}, u32[]{:S(2)}) async-start(bf16[64,8,2048]{2,1,0:T(8,128)(2,1)} %bitcast.39), calls=%async_computation.3 | async-start | bytes 4194304 | tf_op jit(solution)/shard_map/all_to_all | solution.py:501
  179.6 33.7 %all-to-all-start.5 = ((bf16[64,8,2048]{2,1,0:T(8,128)(2,1)}), bf16[64,8,2048]{2,1,0:T(8,128)(2,1)}, u32[]{:S(2)}, u32[]{:S(2)}) async-start(bf16[64,8,2048]{2,1,0:T(8,128)(2,1)} %bitcast.38), calls=%async_computation.5 | async-start | bytes 4194304 | tf_op jit(solution)/shard_map/all_to_all | solution.py:501
